TPU v7x, 32 devices: a whole 2x2x4 slice. The times are simulated.
32 devices in a mesh: ctx: 8 (over z, y), fsdp: 4 (over x, core).
Axes of the slice: x: 2, y: 2, z: 4, core: 2. Of those that a mesh axis runs over, the one named last changes fastest.
Arguments:
- inputs: bfloat16 [4, 4096, 768], P('fsdp', 'ctx'), may hold values from -6 to 6
- encoded: bfloat16 [4, 512, 768], P('fsdp', 'ctx'), may hold values from -6 to 6
- doc_lengths: int32 [4, 4], P('fsdp'), may hold values from 1 to 3840, 4096 in all within a row
- self_gain: bfloat16 [768], P('fsdp'), may hold values from 0.5 to 1.5
- self_query: bfloat16 [768, 768], P('fsdp'), may hold values from -0.0390625 to 0.0390625
- self_key: bfloat16 [768, 768], P('fsdp'), may hold values from -0.21875 to 0.21875
- self_value: bfloat16 [768, 768], P('fsdp'), may hold values from -0.21875 to 0.21875
- self_output: bfloat16 [768, 768], P('fsdp'), may hold values from -1.25 to 1.25
- bias_table: bfloat16 [32, 12], P('fsdp'), may hold values from -4 to 4
- cross_gain: bfloat16 [768], P('fsdp'), may hold values from 0.5 to 1.5
- cross_query: bfloat16 [768, 768], P('fsdp'), may hold values from -0.0390625 to 0.0390625
- cross_key: bfloat16 [768, 768], P('fsdp'), may hold values from -0.21875 to 0.21875
- cross_value: bfloat16 [768, 768], P('fsdp'), may hold values from -0.21875 to 0.21875
- cross_output: bfloat16 [768, 768], P('fsdp'), may hold values from -1.75 to 1.75
- ffn_gain: bfloat16 [768], P('fsdp'), may hold values from 0.5 to 1.5
- ffn_gate: bfloat16 [768, 2048], P(None, 'fsdp'), may hold values from -0.21875 to 0.21875
- ffn_up: bfloat16 [768, 2048], P(None, 'fsdp'), may hold values from -0.21875 to 0.21875
- ffn_down: bfloat16 [2048, 768], P('fsdp'), may hold values from -0.125 to 0.125
- cotangent: bfloat16 [4, 4096, 768], P('fsdp', 'ctx'), may hold values from -6 to 6
Outputs:
- outputs: bfloat16 [4, 4096, 768], P('fsdp', 'ctx')
- grad_inputs: bfloat16 [4, 4096, 768], P('fsdp', 'ctx')
- grad_encoded: bfloat16 [4, 512, 768], P('fsdp', 'ctx')
- grad_self_gain: float32 [768], P('fsdp')
- grad_self_query: float32 [768, 768], P('fsdp')
- grad_self_key: float32 [768, 768], P('fsdp')
- grad_self_value: float32 [768, 768], P('fsdp')
- grad_self_output: float32 [768, 768], P('fsdp')
- grad_bias_table: float32 [32, 12], P('fsdp')
- grad_cross_gain: float32 [768], P('fsdp')
- grad_cross_query: float32 [768, 768], P('fsdp')
- grad_cross_key: float32 [768, 768], P('fsdp')
- grad_cross_value: float32 [768, 768], P('fsdp')
- grad_cross_output: float32 [768, 768], P('fsdp')
- grad_ffn_gain: float32 [768], P('fsdp')
- grad_ffn_gate: float32 [768, 2048], P(None, 'fsdp')
- grad_ffn_up: float32 [768, 2048], P(None, 'fsdp')
- grad_ffn_down: float32 [2048, 768], P('fsdp')
Inputs may be any that keep to these rules, and one draw needn't show every extreme that they name: `doc_lengths`: each row holds the lengths of the 4 documents packed in order into one sequence; they sum to 4096, and the longest is exactly 3840.
All inputs are finite; a program needn't handle non-finite values.
Results may differ from a plain program's by a relative error of at most 0.04.
Values may be sent and summed in bfloat16 or wider, within the bound.
No kernel may reach another device: no remote copies, remote signals or barrier semaphores. Data moves between devices by JAX's collectives and lax.ppermute only.
A program may use at most 320 MiB of HBM per device.

v0:
```python
import math

import jax
import jax.numpy as jnp
from jax import lax
from jax.sharding import PartitionSpec as P

D = 768
H = 12
DH = 64
NB = 32
MAXD = 128


epsilon = 1e-06
negative = -1e30


def matmul(matrix_left, matrix_right):
    return jnp.dot(matrix_left, matrix_right, preferred_element_type=jnp.float32)


def left_matmul(matrix_left, matrix_right):
    return lax.dot_general(
        matrix_left, matrix_right, (((0,), (0,)), ((), ())), preferred_element_type=jnp.float32
    )


def right_matmul(matrix_left, matrix_right):
    return lax.dot_general(
        matrix_left, matrix_right, (((1,), (1,)), ((), ())), preferred_element_type=jnp.float32
    )


def rms_norm(vector, scaling):
    factor = lax.rsqrt(jnp.mean(vector * vector, axis=-1, keepdims=True) + epsilon)
    return vector * factor * scaling


def norm_back(vector, scaling, incoming):
    pull_back = jax.vjp(rms_norm, vector, scaling)[1]
    return pull_back(incoming)


def gated(gate_proj, up_proj):
    return jax.nn.gelu(gate_proj, approximate=True) * up_proj


def bucket_of(offset):
    exact_span = NB // 2
    bucket = jnp.minimum(offset, exact_span)
    for section_index in range(1, exact_span):
        threshold = math.ceil(exact_span * (MAXD / exact_span) ** (section_index / exact_span))
        bucket = bucket + (offset >= threshold).astype(jnp.int32)
    return bucket


def far_offset():
    exact_span = NB // 2
    return math.ceil(exact_span * (MAXD / exact_span) ** ((exact_span - 1) / exact_span))


def document_of(positions, doc_ends):
    return jnp.sum((positions[:, None] >= doc_ends[None, :-1]).astype(jnp.int32), axis=1)


def pair_hot(query_first, key_first, query_count, key_count):
    offset = jnp.maximum(
        query_first
        + jnp.arange(query_count, dtype=jnp.int32)[:, None]
        - key_first
        - jnp.arange(key_count, dtype=jnp.int32)[None, :],
        0,
    )
    return (bucket_of(offset)[:, :, None] == jnp.arange(NB, dtype=jnp.int32)).astype(jnp.bfloat16)


def block_bias(bias_rows, query_first, key_first, query_count, key_count):
    min_offset = query_first - key_first - key_count + 1

    def block_distant(unused):
        return jnp.broadcast_to(bias_rows[NB - 1][:, None, None], (H, query_count, key_count))

    def block_nearby(unused):
        return jnp.einsum(
            "qkb,bh->hqk",
            pair_hot(query_first, key_first, query_count, key_count),
            bias_rows.astype(jnp.bfloat16),
            preferred_element_type=jnp.float32,
        )

    return lax.cond(min_offset >= far_offset(), block_distant, block_nearby, 0)


def table_grad(grad_scores, query_first, key_first):
    query_count = grad_scores.shape[1]
    key_count = grad_scores.shape[2]
    min_offset = query_first - key_first - key_count + 1

    def table_distant(unused):
        totals = jnp.sum(grad_scores.astype(jnp.float32), axis=(1, 2))
        return (jnp.arange(NB) == NB - 1).astype(jnp.float32)[:, None] * totals[None, :]

    def table_nearby(unused):
        return jnp.einsum(
            "hqk,qkb->bh",
            grad_scores,
            pair_hot(query_first, key_first, query_count, key_count),
            preferred_element_type=jnp.float32,
        )

    return lax.cond(min_offset >= far_offset(), table_distant, table_nearby, 0)


def pair_scores(query_heads, key_heads, query_first, key_first, bias_rows, doc_ends, causal):
    query_count = query_heads.shape[0]
    key_count = key_heads.shape[0]
    scores = jnp.einsum("qhd,khd->hqk", query_heads, key_heads, preferred_element_type=jnp.float32)
    if causal:
        scores = scores + block_bias(bias_rows, query_first, key_first, query_count, key_count)
        query_pos = query_first + jnp.arange(query_count, dtype=jnp.int32)
        key_pos = key_first + jnp.arange(key_count, dtype=jnp.int32)
        allowed = (key_pos[None, :] <= query_pos[:, None]) & (
            document_of(query_pos, doc_ends)[:, None] == document_of(key_pos, doc_ends)[None, :]
        )
    else:
        allowed = jnp.ones((query_count, key_count), dtype=bool)
    return (scores, allowed)


def pair_grads(scores, allowed, out_heads, value_heads, log_total, row_dots):
    probs_full = jnp.where(allowed[None], jnp.exp(scores - log_total[:, :, None]), 0.0)
    grad_probs = jnp.einsum(
        "qhd,khd->hqk", out_heads, value_heads, preferred_element_type=jnp.float32
    )
    grad_scores = (probs_full * (grad_probs - row_dots[:, :, None])).astype(jnp.bfloat16)
    return (grad_scores, probs_full.astype(jnp.bfloat16))


def forward_fold(current, pieces, query_heads, query_first, bias_rows, doc_ends, causal):
    key_piece, value_piece = pieces
    piece_rows = key_piece.shape[0]
    block_rows = math.gcd(piece_rows, 512)
    block_count = piece_rows // block_rows
    query_rows = query_heads.shape[0]

    def compute(state, key_heads, value_heads, key_first):
        running_max, running_sum, running_out = state
        scores, allowed = pair_scores(
            query_heads, key_heads, query_first, key_first, bias_rows, doc_ends, causal
        )
        scores = jnp.where(allowed[None], scores, negative)
        new_max = jnp.maximum(running_max, jnp.max(scores, axis=2))
        weights = jnp.where(allowed[None], jnp.exp(scores - new_max[:, :, None]), 0.0)
        factor = jnp.exp(running_max - new_max)
        running_sum = running_sum * factor + jnp.sum(weights, axis=2)
        running_out = running_out * factor[:, :, None] + jnp.einsum(
            "hqk,khd->hqd",
            weights.astype(jnp.bfloat16),
            value_heads,
            preferred_element_type=jnp.float32,
        )
        return (new_max, running_sum, running_out)

    def forward_advance(state, element):
        key_block, value_block, block_index = element
        key_first = block_index * block_rows
        key_heads = key_block.reshape(block_rows, H, DH)
        value_heads = value_block.reshape(block_rows, H, DH)
        if causal:
            state = lax.cond(
                key_first < query_first + query_rows,
                lambda unchanged: compute(unchanged, key_heads, value_heads, key_first),
                lambda unchanged: unchanged,
                state,
            )
        else:
            state = compute(state, key_heads, value_heads, key_first)
        return (state, None)

    current, unused = lax.scan(
        forward_advance,
        current,
        (
            key_piece.reshape(block_count, block_rows, D),
            value_piece.reshape(block_count, block_rows, D),
            jnp.arange(block_count, dtype=jnp.int32),
        ),
    )
    return current


def backward_fold(
    current,
    pieces,
    query_heads,
    out_heads,
    log_total,
    row_dots,
    query_first,
    bias_rows,
    doc_ends,
    causal,
):
    key_piece, value_piece = pieces
    piece_rows = key_piece.shape[0]
    block_rows = math.gcd(piece_rows, 512)
    block_count = piece_rows // block_rows
    query_rows = query_heads.shape[0]

    def compute(state, key_heads, value_heads, key_first):
        scores, allowed = pair_scores(
            query_heads, key_heads, query_first, key_first, bias_rows, doc_ends, causal
        )
        grad_scores, probs_low = pair_grads(
            scores, allowed, out_heads, value_heads, log_total, row_dots
        )
        updated = [
            state[0]
            + jnp.einsum("hqk,khd->qhd", grad_scores, key_heads, preferred_element_type=jnp.float32)
        ]
        grad_key_block = jnp.einsum(
            "hqk,qhd->khd", grad_scores, query_heads, preferred_element_type=jnp.float32
        ).reshape(block_rows, D)
        grad_value_block = jnp.einsum(
            "hqk,qhd->khd", probs_low, out_heads, preferred_element_type=jnp.float32
        ).reshape(block_rows, D)
        block_grads = jnp.concatenate([grad_key_block, grad_value_block], axis=1)
        previous = lax.dynamic_slice_in_dim(state[1], key_first, block_rows, 0)
        updated.append(
            lax.dynamic_update_slice_in_dim(state[1], previous + block_grads, key_first, 0)
        )
        if causal:
            updated.append(state[2] + table_grad(grad_scores, query_first, key_first))
        return tuple(updated)

    def backward_advance(state, element):
        key_block, value_block, block_index = element
        key_first = block_index * block_rows
        key_heads = key_block.reshape(block_rows, H, DH)
        value_heads = value_block.reshape(block_rows, H, DH)
        if causal:
            state = lax.cond(
                key_first < query_first + query_rows,
                lambda unchanged: compute(unchanged, key_heads, value_heads, key_first),
                lambda unchanged: unchanged,
                state,
            )
        else:
            state = compute(state, key_heads, value_heads, key_first)
        return (state, None)

    current, unused = lax.scan(
        backward_advance,
        current,
        (
            key_piece.reshape(block_count, block_rows, D),
            value_piece.reshape(block_count, block_rows, D),
            jnp.arange(block_count, dtype=jnp.int32),
        ),
    )
    return current


def shards(
    inputs,
    encoded,
    doc_lengths,
    self_gain,
    self_query,
    self_key,
    self_value,
    self_output,
    bias_table,
    cross_gain,
    cross_query,
    cross_key,
    cross_value,
    cross_output,
    ffn_gain,
    ffn_gate,
    ffn_up,
    ffn_down,
    cotangent,
):
    gathered = (
        lax.all_gather(self_gain, "fsdp", axis=0, tiled=True),
        lax.all_gather(self_query, "fsdp", axis=0, tiled=True),
        lax.all_gather(self_key, "fsdp", axis=0, tiled=True),
        lax.all_gather(self_value, "fsdp", axis=0, tiled=True),
        lax.all_gather(self_output, "fsdp", axis=0, tiled=True),
        lax.all_gather(bias_table, "fsdp", axis=0, tiled=True),
        lax.all_gather(cross_gain, "fsdp", axis=0, tiled=True),
        lax.all_gather(cross_query, "fsdp", axis=0, tiled=True),
        lax.all_gather(cross_key, "fsdp", axis=0, tiled=True),
        lax.all_gather(cross_value, "fsdp", axis=0, tiled=True),
        lax.all_gather(cross_output, "fsdp", axis=0, tiled=True),
        lax.all_gather(ffn_gain, "fsdp", axis=0, tiled=True),
        lax.all_gather(ffn_gate, "fsdp", axis=1, tiled=True),
        lax.all_gather(ffn_up, "fsdp", axis=1, tiled=True),
        lax.all_gather(ffn_down, "fsdp", axis=0, tiled=True),
    )
    (
        gain_one,
        w_query,
        w_key,
        w_value,
        w_output,
        table_rows,
        gain_two,
        c_query,
        c_key,
        c_value,
        c_output,
        gain_three,
        w_gate,
        w_up,
        w_down,
    ) = gathered
    gain_self = gain_one.astype(jnp.float32)
    gain_cross = gain_two.astype(jnp.float32)
    gain_ffn = gain_three.astype(jnp.float32)
    bias_rows = table_rows.astype(jnp.float32)
    states = inputs[0].astype(jnp.float32)
    encoder = encoded[0]
    tok_rows = states.shape[0]
    enc_rows = encoder.shape[0]
    cycle_size = lax.axis_size("ctx")
    query_first = lax.axis_index("ctx") * tok_rows
    doc_ends = jnp.cumsum(doc_lengths[0])
    normed_one = rms_norm(states, gain_self).astype(jnp.bfloat16)
    query_proj = matmul(normed_one, w_query).astype(jnp.bfloat16)
    key_proj = matmul(normed_one, w_key).astype(jnp.bfloat16)
    value_proj = matmul(normed_one, w_value).astype(jnp.bfloat16)
    query_heads = query_proj.reshape(tok_rows, H, DH)
    start_state = (
        jnp.full((H, tok_rows), negative, jnp.float32),
        jnp.zeros((H, tok_rows), jnp.float32),
        jnp.zeros((H, tok_rows, DH), jnp.float32),
    )
    self_max, self_sum, self_acc = forward_fold(
        start_state,
        (
            lax.all_gather(key_proj, "ctx", axis=0, tiled=True),
            lax.all_gather(value_proj, "ctx", axis=0, tiled=True),
        ),
        query_heads,
        query_first,
        bias_rows,
        doc_ends,
        True,
    )
    log_total = self_max + jnp.log(self_sum)
    self_full = self_acc / self_sum[:, :, None]
    attended = jnp.transpose(self_full, (1, 0, 2)).reshape(tok_rows, D).astype(jnp.bfloat16)
    first_sum = states + matmul(attended, w_output)
    normed_two = rms_norm(first_sum, gain_cross).astype(jnp.bfloat16)
    cross_queries = matmul(normed_two, c_query).astype(jnp.bfloat16)
    cross_keys = matmul(encoder, c_key).astype(jnp.bfloat16)
    cross_values = matmul(encoder, c_value).astype(jnp.bfloat16)
    cross_heads = cross_queries.reshape(tok_rows, H, DH)
    cross_max, cross_sum, cross_acc = forward_fold(
        start_state,
        (
            lax.all_gather(cross_keys, "ctx", axis=0, tiled=True),
            lax.all_gather(cross_values, "ctx", axis=0, tiled=True),
        ),
        cross_heads,
        query_first,
        bias_rows,
        doc_ends,
        False,
    )
    cross_log = cross_max + jnp.log(cross_sum)
    cross_full = cross_acc / cross_sum[:, :, None]
    cross_out = jnp.transpose(cross_full, (1, 0, 2)).reshape(tok_rows, D).astype(jnp.bfloat16)
    second_sum = first_sum + matmul(cross_out, c_output)
    normed_three = rms_norm(second_sum, gain_ffn).astype(jnp.bfloat16)
    gate_proj = matmul(normed_three, w_gate)
    up_proj = matmul(normed_three, w_up)
    hidden = gated(gate_proj, up_proj).astype(jnp.bfloat16)
    outputs = (second_sum + matmul(hidden, w_down)).astype(jnp.bfloat16)
    outer_grad = cotangent[0]
    grad_hidden = right_matmul(outer_grad, w_down)
    grad_down = left_matmul(hidden, outer_grad)
    grad_gate, grad_up = jax.vjp(gated, gate_proj, up_proj)[1](grad_hidden)
    grad_gate = grad_gate.astype(jnp.bfloat16)
    grad_up = grad_up.astype(jnp.bfloat16)
    grad_w_gate = left_matmul(normed_three, grad_gate)
    grad_w_up = left_matmul(normed_three, grad_up)
    grad_normed_three = right_matmul(grad_gate, w_gate) + right_matmul(grad_up, w_up)
    grad_part, grad_gain_ffn = norm_back(second_sum, gain_ffn, grad_normed_three)
    grad_second = outer_grad.astype(jnp.float32) + grad_part
    branch_two = grad_second.astype(jnp.bfloat16)
    grad_c_output = left_matmul(cross_out, branch_two)
    grad_cross_out = right_matmul(branch_two, c_output).astype(jnp.bfloat16)
    cross_grad_heads = grad_cross_out.reshape(tok_rows, H, DH)
    cross_dots = jnp.einsum("qhd,hqd->hq", cross_grad_heads.astype(jnp.float32), cross_full)
    cross_start = (
        jnp.zeros((tok_rows, H, DH), jnp.float32),
        jnp.zeros((enc_rows * cycle_size, 2 * D), jnp.float32),
    )
    grad_cq_full, grad_ckv_full = backward_fold(
        cross_start,
        (
            lax.all_gather(cross_keys, "ctx", axis=0, tiled=True),
            lax.all_gather(cross_values, "ctx", axis=0, tiled=True),
        ),
        cross_heads,
        cross_grad_heads,
        cross_log,
        cross_dots,
        query_first,
        bias_rows,
        doc_ends,
        False,
    )
    grad_ckv = lax.psum_scatter(
        grad_ckv_full.astype(jnp.bfloat16), "ctx", scatter_dimension=0, tiled=True
    ).astype(jnp.float32)
    grad_cross_keys = grad_ckv[:, :D].astype(jnp.bfloat16)
    grad_cross_values = grad_ckv[:, D:].astype(jnp.bfloat16)
    grad_cross_queries = grad_cq_full.reshape(tok_rows, D).astype(jnp.bfloat16)
    grad_c_query = left_matmul(normed_two, grad_cross_queries)
    grad_c_key = left_matmul(encoder, grad_cross_keys)
    grad_c_value = left_matmul(encoder, grad_cross_values)
    grad_encoder = (
        right_matmul(grad_cross_keys, c_key) + right_matmul(grad_cross_values, c_value)
    ).astype(jnp.bfloat16)
    grad_part, grad_gain_cross = norm_back(
        first_sum, gain_cross, right_matmul(grad_cross_queries, c_query)
    )
    grad_first = grad_second + grad_part
    branch_one = grad_first.astype(jnp.bfloat16)
    grad_w_output = left_matmul(attended, branch_one)
    grad_attended = right_matmul(branch_one, w_output).astype(jnp.bfloat16)
    grad_heads = grad_attended.reshape(tok_rows, H, DH)
    row_dots = jnp.einsum("qhd,hqd->hq", grad_heads.astype(jnp.float32), self_full)
    zero_heads = jnp.zeros((tok_rows, H, DH), jnp.float32)
    self_start = (
        zero_heads,
        jnp.zeros((tok_rows * cycle_size, 2 * D), jnp.float32),
        jnp.zeros((NB, H), jnp.float32),
    )
    grad_query_full, grad_kv_full, grad_table = backward_fold(
        self_start,
        (
            lax.all_gather(key_proj, "ctx", axis=0, tiled=True),
            lax.all_gather(value_proj, "ctx", axis=0, tiled=True),
        ),
        query_heads,
        grad_heads,
        log_total,
        row_dots,
        query_first,
        bias_rows,
        doc_ends,
        True,
    )
    grad_kv = lax.psum_scatter(
        grad_kv_full.astype(jnp.bfloat16), "ctx", scatter_dimension=0, tiled=True
    ).astype(jnp.float32)
    grad_keys = grad_kv[:, :D].astype(jnp.bfloat16)
    grad_values = grad_kv[:, D:].astype(jnp.bfloat16)
    grad_queries = grad_query_full.reshape(tok_rows, D).astype(jnp.bfloat16)
    grad_w_query = left_matmul(normed_one, grad_queries)
    grad_w_key = left_matmul(normed_one, grad_keys)
    grad_w_value = left_matmul(normed_one, grad_values)
    grad_normed_one = (
        right_matmul(grad_queries, w_query)
        + right_matmul(grad_keys, w_key)
        + right_matmul(grad_values, w_value)
    )
    grad_part, grad_gain_self = norm_back(states, gain_self, grad_normed_one)
    grad_states = (grad_first + grad_part).astype(jnp.bfloat16)
    shares = (
        lax.psum_scatter(
            grad_gain_self.astype(jnp.bfloat16), "fsdp", scatter_dimension=0, tiled=True
        ).astype(jnp.float32),
        lax.psum_scatter(
            grad_w_query.astype(jnp.bfloat16), "fsdp", scatter_dimension=0, tiled=True
        ).astype(jnp.float32),
        lax.psum_scatter(
            grad_w_key.astype(jnp.bfloat16), "fsdp", scatter_dimension=0, tiled=True
        ).astype(jnp.float32),
        lax.psum_scatter(
            grad_w_value.astype(jnp.bfloat16), "fsdp", scatter_dimension=0, tiled=True
        ).astype(jnp.float32),
        lax.psum_scatter(
            grad_w_output.astype(jnp.bfloat16), "fsdp", scatter_dimension=0, tiled=True
        ).astype(jnp.float32),
        lax.psum_scatter(
            grad_table.astype(jnp.bfloat16), "fsdp", scatter_dimension=0, tiled=True
        ).astype(jnp.float32),
        lax.psum_scatter(
            grad_gain_cross.astype(jnp.bfloat16), "fsdp", scatter_dimension=0, tiled=True
        ).astype(jnp.float32),
        lax.psum_scatter(
            grad_c_query.astype(jnp.bfloat16), "fsdp", scatter_dimension=0, tiled=True
        ).astype(jnp.float32),
        lax.psum_scatter(
            grad_c_key.astype(jnp.bfloat16), "fsdp", scatter_dimension=0, tiled=True
        ).astype(jnp.float32),
        lax.psum_scatter(
            grad_c_value.astype(jnp.bfloat16), "fsdp", scatter_dimension=0, tiled=True
        ).astype(jnp.float32),
        lax.psum_scatter(
            grad_c_output.astype(jnp.bfloat16), "fsdp", scatter_dimension=0, tiled=True
        ).astype(jnp.float32),
        lax.psum_scatter(
            grad_gain_ffn.astype(jnp.bfloat16), "fsdp", scatter_dimension=0, tiled=True
        ).astype(jnp.float32),
        lax.psum_scatter(
            grad_w_gate.astype(jnp.bfloat16), "fsdp", scatter_dimension=1, tiled=True
        ).astype(jnp.float32),
        lax.psum_scatter(
            grad_w_up.astype(jnp.bfloat16), "fsdp", scatter_dimension=1, tiled=True
        ).astype(jnp.float32),
        lax.psum_scatter(
            grad_down.astype(jnp.bfloat16), "fsdp", scatter_dimension=0, tiled=True
        ).astype(jnp.float32),
    )
    totals = (
        lax.psum(shares[0].astype(jnp.bfloat16), "ctx").astype(jnp.float32),
        lax.psum(shares[1].astype(jnp.bfloat16), "ctx").astype(jnp.float32),
        lax.psum(shares[2].astype(jnp.bfloat16), "ctx").astype(jnp.float32),
        lax.psum(shares[3].astype(jnp.bfloat16), "ctx").astype(jnp.float32),
        lax.psum(shares[4].astype(jnp.bfloat16), "ctx").astype(jnp.float32),
        lax.psum(shares[5].astype(jnp.bfloat16), "ctx").astype(jnp.float32),
        lax.psum(shares[6].astype(jnp.bfloat16), "ctx").astype(jnp.float32),
        lax.psum(shares[7].astype(jnp.bfloat16), "ctx").astype(jnp.float32),
        lax.psum(shares[8].astype(jnp.bfloat16), "ctx").astype(jnp.float32),
        lax.psum(shares[9].astype(jnp.bfloat16), "ctx").astype(jnp.float32),
        lax.psum(shares[10].astype(jnp.bfloat16), "ctx").astype(jnp.float32),
        lax.psum(shares[11].astype(jnp.bfloat16), "ctx").astype(jnp.float32),
        lax.psum(shares[12].astype(jnp.bfloat16), "ctx").astype(jnp.float32),
        lax.psum(shares[13].astype(jnp.bfloat16), "ctx").astype(jnp.float32),
        lax.psum(shares[14].astype(jnp.bfloat16), "ctx").astype(jnp.float32),
    )
    return (
        outputs[None],
        grad_states[None],
        grad_encoder[None],
        totals[0],
        totals[1],
        totals[2],
        totals[3],
        totals[4],
        totals[5],
        totals[6],
        totals[7],
        totals[8],
        totals[9],
        totals[10],
        totals[11],
        totals[12],
        totals[13],
        totals[14],
    )


def solution(mesh):
    in_specs = (
        P("fsdp", "ctx", None),
        P("fsdp", "ctx", None),
        P("fsdp", None),
        P("fsdp"),
        P("fsdp", None),
        P("fsdp", None),
        P("fsdp", None),
        P("fsdp", None),
        P("fsdp", None),
        P("fsdp"),
        P("fsdp", None),
        P("fsdp", None),
        P("fsdp", None),
        P("fsdp", None),
        P("fsdp"),
        P(None, "fsdp"),
        P(None, "fsdp"),
        P("fsdp", None),
        P("fsdp", "ctx", None),
    )
    out_specs = (
        P("fsdp", "ctx", None),
        P("fsdp", "ctx", None),
        P("fsdp", "ctx", None),
        P("fsdp"),
        P("fsdp", None),
        P("fsdp", None),
        P("fsdp", None),
        P("fsdp", None),
        P("fsdp", None),
        P("fsdp"),
        P("fsdp", None),
        P("fsdp", None),
        P("fsdp", None),
        P("fsdp", None),
        P("fsdp"),
        P(None, "fsdp"),
        P(None, "fsdp"),
        P("fsdp", None),
    )
    return jax.shard_map(shards, mesh=mesh, in_specs=in_specs, out_specs=out_specs, check_vma=False)
```

profile of v0, /device:TPU:0, one launch (start us, length us, event | category | flops | bytes accessed | tf_op | source)
XLA Modules:
  0.0 1995.8 jit_solution(13107747728302542778)
XLA Ops:
  15.2 8.5 all-reduce.10
  24.0 5.9 all-gather.20.cloned.1.call-done
  32.9 16.2 all-gather.14.cloned.1.call-done
  69.8 32.1 %all_gather.72 = bf16[512,768]{1,0:T(8,128)(2,1)S(1)} all-gather(bf16[64,768]{1,0:T(8,128)(2,1)S(1)} %convolution_convert_fusion.20), channel_id=1, replica_groups=mesh['ctx'=8,'fsdp'=4] {'ctx'}, dimensions={0}, use_global_device_ids=true | all-gather | bytes 884736 | tf_op jit(solution)/shard_map/all_gather | solution.py:365
  104.7 33.8 %all_gather.74 = bf16[512,768]{1,0:T(8,128)(2,1)S(1)} all-gather(bf16[64,768]{1,0:T(8,128)(2,1)S(1)} %convolution_convert_fusion.19), channel_id=1, replica_groups=mesh['ctx'=8,'fsdp'=4] {'ctx'}, dimensions={0}, use_global_device_ids=true | all-gather | bytes 884736 | tf_op jit(solution)/shard_map/all_gather | solution.py:366
  142.9 67.9 %all-gather.22.cloned.1.call-done = bf16[4096,768]{1,0:T(8,128)(2,1)} async-done(((bf16[512,768]{1,0:T(8,128)(2,1)}), bf16[4096,768]{1,0:T(8,128)(2,1)}) %all-gather.22.cloned.1.call-update) | async-done | bytes 6291472 | tf_op jit(solution)/shard_map/all_gather | solution.py:345
  210.8 9.1 copy.173
  219.9 90.9 %all-gather.16.cloned.1.call-done = bf16[4096,768]{1,0:T(8,128)(2,1)} async-done(((bf16[512,768]{1,0:T(8,128)(2,1)}), bf16[4096,768]{1,0:T(8,128)(2,1)}) %all-gather.16.cloned.1.call-update) | async-done | bytes 6291472 | tf_op jit(solution)/shard_map/all_gather | solution.py:344
  310.8 8.6 copy.171
  320.3 53.0 %while.7 = (s32[]{:T(128)}, f32[12,512]{1,0:T(8,128)S(1)}, f32[12,512]{1,0:T(8,128)}, f32[12,512,64]{1,2,0:T(8,128)S(1)}, s32[8]{0:T(128)S(1)}, /*index=5*/s32[]...) while((s32[]{:T(128)}, f32[12,512]{1,0:T(8,128)S(1)}, ...), condition=%wide.region_11.12_spmd, body=%wide.region_2.11_spmd.sunk | while | flops 1057511808 | bytes 100296624 | solution.py:181
  321.5 42.6 %conditional.7 = ((f32[12,512]{1,0:T(8,128)S(1)}, f32[12,512]{1,0:T(8,128)}, f32[12,512,64]{1,2,0:T(8,128)S(1)})) conditional(s32[]{:T(128)} %convert_element_type.922, (f32[12,512]{1,0:T(8,128)S(1)}, f32[12,512]{1,0:T(8,128)}, f32[12,512,64]{1,2,0:T(8,128)S(1)}) %tuple.147, (s32[]{:T(128)}, s32[]{:T(128)}, s32[4]{0:T(128)S(1)}, ...), branch_computations={%region_3.3_spmd, %region_4.10_spmd} | conditional | flops 1057511808 | bytes 100296336 | solution.py:171
  323.4 28.1 %conditional = (f32[12,512,512]{1,2,0:T(8,128)}) conditional(s32[]{:T(128)} %convert_element_type.547, (s32[]{:T(128)}, s32[]{:T(128)}, f32[32,12]{0,1:T(8,128)S(1)}) %tuple.59, (f32[32,12]{0,1:T(8,128)S(1)}) %tuple.99), branch_computations={%region_7.6_spmd, %region_8.7_spmd} | conditional | flops 222299520 | bytes 39851536 | solution.py:92
  325.2 8.5 fusion.2
  333.8 17.8 copy.219
  351.6 6.4 fusion.163
  399.8 5.9 fusion.168
  405.8 20.4 %all-gather.34.cloned.1.call-done = bf16[768,2048]{1,0:T(8,128)(2,1)} async-done(((bf16[768,512]{1,0:T(8,128)(2,1)}), bf16[768,2048]{1,0:T(8,128)(2,1)}) %all-gather.34.cloned.1.call-update) | async-done | bytes 3145744 | tf_op jit(solution)/shard_map/all_gather | solution.py:299
  432.0 24.3 %all-gather.38.cloned.1.call-done = bf16[2048,768]{1,0:T(8,128)(2,1)} async-done(((bf16[512,768]{1,0:T(8,128)(2,1)}), bf16[2048,768]{1,0:T(8,128)(2,1)}) %all-gather.38.cloned.1.call-update) | async-done | bytes 3145744 | tf_op jit(solution)/shard_map/all_gather | solution.py:301
  456.3 9.5 multiply_convert_fusion.1
  477.8 7.0 fusion.120
  486.0 6.3 multiply_convert_fusion
  512.5 11.5 broadcast_in_dim.172
  524.0 98.1 %while.8 = (s32[]{:T(128)}, f32[512,12,64]{0,2,1:T(8,128)}, f32[4096,1536]{0,1:T(8,128)}, f32[32,12]{0,1:T(8,128)S(1)}, s32[8]{0:T(128)S(1)}, /*index=5*/s32[]{:...) while((s32[]{:T(128)}, f32[512,12,64]{0,2,1:T(8,128)}, ...), condition=%wide.region_28.29_spmd, body=%wide.region_18.28_spmd.sunk | while | flops 2482647040 | bytes 190661040 | solution.py:253
  525.4 87.3 %conditional.8 = ((f32[512,12,64]{0,2,1:T(8,128)}, f32[4096,1536]{0,1:T(8,128)}, f32[32,12]{0,1:T(8,128)S(1)})) conditional(s32[]{:T(128)} %convert_element_type.923, (f32[512,12,64]{0,2,1:T(8,128)}, f32[4096,1536]{0,1:T(8,128)}, f32[32,12]{0,1:T(8,128)S(1)}) %tuple.150, (s32[]{:T(128)}, s32[]{:T(128)}, s32[4]{0:T(128)S(1)}, ...), branch_computations={%region_19.19_spmd, %region_20.0_spmd} | conditional | flops 2482647040 | bytes 190660704 | solution.py:243
  527.3 27.9 %conditional.2 = (f32[12,512,512]{1,2,0:T(8,128)}) conditional(s32[]{:T(128)} %convert_element_type.585, (s32[]{:T(128)}, s32[]{:T(128)}, f32[32,12]{0,1:T(8,128)S(1)}) %tuple.64, (f32[32,12]{0,1:T(8,128)S(1)}) %tuple.102), branch_computations={%region_23.22_spmd, %region_24.23_spmd} | conditional | flops 222299520 | bytes 39851536 | solution.py:92
  529.1 8.5 fusion.34
  537.7 17.6 copy.222
  555.3 6.5 fusion.78
  571.8 13.7 conditional.3
  573.6 12.0 fusion.56
  597.6 15.1 dynamic_update_slice.6
  622.1 13.4 convert_element_type.700
  635.6 54.0 %reduce-scatter.40.cloned.1.call-done = bf16[64,1536]{1,0:T(8,128)(2,1)} async-done(((bf16[512,1536]{1,0:T(8,128)(2,1)}), bf16[64,1536]{1,0:T(8,128)(2,1)}) %reduce-scatter.40.cloned.1.call-update) | async-done | bytes 196624
  725.3 717.1 %reduce-scatter.20.cloned.1.call-done = bf16[512,1536]{0,1:T(8,128)(2,1)} async-done(((bf16[4096,1536]{0,1:T(8,128)(2,1)}), bf16[512,1536]{0,1:T(8,128)(2,1)}) %reduce-scatter.20.cloned.1.call-update) | async-done | bytes 1572880 | tf_op jit(solution)/shard_map/reduce_scatter | solution.py:460
  1449.0 20.9 %reduce-scatter.42.cloned.1.call-done = bf16[192,768]{1,0:T(8,128)(2,1)} async-done(((bf16[768,768]{1,0:T(8,128)(2,1)}), bf16[192,768]{1,0:T(8,128)(2,1)}) %reduce-scatter.42.cloned.1.call-update) | async-done | bytes 294928
  1471.7 26.3 %reduce-scatter.44.cloned.1.call-done = bf16[192,768]{1,0:T(8,128)(2,1)} async-done(((bf16[768,768]{1,0:T(8,128)(2,1)}), bf16[192,768]{1,0:T(8,128)(2,1)}) %reduce-scatter.44.cloned.1.call-update) | async-done | bytes 294928
  1499.9 26.5 %reduce-scatter.32.cloned.1.call-done = bf16[192,768]{1,0:T(8,128)(2,1)} async-done(((bf16[768,768]{1,0:T(8,128)(2,1)}), bf16[192,768]{1,0:T(8,128)(2,1)}) %reduce-scatter.32.cloned.1.call-update) | async-done | bytes 294928 | tf_op jit(solution)/shard_map/reduce_scatter | solution.py:507
  1526.4 28.3 %reduce-scatter.30.cloned.1.call-done = bf16[192,768]{1,0:T(8,128)(2,1)} async-done(((bf16[768,768]{1,0:T(8,128)(2,1)}), bf16[192,768]{1,0:T(8,128)(2,1)}) %reduce-scatter.30.cloned.1.call-update) | async-done | bytes 294928 | tf_op jit(solution)/shard_map/reduce_scatter | solution.py:498
  1554.7 28.4 %reduce-scatter.28.cloned.1.call-done = bf16[192,768]{1,0:T(8,128)(2,1)} async-done(((bf16[768,768]{1,0:T(8,128)(2,1)}), bf16[192,768]{1,0:T(8,128)(2,1)}) %reduce-scatter.28.cloned.1.call-update) | async-done | bytes 294928 | tf_op jit(solution)/shard_map/reduce_scatter | solution.py:489
  1583.0 28.9 %reduce-scatter.22.cloned.1.call-done = bf16[192,768]{1,0:T(8,128)(2,1)} async-done(((bf16[768,768]{1,0:T(8,128)(2,1)}), bf16[192,768]{1,0:T(8,128)(2,1)}) %reduce-scatter.22.cloned.1.call-update) | async-done | bytes 294928 | tf_op jit(solution)/shard_map/reduce_scatter | solution.py:480
  1611.9 40.7 %reduce-scatter.38.cloned.1.call-done = bf16[512,768]{1,0:T(8,128)(2,1)} async-done(((bf16[2048,768]{1,0:T(8,128)(2,1)}), bf16[512,768]{1,0:T(8,128)(2,1)}) %reduce-scatter.38.cloned.1.call-update) | async-done | bytes 786448 | tf_op jit(solution)/shard_map/reduce_scatter | solution.py:519
  1652.6 40.5 %reduce-scatter.36.cloned.1.call-done = bf16[768,512]{1,0:T(8,128)(2,1)} async-done(((bf16[768,2048]{1,0:T(8,128)(2,1)}), bf16[768,512]{1,0:T(8,128)(2,1)}) %reduce-scatter.36.cloned.1.call-update) | async-done | bytes 786448 | tf_op jit(solution)/shard_map/reduce_scatter | solution.py:516
  1693.2 40.5 %reduce-scatter.34.cloned.1.call-done = bf16[768,512]{1,0:T(8,128)(2,1)} async-done(((bf16[768,2048]{1,0:T(8,128)(2,1)}), bf16[768,512]{1,0:T(8,128)(2,1)}) %reduce-scatter.34.cloned.1.call-update) | async-done | bytes 786448 | tf_op jit(solution)/shard_map/reduce_scatter | solution.py:513
  1733.7 28.3 %reduce-scatter.26.cloned.1.call-done = bf16[192,768]{1,0:T(8,128)(2,1)} async-done(((bf16[768,768]{1,0:T(8,128)(2,1)}), bf16[192,768]{1,0:T(8,128)(2,1)}) %reduce-scatter.26.cloned.1.call-update) | async-done | bytes 294928 | tf_op jit(solution)/shard_map/reduce_scatter | solution.py:486
  1762.0 28.9 %reduce-scatter.24.cloned.1.call-done = bf16[192,768]{1,0:T(8,128)(2,1)} async-done(((bf16[768,768]{1,0:T(8,128)(2,1)}), bf16[192,768]{1,0:T(8,128)(2,1)}) %reduce-scatter.24.cloned.1.call-update) | async-done | bytes 294928 | tf_op jit(solution)/shard_map/reduce_scatter | solution.py:483
  1805.9 10.9 all-reduce.9
  1817.0 22.7 %all-reduce.7 = (bf16[192]{0:T(256)(128)(2,1)S(1)}, bf16[8,12]{1,0:T(8,128)(2,1)S(1)}, bf16[192]{0:T(256)(128)(2,1)S(1)}, bf16[192]{0:T(256)(128)(2,1)S(1)}) all-reduce(bf16[192]{0:T(256)(128)(2,1)S(1)} %dynamic-slice.6, bf16[8,12]{1,0:T(8,128)(2,1)S(1)} %constant_dynamic-slice_fusion.4, ...), channel_id=1, replica_groups=mesh['ctx'=8,'fsdp'=4] {'ctx'}, use_global_device_ids=true, to_apply=%region_34.35 | all-reduce | flops 672 | bytes 2688 | tf_op jit(solution)/shard_map/psum | solution.py:524
  1844.8 130.7 %all-reduce.13.cloned.1.call-done = (bf16[192,768]{0,1:T(8,128)(2,1)}, bf16[192,768]{0,1:T(8,128)(2,1)}, bf16[192,768]{1,0:T(8,128)(2,1)}, bf16[192,768]{1,0:T(8...) async-done(((bf16[192,768]{0,1:T(8,128)(2,1)}, ...) | async-done | bytes 4718608 | tf_op jit(solution)/shard_map/psum | solution.py:532
  (354 shorter events, 229.1 us)
Async XLA Ops:
  7.2 61.0 %copy-start = (bf16[1,64,768]{2,1,0:T(8,128)(2,1)S(1)}, bf16[1,64,768]{2,1,0:T(8,128)(2,1)}, u32[]{:S(2)}) copy-start(bf16[1,64,768]{2,1,0:T(8,128)(2,1)} %param.34) | copy-start | bytes 294916
  7.2 16.5 copy-start.15
  7.2 22.7 %all-gather.20.cloned.1.call-start = ((), (), s32[]{:S(2)}) async-start(), calls=%async_computation.16 | async-start | bytes 1474560 | tf_op jit(solution)/shard_map/all_gather | solution.py:290
  8.0 41.2 %all-gather.14.cloned.1.call-start = ((), (), s32[]{:S(2)}) async-start(), calls=%async_computation.13 | async-start | bytes 1474560 | tf_op jit(solution)/shard_map/all_gather | solution.py:289
  8.7 59.5 %all-gather.28.cloned.1.call-start = ((), (), s32[]{:S(2)}) async-start(), calls=%async_computation.20 | async-start | bytes 1474560 | tf_op jit(solution)/shard_map/all_gather | solution.py:295
  9.4 93.6 %all-gather.30.cloned.1.call-start = ((), (), s32[]{:S(2)}) async-start(), calls=%async_computation.21 | async-start | bytes 1474560 | tf_op jit(solution)/shard_map/all_gather | solution.py:296
  10.0 129.6 %all-gather.18.cloned.1.call-start = ((), (), s32[]{:S(2)}) async-start(), calls=%async_computation.15 | async-start | bytes 1474560 | tf_op jit(solution)/shard_map/all_gather | solution.py:288
  10.6 200.2 %all-gather.22.cloned.1.call-start = ((), (), s32[]{:S(2)}) async-start(), calls=%async_computation.17 | async-start | bytes 7077888 | tf_op jit(solution)/shard_map/all_gather | solution.py:345
  23.7 115.9 %copy-start.42 = (f32[768]{0:T(1024)}, f32[768]{0:T(1024)S(1)}, u32[]{:S(2)}) copy-start(f32[768]{0:T(1024)S(1)} %convert_element_type.666) | copy-start | bytes 9220
  23.9 9.0 copy-start.51
  23.9 115.7 %copy-start.47 = (f32[512]{0:T(512)}, f32[512]{0:T(512)S(1)}, u32[]{:S(2)}) copy-start(f32[512]{0:T(512)S(1)} %fusion.153) | copy-start | bytes 6148
  32.9 277.9 %all-gather.16.cloned.1.call-start = ((), (), s32[]{:S(2)}) async-start(), calls=%async_computation.14 | async-start | bytes 7077888 | tf_op jit(solution)/shard_map/all_gather | solution.py:344
  52.1 5.6 copy-start.53
  52.1 323.0 %all-gather.24.cloned.1.call-start = ((), (), s32[]{:S(2)}) async-start(), calls=%async_computation.18 | async-start | bytes 1474560 | tf_op jit(solution)/shard_map/all_gather | solution.py:291
  52.9 325.5 %all-gather.26.cloned.1.call-start = ((), (), s32[]{:S(2)}) async-start(), calls=%async_computation.19 | async-start | bytes 1474560 | tf_op jit(solution)/shard_map/all_gather | solution.py:294
  53.6 342.0 %all-gather.32.cloned.1.call-start = ((), (), s32[]{:S(2)}) async-start(), calls=%async_computation.22 | async-start | bytes 1474560 | tf_op jit(solution)/shard_map/all_gather | solution.py:297
  54.2 345.6 %all-gather.36.cloned.1.call-start = ((), (), s32[]{:S(2)}) async-start(), calls=%async_computation.24 | async-start | bytes 3932160 | tf_op jit(solution)/shard_map/all_gather | solution.py:300
  54.9 371.2 %all-gather.34.cloned.1.call-start = ((), (), s32[]{:S(2)}) async-start(), calls=%async_computation.23 | async-start | bytes 3932160 | tf_op jit(solution)/shard_map/all_gather | solution.py:299
  55.5 400.7 %all-gather.38.cloned.1.call-start = ((), (), s32[]{:S(2)}) async-start(), calls=%async_computation.25 | async-start | bytes 3932160 | tf_op jit(solution)/shard_map/all_gather | solution.py:301
  56.3 633.3 %reduce-scatter.40.cloned.1.call-start = ((), (), s32[]{:S(2)}) async-start(), calls=%async_computation.36 | async-start | bytes 1769472
  378.3 127.0 %copy-start.49 = (f32[512]{0:T(512)}, f32[512]{0:T(512)S(1)}, u32[]{:S(2)}) copy-start(f32[512]{0:T(512)S(1)} %fusion.154) | copy-start | bytes 6148
  387.5 4.6 copy-start.2
  387.6 4.5 copy-start.17
  398.6 69.1 %copy-start.9 = (f32[512,768]{1,0:T(8,128)}, f32[512,768]{1,0:T(8,128)S(1)}, u32[]{:S(2)}) copy-start(f32[512,768]{1,0:T(8,128)S(1)} %get-tuple-element.934) | copy-start | bytes 4718596
  456.3 9.5 copy-start.57
  473.8 31.6 %copy-start.7 = (f32[512,768]{1,0:T(8,128)}, f32[512,768]{1,0:T(8,128)S(1)}, u32[]{:S(2)}) copy-start(f32[512,768]{1,0:T(8,128)S(1)} %fusion.110) | copy-start | bytes 4718596
  477.8 7.0 copy-start.14
  477.8 7.0 copy-start.21
  486.0 6.3 copy-start.19
  498.8 943.6 %reduce-scatter.20.cloned.1.call-start = ((), (), s32[]{:S(2)}) async-start(), calls=%async_computation.26 | async-start | bytes 14155776 | tf_op jit(solution)/shard_map/reduce_scatter | solution.py:460
  499.4 4.3 copy-start.12
  585.6 5.1 copy-start.1
  635.6 834.3 %reduce-scatter.42.cloned.1.call-start = ((), (), s32[]{:S(2)}) async-start(), calls=%async_computation.37 | async-start | bytes 1474560
  692.5 805.5 %reduce-scatter.44.cloned.1.call-start = ((), (), s32[]{:S(2)}) async-start(), calls=%async_computation.38 | async-start | bytes 1474560
  694.6 831.7 %reduce-scatter.32.cloned.1.call-start = ((), (), s32[]{:S(2)}) async-start(), calls=%async_computation.32 | async-start | bytes 1474560 | tf_op jit(solution)/shard_map/reduce_scatter | solution.py:507
  697.8 856.9 %reduce-scatter.30.cloned.1.call-start = ((), (), s32[]{:S(2)}) async-start(), calls=%async_computation.31 | async-start | bytes 1474560 | tf_op jit(solution)/shard_map/reduce_scatter | solution.py:498
  701.1 882.0 %reduce-scatter.28.cloned.1.call-start = ((), (), s32[]{:S(2)}) async-start(), calls=%async_computation.30 | async-start | bytes 1474560 | tf_op jit(solution)/shard_map/reduce_scatter | solution.py:489
  704.1 907.8 %reduce-scatter.22.cloned.1.call-start = ((), (), s32[]{:S(2)}) async-start(), calls=%async_computation.27 | async-start | bytes 1474560 | tf_op jit(solution)/shard_map/reduce_scatter | solution.py:480
  708.7 944.0 %reduce-scatter.38.cloned.1.call-start = ((), (), s32[]{:S(2)}) async-start(), calls=%async_computation.35 | async-start | bytes 3932160 | tf_op jit(solution)/shard_map/reduce_scatter | solution.py:519
  713.8 979.4 %reduce-scatter.36.cloned.1.call-start = ((), (), s32[]{:S(2)}) async-start(), calls=%async_computation.34 | async-start | bytes 3932160 | tf_op jit(solution)/shard_map/reduce_scatter | solution.py:516
  720.0 1013.7 %reduce-scatter.34.cloned.1.call-start = ((), (), s32[]{:S(2)}) async-start(), calls=%async_computation.33 | async-start | bytes 3932160 | tf_op jit(solution)/shard_map/reduce_scatter | solution.py:513
  725.2 1036.8 %reduce-scatter.26.cloned.1.call-start = ((), (), s32[]{:S(2)}) async-start(), calls=%async_computation.29 | async-start | bytes 1474560 | tf_op jit(solution)/shard_map/reduce_scatter | solution.py:486
  1445.6 345.4 %reduce-scatter.24.cloned.1.call-start = ((), (), s32[]{:S(2)}) async-start(), calls=%async_computation.28 | async-start | bytes 1474560 | tf_op jit(solution)/shard_map/reduce_scatter | solution.py:483
  1448.9 526.6 %all-reduce.13.cloned.1.call-start = ((), (), s32[]{:S(2)}) async-start(), calls=%async_computation.39 | async-start | bytes 9830400 | tf_op jit(solution)/shard_map/psum | solution.py:532
  1794.8 4.8 copy-start.22
  1794.8 7.2 copy-start.58
  1803.6 38.5 %copy-start.52 = (f32[512]{0:T(512)S(1)}, f32[512]{0:T(512)}, u32[]{:S(2)}) copy-start(f32[512]{0:T(512)} %copy-done.51) | copy-start | bytes 6148
  1975.5 4.9 copy-start.40
  (44 other events, 110.4 us)
Sparse Core Ops, SparseCore 0:
  9.6 20.2 all-gather.19
  31.4 17.6 all-gather.13
  50.7 17.4 all-gather.27
  69.6 17.4 all-gather.29
  88.5 17.4 all-gather.17
  108.7 102.1 all-gather.21
  213.6 97.1 all-gather.15
  312.4 15.6 all-gather.23
  329.6 17.4 all-gather.25
  348.5 17.4 all-gather.31
  367.6 28.5 all-gather.35
  397.6 28.5 all-gather.33
  427.7 28.5 all-gather.37
  499.0 190.5 reduce-scatter.39
  693.5 748.8 reduce-scatter.19
  1445.0 24.8 reduce-scatter.41
  1472.3 25.7 reduce-scatter.43
  1500.6 25.7 reduce-scatter.31
  1528.9 25.7 reduce-scatter.29
  1557.3 25.7 reduce-scatter.27
  1586.2 25.7 reduce-scatter.21
  1614.6 37.9 reduce-scatter.37
  1655.2 37.9 reduce-scatter.35
  1695.7 37.9 reduce-scatter.33
  1736.3 25.7 reduce-scatter.25
  1765.2 25.7 reduce-scatter.23
  1796.4 179.0 all-reduce.12
where the time goes:
time: 2010 us; the launch traced here: 2000 us
  waiting for transfers between devices  1480 us (74%)
  matrix products  187 us (9%)
  local copies, waits for them, and re-layouts  132 us (7%)
  blocking collectives  113 us (6%)
  other arithmetic  54.6 us (3%)
    reduce_scatter x1, waiting for transfers between devices, shards(): lax.psum_scatter(grad_kv_full.astype(jnp.bfloat16), 'ctx', scatter_dimens...  717 us
    psum x1, waiting for transfers between devices, shards(): lax.psum(shares[8].astype(jnp.bfloat16), 'ctx').astype(jnp.float32)  131 us
    unnamed x30, waiting for transfers between devices  108 us
    all_gather x1, waiting for transfers between devices, shards(): lax.all_gather(key_proj, 'ctx', axis=0, tiled=True)  90.9 us
    all_gather x1, waiting for transfers between devices, shards(): lax.all_gather(value_proj, 'ctx', axis=0, tiled=True)  67.9 us
    reduce_scatter x1, waiting for transfers between devices, shards(): lax.psum_scatter(grad_down.astype(jnp.bfloat16), 'fsdp', scatter_dimensio...  40.7 us
    reduce_scatter x1, waiting for transfers between devices, shards(): lax.psum_scatter(grad_w_up.astype(jnp.bfloat16), 'fsdp', scatter_dimensio...  40.5 us
    reduce_scatter x1, waiting for transfers between devices, shards(): lax.psum_scatter(grad_w_gate.astype(jnp.bfloat16), 'fsdp', scatter_dimens...  40.5 us
  transfers between devices with their start and end apart: 27, of which 21 were waited for; matrix products, arithmetic and copies ran while one was open for 16% of the time, Pallas kernels for 0%

commit v1 on v0

v1 whole, which is shorter than its diff:
```python
import functools
import math

import jax
import jax.numpy as jnp
from jax import lax
from jax.experimental import pallas as pl
from jax.experimental.pallas import tpu as pltpu
from jax.sharding import PartitionSpec as P

D = 768
H = 12
DH = 64
NB = 32
MAXD = 128
GROUPS = 4
GH = H // GROUPS
GL = GH * DH
GP = 256

epsilon = 1e-06
negative = -1e30
f32 = jnp.float32
bf16 = jnp.bfloat16
VMEM_LIMIT = 60 * 1024 * 1024


def thresholds():
    exact = NB // 2
    return list(range(1, exact + 1)) + [
        math.ceil(exact * (MAXD / exact) ** (t / exact)) for t in range(1, exact)
    ]


def matmul(a, b):
    return jnp.dot(a, b, preferred_element_type=f32)


def left_matmul(a, b):
    return lax.dot_general(a, b, (((0,), (0,)), ((), ())), preferred_element_type=f32)


def right_matmul(a, b):
    return lax.dot_general(a, b, (((1,), (1,)), ((), ())), preferred_element_type=f32)


def inverse_rms(v):
    return lax.rsqrt(jnp.mean(v * v, axis=-1, keepdims=True) + epsilon)


def norm_back(v, g, e):
    r = inverse_rms(v)
    ge = e * g
    grad_v = r * ge - v * (r * r * r * jnp.mean(ge * v, axis=-1, keepdims=True))
    return grad_v, jnp.sum(e * v * r, axis=0)


def flip(x):
    return x.astype(f32).T.astype(bf16)


def sub_of(i, split, parts):
    return jnp.where(i % 2 == 0, split, parts - 1 - split)


def doc_start(pos, meta):
    start = jnp.zeros_like(pos)
    for d in range(3):
        start = jnp.where(pos >= meta[d], meta[d], start)
    return start


def tile_bias(table, h, base, rows, cols):
    offset = base + (
        lax.broadcasted_iota(jnp.int32, (rows, cols), 1)
        - lax.broadcasted_iota(jnp.int32, (rows, cols), 0)
    )
    bias = jnp.full((rows, cols), table[0, h], f32)
    for b, at in enumerate(thresholds()):
        bias = jnp.where(offset >= at, table[b + 1, h], bias)
    return bias


def head_rows(x_t, h):
    parts = []
    if h:
        parts.append(jnp.zeros((h * DH, x_t.shape[1]), x_t.dtype))
    parts.append(x_t[h * DH : (h + 1) * DH])
    parts.append(jnp.zeros((GP - (h + 1) * DH, x_t.shape[1]), x_t.dtype))
    return jnp.concatenate(parts, axis=0)


def head_lanes(x, h):
    lane = lax.broadcasted_iota(jnp.int32, x.shape, 1)
    keep = (lane >= h * DH) & (lane < (h + 1) * DH)
    return jnp.where(keep, x.astype(f32), 0.0).astype(bf16)


def sweep(meta, first, block, step):
    start_lo = doc_start(first, meta)
    start_hi = doc_start(first + block - 1, meta)
    far_end = jnp.maximum(first // block - 1, 0)
    lo = jnp.minimum(start_lo // block, far_end)
    mid = jnp.clip((start_hi + block - 1) // block, lo, far_end)

    def masked(t, carry):
        step(pl.multiple_of(t * block, block), block, "masked")
        return carry

    lax.fori_loop(lo, mid, masked, 0)
    odd = (far_end - mid) % 2

    @pl.when(odd == 1)
    def _():
        step(pl.multiple_of(mid * block, block), block, "far")

    def far(t, carry):
        step(pl.multiple_of((mid + odd + 2 * t) * block, block), 2 * block, "far")
        return carry

    lax.fori_loop(0, (far_end - mid) // 2, far, 0)

    @pl.when(first > 0)
    def _():
        step(pl.multiple_of(jnp.maximum(first - block, 0), block), block, "prev")

    step(pl.multiple_of(first, block), block, "diag")


def tile_mask(kind, k0, rows, first, block, starts):
    key = k0 + lax.broadcasted_iota(jnp.int32, (rows, block), 0)
    mask = key >= starts
    if kind == "diag":
        query = first + lax.broadcasted_iota(jnp.int32, (rows, block), 1)
        mask = mask & (key <= query)
    return mask


def self_forward_kernel(
    parts, tok, meta, table, q_ref, k_ref, v_ref, o_ref, full_ref, lse_ref,
    v_t, bias, acc, top, total, q_masked,
):
    i = pl.program_id(0)
    block = tok // parts
    first = i * tok + sub_of(i, meta[3], parts) * block

    @pl.when(i == 0)
    def _():
        for h in range(GH):
            bias[h, 0] = tile_bias(table, h, 0, block, block)
            bias[h, 1] = tile_bias(table, h, block, block, block)

        def turn(t, carry):
            at = pl.multiple_of(t * block, block)
            v_t[:, pl.ds(at, block)] = flip(v_ref[pl.ds(at, block), :])
            return carry

        lax.fori_loop(0, v_ref.shape[0] // block, turn, 0)

    q_t = flip(q_ref[...])
    for h in range(GH):
        q_masked[h] = head_rows(q_t, h)
    top[...] = jnp.full_like(top, negative)
    total[...] = jnp.zeros_like(total)
    acc[...] = jnp.zeros_like(acc)
    starts = doc_start(first + lax.broadcasted_iota(jnp.int32, (1, block), 1), meta)

    def step(k0, rows, kind):
        k_tile = k_ref[pl.ds(k0, rows), :]
        if kind != "far":
            mask = tile_mask(kind, k0, rows, first, block, starts)
        for h in range(GH):
            s = matmul(k_tile, q_masked[h])
            shift = table[NB - 1, h]
            if kind == "diag":
                s, shift = s + bias[h, 0], 0.0
            elif kind == "prev":
                s, shift = s + bias[h, 1], 0.0
            if kind != "far":
                s = jnp.where(mask, s, negative)
            old = top[h : h + 1]
            new = jnp.maximum(old, jnp.max(s, axis=0, keepdims=True) + shift)
            scale = jnp.exp(old - new)
            p = jnp.exp(s - (new - shift))
            top[h : h + 1] = new
            total[h : h + 1] = total[h : h + 1] * scale + jnp.sum(p, axis=0, keepdims=True)
            rows_h = slice(h * DH, (h + 1) * DH)
            acc[rows_h] = acc[rows_h] * scale + matmul(
                v_t[rows_h, pl.ds(k0, rows)], p.astype(bf16)
            )

    sweep(meta, first, block, step)
    for h in range(GH):
        rows_h = slice(h * DH, (h + 1) * DH)
        acc[rows_h] = acc[rows_h] / total[h : h + 1]
    full_ref[...] = acc[:GL]
    o_ref[0] = acc[...].T[:, :GL].astype(bf16)
    lse_ref[...] = jnp.zeros_like(lse_ref)
    lse_ref[0:GH] = top[0:GH] + jnp.log(total[0:GH])


def self_backward_kernel(
    parts, tok, meta, table, q_ref, k_ref, v_ref, do_ref, full_ref, lse_ref, out_ref, tab_ref,
    k_t, bias, dk, dv, dq_t, near, far_sum, q_masked, do_masked, q_lanes, do_lanes, delta,
):
    i = pl.program_id(0)
    block = tok // parts
    first = i * tok + sub_of(i, meta[3], parts) * block
    length = k_ref.shape[0]

    @pl.when(i == 0)
    def _():
        for h in range(GH):
            bias[h, 0] = tile_bias(table, h, 0, block, block)
            bias[h, 1] = tile_bias(table, h, block, block, block)
        near[...] = jnp.zeros_like(near)
        far_sum[...] = jnp.zeros_like(far_sum)

        def turn(t, carry):
            at = pl.multiple_of(t * block, block)
            rows = pl.ds(at, block)
            k_t[:, rows] = flip(k_ref[rows, :])
            dk[rows, :] = jnp.zeros((block, GP), f32)
            dv[rows, :] = jnp.zeros((block, GP), f32)
            out_ref[rows, 0:GP] = jnp.zeros((block, GP), bf16)
            return carry

        lax.fori_loop(0, length // block, turn, 0)

    do_full = do_ref[0]
    q_t = flip(q_ref[...])
    do_t = do_full.astype(f32).T
    for h in range(GH):
        rows_h = slice(h * DH, (h + 1) * DH)
        delta[h : h + 1] = jnp.sum(do_t[rows_h] * full_ref[rows_h], axis=0, keepdims=True)
        q_masked[h] = head_rows(q_t, h)
        do_masked[h] = head_rows(do_t.astype(bf16), h)
        q_lanes[h * block : (h + 1) * block] = head_lanes(q_ref[...], h)
        do_lanes[h * block : (h + 1) * block] = head_lanes(do_full, h)
    dq_t[...] = jnp.zeros_like(dq_t)
    starts = doc_start(first + lax.broadcasted_iota(jnp.int32, (1, block), 1), meta)

    def step(k0, rows, kind):
        at = pl.ds(k0, rows)
        k_tile = k_ref[at, :]
        v_tile = v_ref[at, :]
        if kind != "far":
            mask = tile_mask(kind, k0, rows, first, block, starts)
        probs, grads = [], []
        for h in range(GH):
            s = matmul(k_tile, q_masked[h])
            shift = lse_ref[h : h + 1]
            if kind == "diag":
                s = s + bias[h, 0]
            elif kind == "prev":
                s = s + bias[h, 1]
            else:
                shift = shift - table[NB - 1, h]
            p = jnp.exp(s - shift)
            if kind != "far":
                p = jnp.where(mask, p, 0.0)
            ds = p * (matmul(v_tile, do_masked[h]) - delta[h : h + 1])
            if kind == "diag":
                near[h, 0] += ds
            elif kind == "prev":
                near[h, 1] += ds
            else:
                far_sum[h : h + 1] += jnp.sum(ds, axis=0, keepdims=True)
            probs.append(p.astype(bf16))
            grads.append(ds.astype(bf16))
            rows_h = slice(h * DH, (h + 1) * DH)
            dq_t[rows_h] += matmul(k_t[rows_h, at], grads[h])
        dv[at, :] += matmul(jnp.concatenate(probs, axis=1), do_lanes[...])
        dk[at, :] += matmul(jnp.concatenate(grads, axis=1), q_lanes[...])

    sweep(meta, first, block, step)
    out_ref[pl.ds(pl.multiple_of(first, block), block), 0:GP] = dq_t[...].T.astype(bf16)

    @pl.when(i == pl.num_programs(0) - 1)
    def _():
        def emit(t, carry):
            rows = pl.ds(pl.multiple_of(t * block, block), block)
            out_ref[rows, GP : 2 * GP] = dk[rows, :].astype(bf16)
            out_ref[rows, 2 * GP : 3 * GP] = dv[rows, :].astype(bf16)
            return carry

        lax.fori_loop(0, length // block, emit, 0)
        offset = lax.broadcasted_iota(jnp.int32, (block, block), 1) - lax.broadcasted_iota(
            jnp.int32, (block, block), 0
        )
        edges = [None] + thresholds()
        for h in range(GH):
            tails = []
            for at in edges:
                if at is None:
                    part = near[h, 0] + near[h, 1]
                else:
                    part = jnp.where(offset >= at, near[h, 0], 0.0) + jnp.where(
                        offset + block >= at, near[h, 1], 0.0
                    )
                tails.append(jnp.sum(part, axis=0, keepdims=True))
            for b in range(NB):
                if b + 1 < NB:
                    row = tails[b] - tails[b + 1]
                else:
                    row = tails[b] + far_sum[h : h + 1]
                tab_ref[h * NB + b : h * NB + b + 1] = row


def self_specs(parts, tok, length):
    block = tok // parts
    q_spec = pl.BlockSpec((block, GP), lambda i, m: (i * parts + sub_of(i, m[3], parts), 0))
    k_spec = pl.BlockSpec((length, GP), lambda i, m: (0, 1), pipeline_mode=pl.Buffered(1))
    v_spec = pl.BlockSpec((length, GP), lambda i, m: (0, 2), pipeline_mode=pl.Buffered(1))
    table_spec = pl.BlockSpec(memory_space=pltpu.SMEM)
    return table_spec, q_spec, k_spec, v_spec


def pair_count(length):
    return GH * length * length // 8


def self_forward(qkv, meta, table, parts, count, tok):
    length = qkv.shape[0]
    block = tok // parts
    rows = count * block
    return pl.pallas_call(
        functools.partial(self_forward_kernel, parts, tok),
        grid_spec=pltpu.PrefetchScalarGridSpec(
            num_scalar_prefetch=1,
            grid=(count,),
            in_specs=list(self_specs(parts, tok, length)),
            out_specs=[
                pl.BlockSpec((1, block, GL), lambda i, m: (i, 0, 0)),
                pl.BlockSpec((GL, block), lambda i, m: (0, i)),
                pl.BlockSpec((8, block), lambda i, m: (0, i)),
            ],
            scratch_shapes=[
                pltpu.VMEM((GP, length), bf16),
                pltpu.VMEM((GH, 2, block, block), f32),
                pltpu.VMEM((GP, block), f32),
                pltpu.VMEM((8, block), f32),
                pltpu.VMEM((8, block), f32),
                pltpu.VMEM((GH, GP, block), bf16),
            ],
        ),
        out_shape=[
            jax.ShapeDtypeStruct((count, block, GL), bf16),
            jax.ShapeDtypeStruct((GL, rows), f32),
            jax.ShapeDtypeStruct((8, rows), f32),
        ],
        compiler_params=pltpu.CompilerParams(vmem_limit_bytes=VMEM_LIMIT),
        cost_estimate=pl.CostEstimate(
            flops=pair_count(length) * 1024,
            transcendentals=pair_count(length),
            bytes_accessed=length * GP * 8,
        ),
        name="self_forward",
    )(meta, table, qkv, qkv, qkv)


def self_backward(qkv, meta, table, d_o, full, lse, parts, count, tok):
    length = qkv.shape[0]
    block = tok // parts
    return pl.pallas_call(
        functools.partial(self_backward_kernel, parts, tok),
        grid_spec=pltpu.PrefetchScalarGridSpec(
            num_scalar_prefetch=1,
            grid=(count,),
            in_specs=list(self_specs(parts, tok, length))
            + [
                pl.BlockSpec((1, block, GP), lambda i, m: (i, 0, 0)),
                pl.BlockSpec((GL, block), lambda i, m: (0, i)),
                pl.BlockSpec((8, block), lambda i, m: (0, i)),
            ],
            out_specs=[
                pl.BlockSpec((length, 3 * GP), lambda i, m: (0, 0), pipeline_mode=pl.Buffered(1)),
                pl.BlockSpec((GH * NB, block), lambda i, m: (0, 0)),
            ],
            scratch_shapes=[
                pltpu.VMEM((GP, length), bf16),
                pltpu.VMEM((GH, 2, block, block), f32),
                pltpu.VMEM((length, GP), f32),
                pltpu.VMEM((length, GP), f32),
                pltpu.VMEM((GP, block), f32),
                pltpu.VMEM((GH, 2, block, block), f32),
                pltpu.VMEM((8, block), f32),
                pltpu.VMEM((GH, GP, block), bf16),
                pltpu.VMEM((GH, GP, block), bf16),
                pltpu.VMEM((GH * block, GP), bf16),
                pltpu.VMEM((GH * block, GP), bf16),
                pltpu.VMEM((8, block), f32),
            ],
        ),
        out_shape=[
            jax.ShapeDtypeStruct((length, 3 * GP), bf16),
            jax.ShapeDtypeStruct((GH * NB, block), f32),
        ],
        compiler_params=pltpu.CompilerParams(vmem_limit_bytes=VMEM_LIMIT),
        cost_estimate=pl.CostEstimate(
            flops=pair_count(length) * 2560,
            transcendentals=pair_count(length),
            bytes_accessed=length * GP * 16,
        ),
        name="self_backward",
    )(meta, table, qkv, qkv, qkv, d_o, full, lse)


PAIR = 2 * DH


def pair_rows(x_t, h):
    zeros = jnp.zeros((DH, x_t.shape[1]), x_t.dtype)
    own = x_t[h * DH : (h + 1) * DH]
    return jnp.concatenate([own, zeros] if h == 0 else [zeros, own], axis=0)


def cross_forward_kernel(q_ref, k_ref, v_ref, o_ref, full_ref, lse_ref, v_t, q_t):
    tok = q_ref.shape[0]
    chunk = math.gcd(tok, 256)
    v_t[...] = flip(v_ref[...])
    q_t[...] = flip(q_ref[...])
    lse_ref[...] = jnp.zeros_like(lse_ref)
    for at in range(0, tok, chunk):
        cols = slice(at, at + chunk)
        for h in range(2):
            rows_h = slice(h * DH, (h + 1) * DH)
            s = matmul(k_ref[...], pair_rows(q_t[:, cols], h))
            top = jnp.max(s, axis=0, keepdims=True)
            p = jnp.exp(s - top)
            total = jnp.sum(p, axis=0, keepdims=True)
            full_ref[rows_h, cols] = matmul(v_t[rows_h], p.astype(bf16)) / total
            lse_ref[h : h + 1, cols] = top + jnp.log(total)
    o_ref[...] = full_ref[...].T.astype(bf16)


def cross_backward_kernel(
    q_ref, k_ref, v_ref, do_ref, full_ref, lse_ref, dq_ref, dk_ref, dv_ref, k_t, q_t, do_t, dq_t,
    dk, dv,
):
    tok = q_ref.shape[0]
    chunk = math.gcd(tok, 256)
    k_t[...] = flip(k_ref[...])
    q_t[...] = flip(q_ref[...])
    do_t[...] = do_ref[...].astype(f32).T
    for at in range(0, tok, chunk):
        cols = slice(at, at + chunk)
        probs, grads, q_lanes, do_lanes = [], [], [], []
        for h in range(2):
            rows_h = slice(h * DH, (h + 1) * DH)
            s = matmul(k_ref[...], pair_rows(q_t[:, cols], h))
            p = jnp.exp(s - lse_ref[h : h + 1, cols])
            delta = jnp.sum(do_t[rows_h, cols] * full_ref[rows_h, cols], axis=0, keepdims=True)
            dp = matmul(v_ref[...], pair_rows(do_t[:, cols].astype(bf16), h))
            ds = (p * (dp - delta)).astype(bf16)
            probs.append(p.astype(bf16))
            grads.append(ds)
            dq_t[rows_h, cols] = matmul(k_t[rows_h], ds)
            q_lanes.append(head_lanes(q_ref[cols, :], h))
            do_lanes.append(head_lanes(do_ref[cols, :], h))
        part_v = matmul(jnp.concatenate(probs, axis=1), jnp.concatenate(do_lanes, axis=0))
        part_k = matmul(jnp.concatenate(grads, axis=1), jnp.concatenate(q_lanes, axis=0))
        if at == 0:
            dv[...] = part_v
            dk[...] = part_k
        else:
            dv[...] += part_v
            dk[...] += part_k
    dq_ref[...] = dq_t[...].T.astype(bf16)
    dk_ref[...] = dk[...].astype(bf16)
    dv_ref[...] = dv[...].astype(bf16)


def cross_forward(q, k, v):
    tok, enc = q.shape[0], k.shape[0]
    pairs = H // 2
    col = lambda p: (0, p)
    row = lambda p: (p, 0)
    return pl.pallas_call(
        cross_forward_kernel,
        grid=(pairs,),
        in_specs=[
            pl.BlockSpec((tok, PAIR), col),
            pl.BlockSpec((enc, PAIR), col),
            pl.BlockSpec((enc, PAIR), col),
        ],
        out_specs=[
            pl.BlockSpec((tok, PAIR), col),
            pl.BlockSpec((PAIR, tok), row),
            pl.BlockSpec((8, tok), row),
        ],
        out_shape=[
            jax.ShapeDtypeStruct((tok, D), bf16),
            jax.ShapeDtypeStruct((D, tok), f32),
            jax.ShapeDtypeStruct((8 * pairs, tok), f32),
        ],
        scratch_shapes=[pltpu.VMEM((PAIR, enc), bf16), pltpu.VMEM((PAIR, tok), bf16)],
        compiler_params=pltpu.CompilerParams(vmem_limit_bytes=VMEM_LIMIT),
        cost_estimate=pl.CostEstimate(
            flops=H * tok * enc * 1024, transcendentals=H * tok * enc, bytes_accessed=D * tok * 12
        ),
        name="cross_forward",
    )(q, k, v)


def cross_backward(q, k, v, d_o, full, lse):
    tok, enc = q.shape[0], k.shape[0]
    pairs = H // 2
    col = lambda p: (0, p)
    row = lambda p: (p, 0)
    return pl.pallas_call(
        cross_backward_kernel,
        grid=(pairs,),
        in_specs=[
            pl.BlockSpec((tok, PAIR), col),
            pl.BlockSpec((enc, PAIR), col),
            pl.BlockSpec((enc, PAIR), col),
            pl.BlockSpec((tok, PAIR), col),
            pl.BlockSpec((PAIR, tok), row),
            pl.BlockSpec((8, tok), row),
        ],
        out_specs=[
            pl.BlockSpec((tok, PAIR), col),
            pl.BlockSpec((enc, PAIR), col),
            pl.BlockSpec((enc, PAIR), col),
        ],
        out_shape=[
            jax.ShapeDtypeStruct((tok, D), bf16),
            jax.ShapeDtypeStruct((enc, D), bf16),
            jax.ShapeDtypeStruct((enc, D), bf16),
        ],
        scratch_shapes=[
            pltpu.VMEM((PAIR, enc), bf16),
            pltpu.VMEM((PAIR, tok), bf16),
            pltpu.VMEM((PAIR, tok), f32),
            pltpu.VMEM((PAIR, tok), f32),
            pltpu.VMEM((enc, PAIR), f32),
            pltpu.VMEM((enc, PAIR), f32),
        ],
        compiler_params=pltpu.CompilerParams(vmem_limit_bytes=VMEM_LIMIT),
        cost_estimate=pl.CostEstimate(
            flops=H * tok * enc * 2560, transcendentals=H * tok * enc, bytes_accessed=D * tok * 20
        ),
        name="cross_backward",
    )(q, k, v, d_o, full, lse)


def gelu_pair(v):
    inner = math.sqrt(2 / math.pi) * (v + 0.044715 * (v * v * v))
    t = jnp.tanh(inner)
    half = 0.5 * (1.0 + t)
    slope = half + 0.5 * v * (1.0 - t * t) * (
        math.sqrt(2 / math.pi) * (1.0 + 3 * 0.044715 * (v * v))
    )
    return v * half, slope


def ffn_kernel(
    x_ref, c_ref, gate_ref, up_ref, down_ref, out_ref, gx_ref, dg_ref, du_ref, dd_ref, x_t
):
    f = pl.program_id(0)

    @pl.when(f == 0)
    def _():
        x_t[...] = flip(x_ref[...])
        out_ref[...] = jnp.zeros_like(out_ref)
        gx_ref[...] = jnp.zeros_like(gx_ref)

    x = x_ref[...]
    c = c_ref[...]
    w_gate, w_up, w_down = gate_ref[0], up_ref[0], down_ref[0]
    gate = matmul(x, w_gate)
    up = matmul(x, w_up)
    act, slope = gelu_pair(gate)
    hidden_full = act * up
    hidden = hidden_full.astype(bf16)
    out_ref[...] += matmul(hidden, w_down)
    grad_hidden = right_matmul(c, w_down)
    dd_ref[0] = matmul(hidden.astype(f32).T.astype(bf16), c).astype(bf16)
    grad_gate = (grad_hidden * up * slope).astype(bf16)
    grad_up = (grad_hidden * act).astype(bf16)
    dg_ref[0] = matmul(x_t[...], grad_gate).astype(bf16)
    du_ref[0] = matmul(x_t[...], grad_up).astype(bf16)
    gx_ref[...] += right_matmul(grad_gate, w_gate) + right_matmul(grad_up, w_up)


def ffn(x, c, gate, up, down):
    tok = x.shape[0]
    parts, _, width = gate.shape
    whole = pl.BlockSpec((tok, D), lambda f: (0, 0))
    wide = pl.BlockSpec((1, D, width), lambda f: (f, 0, 0))
    tall = pl.BlockSpec((1, width, D), lambda f: (f, 0, 0))
    total = parts * width
    return pl.pallas_call(
        ffn_kernel,
        grid=(parts,),
        in_specs=[whole, whole, wide, wide, tall],
        out_specs=[whole, whole, wide, wide, tall],
        out_shape=[
            jax.ShapeDtypeStruct((tok, D), f32),
            jax.ShapeDtypeStruct((tok, D), f32),
            jax.ShapeDtypeStruct(gate.shape, bf16),
            jax.ShapeDtypeStruct(gate.shape, bf16),
            jax.ShapeDtypeStruct(down.shape, bf16),
        ],
        scratch_shapes=[pltpu.VMEM((D, tok), bf16)],
        compiler_params=pltpu.CompilerParams(vmem_limit_bytes=VMEM_LIMIT),
        cost_estimate=pl.CostEstimate(
            flops=18 * tok * D * total, transcendentals=tok * total, bytes_accessed=12 * D * total
        ),
        name="feed_forward",
    )(x, c, gate, up, down)


def shards(
    inputs,
    encoded,
    doc_lengths,
    self_gain,
    self_query,
    self_key,
    self_value,
    self_output,
    bias_table,
    cross_gain,
    cross_query,
    cross_key,
    cross_value,
    cross_output,
    ffn_gain,
    ffn_gate,
    ffn_up,
    ffn_down,
    cotangent,
):
    count = lax.axis_size("ctx")
    owners = lax.axis_size("fsdp")
    parts = count // GROUPS
    lines = count // 2
    me = lax.axis_index("ctx")
    group, split = me // parts, me % parts
    line, side = me // 2, me % 2
    tok = inputs.shape[1]
    block = tok // parts
    length = count * tok
    rows = self_query.shape[0]

    swap = [(i, i ^ 1) for i in range(count)]
    ring = [(i, (i + 2) % count) for i in range(count)]

    def columns(w):
        return lax.dynamic_slice(w, (0, group * GL), (rows, GL))

    def as_row(v):
        v = v.reshape(1, -1)
        return jnp.pad(v, ((0, 0), (0, 3 * GL - v.shape[1])))

    packed = jnp.concatenate(
        [columns(self_query), columns(self_key), columns(self_value)], axis=1
    )
    packed = jnp.concatenate(
        [packed, as_row(jnp.concatenate([self_gain, cross_gain, ffn_gain])), as_row(bias_table)],
        axis=0,
    )
    packed = jnp.pad(packed, ((0, 14), (0, 0)))
    packed = lax.all_gather(packed, "fsdp", axis=0)
    w_qkv = packed[:, :rows].reshape(D, 3, GL)
    w_qkv = jnp.pad(w_qkv, ((0, 0), (0, 0), (0, GP - GL))).reshape(D, 3 * GP)
    gains = packed[:, rows, : 3 * rows].reshape(owners, 3, rows).transpose(1, 0, 2).reshape(3, D)
    gains = gains.astype(f32)
    gain_self, gain_cross, gain_ffn = gains[0], gains[1], gains[2]
    table_all = packed[:, rows + 1, : bias_table.size].reshape(NB, H).astype(f32)
    table = lax.dynamic_slice(table_all, (0, group * GH), (NB, GH))
    sizes = doc_lengths[0]
    ends = [sizes[0], sizes[0] + sizes[1], sizes[0] + sizes[1] + sizes[2]]
    meta = jnp.stack(ends + [split]).astype(jnp.int32)

    def project(x):
        v = x.astype(f32)
        normed = (v * inverse_rms(v) * gain_self).astype(bf16)
        return normed, matmul(normed, w_qkv).astype(bf16)

    normed_all = jnp.zeros((length, D), bf16)
    qkv = jnp.zeros((length, 3 * GP), bf16)
    piece = inputs[0]
    for s in range(lines):
        at = (line - s) % lines
        beside = lax.ppermute(piece, "ctx", swap)
        following = lax.ppermute(piece, "ctx", ring) if s + 1 < lines else None
        for x, owner in ((piece, 2 * at + side), (beside, 2 * at + 1 - side)):
            normed, projected = project(x)
            normed_all = lax.dynamic_update_slice(normed_all, normed, (owner * tok, 0))
            qkv = lax.dynamic_update_slice(qkv, projected, (owner * tok, 0))
        piece = following

    encoder = lax.all_gather(encoded[0], "ctx", axis=0, tiled=True)
    gather = lambda w: lax.all_gather(w, "fsdp", axis=0, tiled=True)
    w_output = gather(self_output)
    c_query = gather(cross_query)
    c_key = gather(cross_key)
    c_value = gather(cross_value)
    c_output = gather(cross_output)
    w_gate = lax.all_gather(ffn_gate, "fsdp", axis=0)
    w_up = lax.all_gather(ffn_up, "fsdp", axis=0)
    w_down = lax.all_gather(ffn_down, "fsdp", axis=0)

    out_chunks, self_full, lse = self_forward(qkv, meta, table, parts, count, tok)

    def to_owner(chunks):
        got = lax.all_to_all(chunks, "ctx", 0, 0, tiled=True)
        got = got.reshape(GROUPS, parts, block, GL)
        got = jnp.where(me % 2 == 0, got, got[:, ::-1])
        return got.transpose(1, 2, 0, 3).reshape(tok, D)

    def to_groups(x):
        got = x.reshape(parts, block, GROUPS, GL).transpose(2, 0, 1, 3)
        got = jnp.where(me % 2 == 0, got, got[:, ::-1])
        return lax.all_to_all(got.reshape(count, block, GL), "ctx", 0, 0, tiled=True)

    attended = to_owner(out_chunks)
    states = inputs[0].astype(f32)
    first_sum = states + matmul(attended, w_output)
    normed_two = (first_sum * inverse_rms(first_sum) * gain_cross).astype(bf16)
    cross_queries = matmul(normed_two, c_query).astype(bf16)
    cross_keys = matmul(encoder, c_key).astype(bf16)
    cross_values = matmul(encoder, c_value).astype(bf16)
    cross_out, cross_full, cross_lse = cross_forward(cross_queries, cross_keys, cross_values)
    second_sum = first_sum + matmul(cross_out, c_output)
    normed_three = (second_sum * inverse_rms(second_sum) * gain_ffn).astype(bf16)
    outer = cotangent[0]
    down_out, grad_three, d_gate, d_up, d_down = ffn(normed_three, outer, w_gate, w_up, w_down)
    outputs = (second_sum + down_out).astype(bf16)

    def reduce_weight(g):
        share = lax.psum_scatter(g, "fsdp", scatter_dimension=0, tiled=True)
        return lax.psum(share, "ctx").astype(f32)

    d_gate = reduce_weight(d_gate)[0]
    d_up = reduce_weight(d_up)[0]
    d_down = reduce_weight(d_down)[0]

    grad_part, grad_gain_ffn = norm_back(second_sum, gain_ffn, grad_three)
    grad_second = outer.astype(f32) + grad_part
    branch_two = grad_second.astype(bf16)
    grad_cross_out = right_matmul(branch_two, c_output).astype(bf16)
    grad_cq, grad_ck, grad_cv = cross_backward(
        cross_queries, cross_keys, cross_values, grad_cross_out, cross_full, cross_lse
    )
    grad_part, grad_gain_cross = norm_back(first_sum, gain_cross, right_matmul(grad_cq, c_query))
    grad_first = grad_second + grad_part
    branch_one = grad_first.astype(bf16)
    grad_attended = right_matmul(branch_one, w_output).astype(bf16)
    d_o = to_groups(grad_attended)
    d_o = jnp.pad(d_o, ((0, 0), (0, 0), (0, GP - GL)))

    d_c_output = reduce_weight(left_matmul(cross_out, branch_two).astype(bf16))
    d_c_query = reduce_weight(left_matmul(normed_two, grad_cq).astype(bf16))
    d_c_key = reduce_weight(left_matmul(encoder, grad_ck).astype(bf16))
    d_c_value = reduce_weight(left_matmul(encoder, grad_cv).astype(bf16))
    d_output = reduce_weight(left_matmul(attended, branch_one).astype(bf16))
    grad_enc = (right_matmul(grad_ck, c_key) + right_matmul(grad_cv, c_value)).astype(bf16)
    grad_enc = lax.psum_scatter(grad_enc, "ctx", scatter_dimension=0, tiled=True)

    d_qkv, table_rows = self_backward(qkv, meta, table, d_o, self_full, lse, parts, count, tok)

    def partial_at(at):
        return right_matmul(lax.dynamic_slice(d_qkv, (at * tok, 0), (tok, 3 * GP)), w_qkv)

    travelling = None
    for s in range(1, lines + 1):
        at = (line - s) % lines
        theirs = lax.ppermute(partial_at(2 * at + 1 - side).astype(bf16), "ctx", swap)
        both = partial_at(2 * at + side) + theirs.astype(f32)
        if travelling is not None:
            both = both + lax.ppermute(travelling.astype(bf16), "ctx", ring).astype(f32)
        travelling = both
    grad_one = travelling

    d_w = left_matmul(normed_all, d_qkv).reshape(D, 3, GP)[:, :, :GL].reshape(D, 3 * GL)
    d_w = lax.psum_scatter(d_w.astype(bf16), "fsdp", scatter_dimension=0, tiled=True)
    d_w = lax.all_gather(d_w, "ctx", axis=0)
    d_w = jnp.sum(d_w.astype(f32).reshape(GROUPS, parts, rows, 3, GL), axis=1)
    d_w = d_w.transpose(2, 1, 0, 3).reshape(3, rows, D)

    grad_part, grad_gain_self = norm_back(states, gain_self, grad_one)
    grad_states = (grad_first + grad_part).astype(bf16)

    grad_table = jnp.sum(table_rows, axis=1).reshape(GH, NB).T
    grad_table = lax.dynamic_update_slice(jnp.zeros((NB, H), f32), grad_table, (0, group * GH))
    small = jnp.concatenate(
        [grad_gain_self, grad_gain_cross, grad_gain_ffn, grad_table.reshape(-1)]
    )
    small = lax.psum(small, ("fsdp", "ctx"))
    owner = lax.axis_index("fsdp")
    own_gain = lambda k: lax.dynamic_slice(small, (k * D + owner * rows,), (rows,))
    own_table = lax.dynamic_slice(
        small[3 * D :].reshape(NB, H), (owner * (NB // owners), 0), (NB // owners, H)
    )
    return (
        outputs[None],
        grad_states[None],
        grad_enc[None],
        own_gain(0),
        d_w[0],
        d_w[1],
        d_w[2],
        d_output,
        own_table,
        own_gain(1),
        d_c_query,
        d_c_key,
        d_c_value,
        d_c_output,
        own_gain(2),
        d_gate,
        d_up,
        d_down,
    )


def solution(mesh):
    tokens = P("fsdp", "ctx", None)
    row = P("fsdp", None)
    col = P(None, "fsdp")
    vec = P("fsdp")
    in_specs = (
        (tokens, tokens, row, vec, row, row, row, row, row, vec, row, row, row, row, vec)
        + (col, col, row, tokens)
    )
    out_specs = (
        (tokens, tokens, tokens, vec, row, row, row, row, row, vec, row, row, row, row, vec)
        + (col, col, row)
    )
    return jax.shard_map(shards, mesh=mesh, in_specs=in_specs, out_specs=out_specs, check_vma=False)
```

time: 2010 us -> 1030 us (0.51)
  waiting for transfers between devices: 1480 us -> 497 us
  Pallas kernels: 0 us -> 189 us
  matrix products: 187 us -> 85.8 us
  local copies, waits for them, and re-layouts: 132 us -> 59.7 us
  starting transfers between devices: 1.72 us -> 22.3 us
    reduce_scatter x10 -> x8, waiting for transfers between devices: 1010 us -> 261 us  [the longest x6 205 us: reduce_weight(): share = lax.psum_scatter(g, 'fsdp', scatter_dimension=0, tiled=True)]
    all_gather x13 -> x9, waiting for transfers between devices: 231 us -> 0.05 us  [the longest x5 0.05 us: shards(): gather = lambda w: lax.all_gather(w, 'fsdp', axis=0, tiled=True)]
    pallas_call x0 -> x5, Pallas kernels: none -> 189 us  [the longest x1 76.5 us: self_backward(): pl.pallas_call(functools.partial(self_backward_kernel, parts, tok), grid_...]
    ppermute x0 -> x14, waiting for transfers between devices: none -> 121 us  [the longest x3 58.7 us: shards(): both = both + lax.ppermute(travelling.astype(bf16), 'ctx', ring).astype(f32)]
    dot_general x49 -> x32, matrix products: 187 us -> 85.8 us  [the longest x13 30.5 us: matmul(): return jnp.dot(a, b, preferred_element_type=f32)]
    psum x1, waiting for transfers between devices: 131 us -> 51.8 us  [reduce_weight(): return lax.psum(share, 'ctx').astype(f32)]
    unnamed x30 -> x22, waiting for transfers between devices: 108 us -> 57.2 us
    cond x7 -> x0, local copies, waits for them, and re-layouts: 35.4 us -> none  [the longest x2 35.4 us: block_bias(): return lax.cond(min_offset >= far_offset(), block_distant, block_nearby, 0)]
  transfers between devices with their start and end apart: 27 -> 36, of which waited for: 21 -> 21; matrix products, arithmetic and copies ran while one was open for 16% -> 15% of each run, Pallas kernels for 0% -> 8%
where the time goes in v1:
time: 1030 us; the launch traced here: 1020 us
  waiting for transfers between devices  497 us (48%)
  Pallas kernels  189 us (18%)
  blocking collectives  99.2 us (10%)
  matrix products  85.8 us (8%)
  local copies, waits for them, and re-layouts  59.7 us (6%)
  other arithmetic  49.4 us (5%)
  starting transfers between devices  22.3 us (2%)
  between operations  17.3 us (2%)
    reduce_scatter x6, waiting for transfers between devices, reduce_weight(): share = lax.psum_scatter(g, 'fsdp', scatter_dimension=0, tiled=True)  205 us
    pallas_call x1, Pallas kernels, self_backward(): pl.pallas_call(functools.partial(self_backward_kernel, parts, tok), grid_...  76.5 us
    pallas_call x1, Pallas kernels, self_forward(): pl.pallas_call(functools.partial(self_forward_kernel, parts, tok), grid_s...  64.1 us
    ppermute x3, waiting for transfers between devices, shards(): both = both + lax.ppermute(travelling.astype(bf16), 'ctx', ring).astype(f32)  58.7 us
    unnamed x22, waiting for transfers between devices  57.2 us
    reduce_scatter x1, waiting for transfers between devices, shards(): lax.psum_scatter(grad_enc, 'ctx', scatter_dimension=0, tiled=True)  55.6 us
    psum x1, waiting for transfers between devices, reduce_weight(): return lax.psum(share, 'ctx').astype(f32)  51.8 us
    psum x1, blocking collectives, shards(): small = lax.psum(small, ('fsdp', 'ctx'))  46.5 us
  transfers between devices with their start and end apart: 36, of which 21 were waited for; matrix products, arithmetic and copies ran while one was open for 15% of the time, Pallas kernels for 8%

profile of v1, /device:TPU:0, one launch (start us, length us, event | category | flops | bytes accessed | tf_op | source)
XLA Modules:
  0.0 1019.7 jit_solution(15694909891338085923)
XLA Ops:
  12.0 3.0 collective-permute-start
  18.3 15.8 %all-gather = bf16[832,576]{1,0:T(8,128)(2,1)S(1)} all-gather(bf16[208,576]{1,0:T(8,128)(2,1)S(1)} %pad.17), channel_id=2, replica_groups=mesh['ctx'=8,'fsdp'=4] {'fsdp'}, dimensions={0}, use_global_device_ids=true | all-gather | bytes 1198080 | tf_op jit(solution)/shard_map/all_gather | solution.py:666
  42.2 3.1 broadcast.177.clone
  51.5 2.9 fusion.33
  54.4 2.9 fusion.34
  57.3 12.5 %collective-permute-done.2 = bf16[512,768]{1,0:T(8,128)(2,1)S(1)} collective-permute-done((bf16[512,768]{1,0:T(8,128)(2,1)}, bf16[512,768]{1,0:T(8,128)(2,1)S(1)}, u32[]{:S(2)}, u32[]{:S(2)}) %collective-permute-start.2) | collective-permute-done | bytes 786464 | tf_op jit(solution)/shard_map/ppermute | solution.py:688
  77.3 13.6 %collective-permute-done.4 = bf16[512,768]{1,0:T(8,128)(2,1)S(1)} collective-permute-done((bf16[512,768]{1,0:T(8,128)(2,1)S(1)}, bf16[512,768]{1,0:T(8,128)(2,1)S(1)}, u32[]{:S(2)}, u32[]{:S(2)}) %collective-permute-start.4) | collective-permute-done | bytes 786464 | tf_op jit(solution)/shard_map/ppermute | solution.py:688
  98.5 13.2 %collective-permute-done.6 = bf16[512,768]{1,0:T(8,128)(2,1)S(1)} collective-permute-done((bf16[512,768]{1,0:T(8,128)(2,1)S(1)}, bf16[512,768]{1,0:T(8,128)(2,1)S(1)}, u32[]{:S(2)}, u32[]{:S(2)}) %collective-permute-start.6) | collective-permute-done | bytes 786464 | tf_op jit(solution)/shard_map/ppermute | solution.py:688
  114.4 64.1 %self_forward.1 = (bf16[8,256,192]{2,1,0:T(8,128)(2,1)}, f32[192,2048]{1,0:T(8,128)}, f32[8,2048]{1,0:T(8,128)}) custom-call(s32[4]{0:T(128)} %pad_add_fusion.meta, f32[32,3]{1,0:T(8,128)} %constant_dynamic-slice_fusion.1.table, bf16[4096,768]{1,0:T(8,128)(2,1)} %fusion.39.q_ref.k_ref.v_ref, bf16[4096,768]{1,0:T(8,128)(2,1)} %fusion.39.q_ref.k_ref.v_ref, ...), custom_call_target="tpu_custom_call" | custom-call | flops 6442450944 | bytes 8388608 | tf_op jit(solution)/shard_map/self_forward/pallas_call | solution.py:327
  180.7 3.5 all-to-all-start
  184.3 3.0 broadcast.177.clone.1
  188.5 36.8 %all-gather.1 = bf16[1,512,768]{2,1,0:T(8,128)(2,1)S(1)} all-gather(bf16[1,64,768]{2,1,0:T(8,128)(2,1)S(1)} %copy-done.32), channel_id=3, replica_groups=mesh['ctx'=8,'fsdp'=4] {'ctx'}, dimensions={1}, use_global_device_ids=true | all-gather | bytes 884736 | tf_op jit(solution)/shard_map/all_gather | solution.py:696
  227.8 2.9 convolution_convert_fusion.12.v_ref
  230.8 3.0 convolution_convert_fusion.13.k_ref
  237.4 3.5 convolution_convert_fusion.14.q_ref
  241.0 13.6 %cross_forward.1 = (bf16[512,768]{1,0:T(8,128)(2,1)}, f32[768,512]{1,0:T(8,128)}, f32[48,512]{1,0:T(8,128)}) custom-call(bf16[512,768]{1,0:T(8,128)(2,1)} %convolution_convert_fusion.14.q_ref, bf16[512,768]{1,0:T(8,128)(2,1)} %convolution_convert_fusion.13.k_ref, bf16[512,768]{1,0:T(8,128)(2,1)} %convolution_convert_fusion.12.v_ref), custom_call_target="tpu_custom_call" | custom-call | flops 3221225472 | bytes 4718592 | tf_op jit(solution)/shard_map/cross_forward/pallas_call | solution.py:479
  258.1 20.7 %feed_forward.1 = (f32[512,768]{1,0:T(8,128)}, f32[512,768]{1,0:T(8,128)}, bf16[4,768,512]{2,1,0:T(8,128)(2,1)}, bf16[4,768,512]{2,1,0:T(8,128)(2,1)}, bf16[4,512,768]{2,1,0:T(8,128)(2,1)}) custom-call(bf16[512,768]{1,0:T(8,128)(2,1)} %multiply_convert_fusion.x_ref, bf16[512,768]{1,0:T(8,128)(2,1)} %bitcast.135, bf16[4,768,512]{2,1,0:T(8,128)(2,1)} %bitcast.142, ...), custom_call_target="tpu_custom_call" | custom-call | flops 14495514624 | bytes 18874368 | tf_op jit(solution)/shard_map/feed_forward/pallas_call | solution.py:594
  285.4 14.0 %cross_backward.1 = (bf16[512,768]{1,0:T(8,128)(2,1)}, bf16[512,768]{1,0:T(8,128)(2,1)}, bf16[512,768]{1,0:T(8,128)(2,1)}) custom-call(bf16[512,768]{1,0:T(8,128)(2,1)} %convolution_convert_fusion.14.q_ref, bf16[512,768]{1,0:T(8,128)(2,1)} %convolution_convert_fusion.13.k_ref, bf16[512,768]{1,0:T(8,128)(2,1)} %convolution_convert_fusion.12.v_ref, ...), custom_call_target="tpu_custom_call" | custom-call | flops 8053063680 | bytes 7864320 | tf_op jit(solution)/shard_map/cross_backward/pallas_call | solution.py:511
  305.1 3.6 reshape.275
  313.5 4.2 all-to-all-start.1
  325.9 6.1 all-to-all-done.1
  336.7 76.5 %self_backward.1 = (bf16[4096,768]{1,0:T(8,128)(2,1)}, f32[96,256]{1,0:T(8,128)}) custom-call(s32[4]{0:T(128)} %pad_add_fusion.meta, f32[32,3]{1,0:T(8,128)} %constant_dynamic-slice_fusion.1.table, bf16[4096,768]{1,0:T(8,128)(2,1)} %fusion.39.q_ref.k_ref.v_ref, bf16[4096,768]{1,0:T(8,128)(2,1)} %fusion.39.q_ref.k_ref.v_ref, ...), custom_call_target="tpu_custom_call" | custom-call | flops 16106127360 | bytes 16777216 | tf_op jit(solution)/shard_map/self_backward/pallas_call | solution.py:365
  413.1 9.1 convolution_convert_fusion.5
  425.9 3.2 fusion.31
  431.6 3.2 fusion.30
  437.2 3.6 convolution_convert_fusion.3
  440.9 3.0 convolution_convert_fusion
  444.0 2.9 convolution_convert_fusion.4
  452.2 23.6 %reduce-scatter.35.cloned.1.call-done = bf16[192,768]{1,0:T(8,128)(2,1)} async-done(((bf16[768,768]{1,0:T(8,128)(2,1)}), bf16[192,768]{1,0:T(8,128)(2,1)}) %reduce-scatter.35.cloned.1.call-update) | async-done | bytes 294928
  477.7 27.0 %reduce-scatter.33.cloned.1.call-done = bf16[192,768]{1,0:T(8,128)(2,1)} async-done(((bf16[768,768]{1,0:T(8,128)(2,1)}), bf16[192,768]{1,0:T(8,128)(2,1)}) %reduce-scatter.33.cloned.1.call-update) | async-done | bytes 294928
  506.6 26.5 %reduce-scatter.21.cloned.1.call-done = bf16[192,768]{1,0:T(8,128)(2,1)} async-done(((bf16[768,768]{1,0:T(8,128)(2,1)}), bf16[192,768]{1,0:T(8,128)(2,1)}) %reduce-scatter.21.cloned.1.call-update) | async-done | bytes 294928 | tf_op jit(solution)/shard_map/reduce_scatter | solution.py:735
  533.1 28.3 %reduce-scatter.23.cloned.1.call-done = bf16[192,768]{1,0:T(8,128)(2,1)} async-done(((bf16[768,768]{1,0:T(8,128)(2,1)}), bf16[192,768]{1,0:T(8,128)(2,1)}) %reduce-scatter.23.cloned.1.call-update) | async-done | bytes 294928 | tf_op jit(solution)/shard_map/reduce_scatter | solution.py:735
  561.4 28.9 %reduce-scatter.19.cloned.1.call-done = bf16[192,768]{1,0:T(8,128)(2,1)} async-done(((bf16[768,768]{1,0:T(8,128)(2,1)}), bf16[192,768]{1,0:T(8,128)(2,1)}) %reduce-scatter.19.cloned.1.call-update) | async-done | bytes 294928 | tf_op jit(solution)/shard_map/reduce_scatter | solution.py:735
  590.3 40.3 %reduce-scatter.25.cloned.1.call-done = bf16[1,768,512]{2,1,0:T(8,128)(2,1)} async-done(((bf16[4,768,512]{2,1,0:T(8,128)(2,1)}), bf16[1,768,512]{2,1,0:T(8,128)(2,1)}) %reduce-scatter.25.cloned.1.call-update) | async-done | bytes 786448 | tf_op jit(solution)/shard_map/reduce_scatter | solution.py:735
  630.6 40.5 %reduce-scatter.27.cloned.1.call-done = bf16[1,768,512]{2,1,0:T(8,128)(2,1)} async-done(((bf16[4,768,512]{2,1,0:T(8,128)(2,1)}), bf16[1,768,512]{2,1,0:T(8,128)(2,1)}) %reduce-scatter.27.cloned.1.call-update) | async-done | bytes 786448 | tf_op jit(solution)/shard_map/reduce_scatter | solution.py:735
  671.2 40.3 %reduce-scatter.29.cloned.1.call-done = bf16[1,512,768]{2,1,0:T(8,128)(2,1)} async-done(((bf16[4,512,768]{2,1,0:T(8,128)(2,1)}), bf16[1,512,768]{2,1,0:T(8,128)(2,1)}) %reduce-scatter.29.cloned.1.call-update) | async-done | bytes 786448 | tf_op jit(solution)/shard_map/reduce_scatter | solution.py:735
  724.1 12.6 %collective-permute-done.9 = bf16[512,768]{1,0:T(8,128)(2,1)S(1)} collective-permute-done((bf16[512,768]{1,0:T(8,128)(2,1)S(1)}, bf16[512,768]{1,0:T(8,128)(2,1)S(1)}, u32[]{:S(2)}, u32[]{:S(2)}) %collective-permute-start.9) | collective-permute-done | bytes 786464 | tf_op jit(solution)/shard_map/ppermute | solution.py:772
  736.7 9.4 collective-permute-done.11
  752.5 6.2 collective-permute-done.8
  758.7 23.1 %collective-permute-done.12 = bf16[512,768]{1,0:T(8,128)(2,1)} collective-permute-done((bf16[512,768]{1,0:T(8,128)(2,1)}, bf16[512,768]{1,0:T(8,128)(2,1)}, u32[]{:S(2)}, u32[]{:S(2)}) %collective-permute-start.12) | collective-permute-done | bytes 786464 | tf_op jit(solution)/shard_map/ppermute | solution.py:775
  789.0 26.2 %collective-permute-done.13 = bf16[512,768]{1,0:T(8,128)(2,1)S(1)} collective-permute-done((bf16[512,768]{1,0:T(8,128)(2,1)}, bf16[512,768]{1,0:T(8,128)(2,1)S(1)}, u32[]{:S(2)}, u32[]{:S(2)}) %collective-permute-start.13) | collective-permute-done | bytes 786464 | tf_op jit(solution)/shard_map/ppermute | solution.py:775
  815.3 4.0 fusion.27
  819.3 46.5 %psum.63 = f32[2688]{0:T(1024)S(1)} all-reduce(f32[2688]{0:T(1024)S(1)} %pad_maximum_fusion), channel_id=1, replica_groups=mesh['ctx'=8,'fsdp'=4] {'fsdp','ctx'}, use_global_device_ids=true, to_apply=%region_18.19 | all-reduce | flops 2688 | bytes 21504 | tf_op jit(solution)/shard_map/psum | solution.py:793
  867.2 3.1 fusion.45
  872.9 6.0 reshape.264
  878.9 8.7 reduce_sum.191
  895.5 51.8 %all-reduce.7.cloned.1.call-done = (bf16[192,768]{0,1:T(8,128)(2,1)}, bf16[192,768]{0,1:T(8,128)(2,1)}, bf16[192,768]{1,0:T(8,128)(2,1)}, bf16[192,768]{1,0:T(8,...) async-done(((bf16[192,768]{0,1:T(8,128)(2,1)}, bf16[192,768]{0,1:T(8,128)(2,1)}, ...) | async-done | bytes 3833872 | tf_op jit(solution)/shard_map/psum | solution.py:736
  957.1 55.6 %reduce-scatter.17.cloned.1.call-done = bf16[64,768]{1,0:T(8,128)(2,1)} async-done(((bf16[512,768]{1,0:T(8,128)(2,1)}), bf16[64,768]{1,0:T(8,128)(2,1)}) %reduce-scatter.17.cloned.1.call-update) | async-done | bytes 98320 | tf_op jit(solution)/shard_map/reduce_scatter | solution.py:762
  (276 shorter events, 145.8 us)
Async XLA Ops:
  7.2 9.7 copy-start
  7.2 220.6 %all-gather.22.cloned.1.call-start = ((), (), s32[]{:S(2)}) async-start(), calls=%async_computation.15 | async-start | bytes 1474560 | tf_op jit(solution)/shard_map/all_gather | solution.py:697
  8.0 222.8 %all-gather.20.cloned.1.call-start = ((), (), s32[]{:S(2)}) async-start(), calls=%async_computation.14 | async-start | bytes 1474560 | tf_op jit(solution)/shard_map/all_gather | solution.py:697
  8.7 8.0 copy-start.36
  8.7 8.0 copy-start.37
  8.7 8.0 copy-start.38
  8.7 226.2 %all-gather.16.cloned.1.call-start = ((), (), s32[]{:S(2)}) async-start(), calls=%async_computation.12 | async-start | bytes 1474560 | tf_op jit(solution)/shard_map/all_gather | solution.py:697
  9.5 7.3 copy-start.35
  9.5 227.9 %all-gather.18.cloned.1.call-start = ((), (), s32[]{:S(2)}) async-start(), calls=%async_computation.13 | async-start | bytes 1474560 | tf_op jit(solution)/shard_map/all_gather | solution.py:697
  10.1 244.5 %all-gather.24.cloned.1.call-start = ((), (), s32[]{:S(2)}) async-start(), calls=%async_computation.16 | async-start | bytes 1474560 | tf_op jit(solution)/shard_map/all_gather | solution.py:697
  10.6 247.4 %all-gather.26.cloned.1.call-start = ((), (), s32[]{:S(2)}) async-start(), calls=%async_computation.24 | async-start | bytes 3932160 | tf_op jit(solution)/shard_map/all_gather | solution.py:703
  11.2 246.9 %all-gather.28.cloned.1.call-start = ((), (), s32[]{:S(2)}) async-start(), calls=%async_computation.25 | async-start | bytes 3932160 | tf_op jit(solution)/shard_map/all_gather | solution.py:704
  12.0 246.1 %all-gather.30.cloned.1.call-start = ((), (), s32[]{:S(2)}) async-start(), calls=%async_computation.26 | async-start | bytes 3932160 | tf_op jit(solution)/shard_map/all_gather | solution.py:705
  12.0 35.0 %collective-permute-start = (bf16[512,768]{1,0:T(8,128)(2,1)S(1)}, bf16[512,768]{1,0:T(8,128)(2,1)}, u32[]{:S(2)}, u32[]{:S(2)}) collective-permute-start(bf16[512,768]{1,0:T(8,128)(2,1)S(1)} %bitcast.107), channel_id=1, source_target_pairs={{0,4},{4,0},{8,12},{12,8},{16,20},{20,16},{24,28},{28,24},{1,5},{5... | collective-permute-start | bytes 2359304 | tf_op jit(solution)/shard_map/ppermute | solution.py:688
  15.1 33.3 %collective-permute-start.1 = (bf16[512,768]{1,0:T(8,128)(2,1)S(1)}, bf16[512,768]{1,0:T(8,128)(2,1)}, u32[]{:S(2)}, u32[]{:S(2)}) collective-permute-start(bf16[512,768]{1,0:T(8,128)(2,1)S(1)} %bitcast.108), channel_id=1, source_target_pairs={{0,8},{4,12},{8,16},{12,20},{16,24},{20,28},{24,0},{28,4},{1,9},{5... | collective-permute-start | bytes 2359304 | tf_op jit(solution)/shard_map/ppermute | solution.py:689
  37.9 74.1 %copy-start.21 = (bf16[768,3,256]{0,2,1:T(8,128)(2,1)}, bf16[768,3,256]{0,2,1:T(8,128)(2,1)S(1)}, u32[]{:S(2)}) copy-start(bf16[768,3,256]{0,2,1:T(8,128)(2,1)S(1)} %pad.18) | copy-start | bytes 3538948
  49.7 20.1 %collective-permute-start.2 = (bf16[512,768]{1,0:T(8,128)(2,1)}, bf16[512,768]{1,0:T(8,128)(2,1)S(1)}, u32[]{:S(2)}, u32[]{:S(2)}) collective-permute-start(bf16[512,768]{1,0:T(8,128)(2,1)} %collective-permute-done.1), channel_id=1, source_target_pairs={{0,4},{4,0},{8,12},{12,8},{16,20},{20,16},{24,28},{28,24},{1,5},{5... | collective-permute-start | bytes 2359304 | tf_op jit(solution)/shard_map/ppermute | solution.py:688
  49.9 21.8 %collective-permute-start.3 = (bf16[512,768]{1,0:T(8,128)(2,1)}, bf16[512,768]{1,0:T(8,128)(2,1)S(1)}, u32[]{:S(2)}, u32[]{:S(2)}) collective-permute-start(bf16[512,768]{1,0:T(8,128)(2,1)} %collective-permute-done.1), channel_id=1, source_target_pairs={{0,8},{4,12},{8,16},{12,20},{16,24},{20,28},{24,0},{28,4},{1,9},{5... | collective-permute-start | bytes 2359304 | tf_op jit(solution)/shard_map/ppermute | solution.py:689
  69.8 5.8 copy-start.10
  71.9 19.1 %collective-permute-start.4 = (bf16[512,768]{1,0:T(8,128)(2,1)S(1)}, bf16[512,768]{1,0:T(8,128)(2,1)S(1)}, u32[]{:S(2)}, u32[]{:S(2)}) collective-permute-start(bf16[512,768]{1,0:T(8,128)(2,1)S(1)} %collective-permute-done.3), channel_id=1, source_target_pairs={{0,4},{4,0},{8,12},{12,8},{16,20},{20,16},{24,28},{28,24},{1,5},{5... | collective-permute-start | bytes 2359304 | tf_op jit(solution)/shard_map/ppermute | solution.py:688
  73.7 20.3 %collective-permute-start.5 = (bf16[512,768]{1,0:T(8,128)(2,1)S(1)}, bf16[512,768]{1,0:T(8,128)(2,1)S(1)}, u32[]{:S(2)}, u32[]{:S(2)}) collective-permute-start(bf16[512,768]{1,0:T(8,128)(2,1)S(1)} %collective-permute-done.3), channel_id=1, source_target_pairs={{0,8},{4,12},{8,16},{12,20},{16,24},{20,28},{24,0},{28,4},{1,9},{5... | collective-permute-start | bytes 2359304 | tf_op jit(solution)/shard_map/ppermute | solution.py:689
  94.2 17.5 %collective-permute-start.6 = (bf16[512,768]{1,0:T(8,128)(2,1)S(1)}, bf16[512,768]{1,0:T(8,128)(2,1)S(1)}, u32[]{:S(2)}, u32[]{:S(2)}) collective-permute-start(bf16[512,768]{1,0:T(8,128)(2,1)S(1)} %collective-permute-done.5), channel_id=1, source_target_pairs={{0,4},{4,0},{8,12},{12,8},{16,20},{20,16},{24,28},{28,24},{1,5},{5... | collective-permute-start | bytes 2359304 | tf_op jit(solution)/shard_map/ppermute | solution.py:688
  180.7 53.0 %all-to-all-start = ((bf16[8,256,192]{1,2,0:T(8,128)(2,1)}), bf16[8,256,192]{1,2,0:T(8,128)(2,1)S(1)}, u32[]{:S(2)}, u32[]{:S(2)}) async-start(bf16[8,256,192]{1,2,0:T(8,128)(2,1)} %copy.81), calls=%async_computation | async-start | bytes 1572864 | tf_op jit(solution)/shard_map/all_to_all | solution.py:710
  237.4 17.2 %copy-start.5 = (f32[512,768]{1,0:T(8,128)}, f32[512,768]{1,0:T(8,128)S(1)}, u32[]{:S(2)}) copy-start(f32[512,768]{1,0:T(8,128)S(1)} %get-tuple-element.169) | copy-start | bytes 4718596
  285.4 14.0 %copy-start.6 = (f32[512,768]{1,0:T(8,128)S(1)}, f32[512,768]{1,0:T(8,128)}, u32[]{:S(2)}) copy-start(f32[512,768]{1,0:T(8,128)} %copy-done.5) | copy-start | bytes 4718596
  313.5 18.5 %all-to-all-start.1 = ((bf16[8,256,192]{1,2,0:T(8,128)(2,1)}), bf16[8,256,192]{1,2,0:T(8,128)(2,1)}, u32[]{:S(2)}, u32[]{:S(2)}) async-start(bf16[8,256,192]{1,2,0:T(8,128)(2,1)} %bitcast.116), calls=%async_computation.1 | async-start | bytes 1572864 | tf_op jit(solution)/shard_map/all_to_all | solution.py:718
  317.8 131.0 %reduce-scatter.31.cloned.1.call-start = ((), (), s32[]{:S(2)}) async-start(), calls=%async_computation.28 | async-start | bytes 1228800 | tf_op jit(solution)/shard_map/reduce_scatter | solution.py:780
  425.4 50.4 %reduce-scatter.35.cloned.1.call-start = ((), (), s32[]{:S(2)}) async-start(), calls=%async_computation.30 | async-start | bytes 1474560
  431.5 73.2 %reduce-scatter.33.cloned.1.call-start = ((), (), s32[]{:S(2)}) async-start(), calls=%async_computation.29 | async-start | bytes 1474560
  437.2 95.9 %reduce-scatter.21.cloned.1.call-start = ((), (), s32[]{:S(2)}) async-start(), calls=%async_computation.19 | async-start | bytes 1474560 | tf_op jit(solution)/shard_map/reduce_scatter | solution.py:735
  440.8 120.5 %reduce-scatter.23.cloned.1.call-start = ((), (), s32[]{:S(2)}) async-start(), calls=%async_computation.20 | async-start | bytes 1474560 | tf_op jit(solution)/shard_map/reduce_scatter | solution.py:735
  443.9 146.4 %reduce-scatter.19.cloned.1.call-start = ((), (), s32[]{:S(2)}) async-start(), calls=%async_computation.18 | async-start | bytes 1474560 | tf_op jit(solution)/shard_map/reduce_scatter | solution.py:735
  446.9 183.7 %reduce-scatter.25.cloned.1.call-start = ((), (), s32[]{:S(2)}) async-start(), calls=%async_computation.21 | async-start | bytes 3932160 | tf_op jit(solution)/shard_map/reduce_scatter | solution.py:735
  447.5 223.7 %reduce-scatter.27.cloned.1.call-start = ((), (), s32[]{:S(2)}) async-start(), calls=%async_computation.22 | async-start | bytes 3932160 | tf_op jit(solution)/shard_map/reduce_scatter | solution.py:735
  448.1 263.4 %reduce-scatter.29.cloned.1.call-start = ((), (), s32[]{:S(2)}) async-start(), calls=%async_computation.23 | async-start | bytes 3932160 | tf_op jit(solution)/shard_map/reduce_scatter | solution.py:735
  448.7 421.5 %all-gather.32.cloned.1.call-start = ((), (), s32[]{:S(2)}) async-start(), calls=%async_computation.27 | async-start | bytes 2211840 | tf_op jit(solution)/shard_map/all_gather | solution.py:781
  449.3 498.1 %all-reduce.7.cloned.1.call-start = ((), (), s32[]{:S(2)}) async-start(), calls=%async_computation.31 | async-start | bytes 8060928 | tf_op jit(solution)/shard_map/psum | solution.py:736
  452.2 262.9 %collective-permute-start.10 = (bf16[512,768]{1,0:T(8,128)(2,1)}, bf16[512,768]{1,0:T(8,128)(2,1)}, u32[]{:S(2)}, u32[]{:S(2)}) collective-permute-start(bf16[512,768]{1,0:T(8,128)(2,1)} %convolution_convert_fusion.6), channel_id=1, source_target_pairs={{0,4},{4,0},{8,12},{12,8},{16,20},{20,16},{24,28},{28,24},{1,5},{5... | collective-permute-start | bytes 2359304 | tf_op jit(solution)/shard_map/ppermute | solution.py:772
  711.6 301.1 %reduce-scatter.17.cloned.1.call-start = ((), (), s32[]{:S(2)}) async-start(), calls=%async_computation.17 | async-start | bytes 884736 | tf_op jit(solution)/shard_map/reduce_scatter | solution.py:762
  713.5 23.1 %collective-permute-start.9 = (bf16[512,768]{1,0:T(8,128)(2,1)S(1)}, bf16[512,768]{1,0:T(8,128)(2,1)S(1)}, u32[]{:S(2)}, u32[]{:S(2)}) collective-permute-start(bf16[512,768]{1,0:T(8,128)(2,1)S(1)} %convolution_convert_fusion.7), channel_id=1, source_target_pairs={{0,4},{4,0},{8,12},{12,8},{16,20},{20,16},{24,28},{28,24},{1,5},{5... | collective-permute-start | bytes 2359304 | tf_op jit(solution)/shard_map/ppermute | solution.py:772
  717.2 28.8 %collective-permute-start.11 = (bf16[512,768]{1,0:T(8,128)(2,1)S(1)}, bf16[512,768]{1,0:T(8,128)(2,1)S(1)}, u32[]{:S(2)}, u32[]{:S(2)}) collective-permute-start(bf16[512,768]{1,0:T(8,128)(2,1)S(1)} %add_convert_fusion.3), channel_id=1, source_target_pairs={{0,8},{4,12},{8,16},{12,20},{16,24},{20,28},{24,0},{28,4},{1,9},{5... | collective-permute-start | bytes 2359304 | tf_op jit(solution)/shard_map/ppermute | solution.py:775
  721.5 37.2 %collective-permute-start.8 = (bf16[512,768]{1,0:T(8,128)(2,1)}, bf16[512,768]{1,0:T(8,128)(2,1)}, u32[]{:S(2)}, u32[]{:S(2)}) collective-permute-start(bf16[512,768]{1,0:T(8,128)(2,1)} %convolution_convert_fusion.8), channel_id=1, source_target_pairs={{0,4},{4,0},{8,12},{12,8},{16,20},{20,16},{24,28},{28,24},{1,5},{5... | collective-permute-start | bytes 2359304 | tf_op jit(solution)/shard_map/ppermute | solution.py:772
  747.1 34.7 %collective-permute-start.12 = (bf16[512,768]{1,0:T(8,128)(2,1)}, bf16[512,768]{1,0:T(8,128)(2,1)}, u32[]{:S(2)}, u32[]{:S(2)}) collective-permute-start(bf16[512,768]{1,0:T(8,128)(2,1)} %add_convert_fusion.2), channel_id=1, source_target_pairs={{0,8},{4,12},{8,16},{12,20},{16,24},{20,28},{24,0},{28,4},{1,9},{5... | collective-permute-start | bytes 2359304 | tf_op jit(solution)/shard_map/ppermute | solution.py:775
  749.9 39.1 %collective-permute-start.7 = (bf16[512,768]{1,0:T(8,128)(2,1)}, bf16[512,768]{1,0:T(8,128)(2,1)}, u32[]{:S(2)}, u32[]{:S(2)}) collective-permute-start(bf16[512,768]{1,0:T(8,128)(2,1)} %convolution_convert_fusion.9), channel_id=1, source_target_pairs={{0,4},{4,0},{8,12},{12,8},{16,20},{20,16},{24,28},{28,24},{1,5},{5... | collective-permute-start | bytes 2359304 | tf_op jit(solution)/shard_map/ppermute | solution.py:772
  752.5 31.9 %copy-start.42 = (bf16[512,768]{1,0:T(8,128)(2,1)S(1)}, bf16[512,768]{1,0:T(8,128)(2,1)}, u32[]{:S(2)}) copy-start(bf16[512,768]{1,0:T(8,128)(2,1)} %get-tuple-element.44) | copy-start | bytes 2359300
  784.4 30.9 %collective-permute-start.13 = (bf16[512,768]{1,0:T(8,128)(2,1)}, bf16[512,768]{1,0:T(8,128)(2,1)S(1)}, u32[]{:S(2)}, u32[]{:S(2)}) collective-permute-start(bf16[512,768]{1,0:T(8,128)(2,1)} %add_convert_fusion.1), channel_id=1, source_target_pairs={{0,8},{4,12},{8,16},{12,20},{16,24},{20,28},{24,0},{28,4},{1,9},{5... | collective-permute-start | bytes 2359304 | tf_op jit(solution)/shard_map/ppermute | solution.py:775
  786.7 28.6 %copy-start.3 = (bf16[1,512,768]{2,1,0:T(8,128)(2,1)S(1)}, bf16[1,512,768]{2,1,0:T(8,128)(2,1)}, u32[]{:S(2)}) copy-start(bf16[1,512,768]{2,1,0:T(8,128)(2,1)} %param.19) | copy-start | bytes 2359300
  953.4 59.3 %copy-start.1 = (bf16[192,768]{1,0:T(8,128)(2,1)S(1)}, bf16[192,768]{1,0:T(8,128)(2,1)}, u32[]{:S(2)}) copy-start(bf16[192,768]{1,0:T(8,128)(2,1)} %param.23) | copy-start | bytes 884740
  (31 other events, 78.4 us)
Sparse Core Ops, SparseCore 0:
  9.6 25.6 all-gather.21
  36.8 15.8 all-gather.19
  54.3 17.4 all-gather.15
  73.2 17.4 all-gather.17
  92.1 17.4 all-gather.23
  111.0 28.5 all-gather.25
  141.2 28.5 all-gather.27
  171.3 28.4 all-gather.29
  425.6 21.3 reduce-scatter.30
  450.1 25.7 reduce-scatter.34
  479.0 25.7 reduce-scatter.32
  507.3 25.6 reduce-scatter.20
  535.6 25.7 reduce-scatter.22
  564.6 25.6 reduce-scatter.18
  592.7 37.9 reduce-scatter.24
  633.2 37.9 reduce-scatter.26
  673.6 37.9 reduce-scatter.28
  713.8 69.5 all-gather.31
  789.2 158.0 all-reduce.6
  951.4 61.2 reduce-scatter.16

commit v2 on v1

--- a/solution.py
+++ b/solution.py
@@ -201,7 +201,7 @@
 
 def self_backward_kernel(
     parts, tok, meta, table, q_ref, k_ref, v_ref, do_ref, full_ref, lse_ref, out_ref, tab_ref,
-    k_t, bias, dk, dv, dq_t, near, far_sum, q_masked, do_masked, q_lanes, do_lanes, delta,
+    k_t, bias, dk, dv, dq_t, near, far_sum, q_masked, do_masked, q_lanes, do_lanes, delta, do_wide,
 ):
     i = pl.program_id(0)
     block = tok // parts
@@ -215,6 +215,7 @@
             bias[h, 1] = tile_bias(table, h, block, block, block)
         near[...] = jnp.zeros_like(near)
         far_sum[...] = jnp.zeros_like(far_sum)
+        do_wide[...] = jnp.zeros_like(do_wide)
 
         def turn(t, carry):
             at = pl.multiple_of(t * block, block)
@@ -227,9 +228,10 @@
 
         lax.fori_loop(0, length // block, turn, 0)
 
-    do_full = do_ref[0]
+    do_wide[:, :GL] = do_ref[0].astype(f32)
+    do_full = do_wide[...]
     q_t = flip(q_ref[...])
-    do_t = do_full.astype(f32).T
+    do_t = do_full.T
     for h in range(GH):
         rows_h = slice(h * DH, (h + 1) * DH)
         delta[h : h + 1] = jnp.sum(do_t[rows_h] * full_ref[rows_h], axis=0, keepdims=True)
@@ -369,7 +371,7 @@
             grid=(count,),
             in_specs=list(self_specs(parts, tok, length))
             + [
-                pl.BlockSpec((1, block, GP), lambda i, m: (i, 0, 0)),
+                pl.BlockSpec((1, block, GL), lambda i, m: (i, 0, 0)),
                 pl.BlockSpec((GL, block), lambda i, m: (0, i)),
                 pl.BlockSpec((8, block), lambda i, m: (0, i)),
             ],
@@ -390,6 +392,7 @@
                 pltpu.VMEM((GH * block, GP), bf16),
                 pltpu.VMEM((GH * block, GP), bf16),
                 pltpu.VMEM((8, block), f32),
+                pltpu.VMEM((block, GP), f32),
             ],
         ),
         out_shape=[
@@ -545,6 +548,9 @@
     )(q, k, v, d_o, full, lse)
 
 
+LANES = 128
+
+
 def gelu_pair(v):
     inner = math.sqrt(2 / math.pi) * (v + 0.044715 * (v * v * v))
     t = jnp.tanh(inner)
@@ -556,7 +562,7 @@
 
 
 def ffn_kernel(
-    x_ref, c_ref, gate_ref, up_ref, down_ref, out_ref, gx_ref, dg_ref, du_ref, dd_ref, x_t
+    x_ref, c_ref, gate_ref, up_ref, down_ref, out_ref, gx_ref, dw_ref, x_t
 ):
     f = pl.program_id(0)
 
@@ -565,6 +571,12 @@
         x_t[...] = flip(x_ref[...])
         out_ref[...] = jnp.zeros_like(out_ref)
         gx_ref[...] = jnp.zeros_like(gx_ref)
+
+    def emit(g, at):
+        for lane in range(0, g.shape[1], LANES):
+            dw_ref[0, 0, at : at + g.shape[0]] = g[:, lane : lane + LANES].astype(bf16)
+            at += g.shape[0]
+        return at
 
     x = x_ref[...]
     c = c_ref[...]
@@ -576,11 +588,11 @@
     hidden = hidden_full.astype(bf16)
     out_ref[...] += matmul(hidden, w_down)
     grad_hidden = right_matmul(c, w_down)
-    dd_ref[0] = matmul(hidden.astype(f32).T.astype(bf16), c).astype(bf16)
+    at = emit(matmul(flip(hidden), c), 0)
     grad_gate = (grad_hidden * up * slope).astype(bf16)
     grad_up = (grad_hidden * act).astype(bf16)
-    dg_ref[0] = matmul(x_t[...], grad_gate).astype(bf16)
-    du_ref[0] = matmul(x_t[...], grad_up).astype(bf16)
+    at = emit(matmul(x_t[...], grad_gate), at)
+    at = emit(matmul(x_t[...], grad_up), at)
     gx_ref[...] += right_matmul(grad_gate, w_gate) + right_matmul(grad_up, w_up)
 
 
@@ -591,17 +603,20 @@
     wide = pl.BlockSpec((1, D, width), lambda f: (f, 0, 0))
     tall = pl.BlockSpec((1, width, D), lambda f: (f, 0, 0))
     total = parts * width
+    lines = 3 * D * width // LANES
     return pl.pallas_call(
         ffn_kernel,
         grid=(parts,),
         in_specs=[whole, whole, wide, wide, tall],
-        out_specs=[whole, whole, wide, wide, tall],
+        out_specs=[
+            whole,
+            whole,
+            pl.BlockSpec((1, 1, lines, LANES), lambda f: (f % 2, f // 2, 0, 0)),
+        ],
         out_shape=[
             jax.ShapeDtypeStruct((tok, D), f32),
             jax.ShapeDtypeStruct((tok, D), f32),
-            jax.ShapeDtypeStruct(gate.shape, bf16),
-            jax.ShapeDtypeStruct(gate.shape, bf16),
-            jax.ShapeDtypeStruct(down.shape, bf16),
+            jax.ShapeDtypeStruct((2, parts // 2, lines, LANES), bf16),
         ],
         scratch_shapes=[pltpu.VMEM((D, tok), bf16)],
         compiler_params=pltpu.CompilerParams(vmem_limit_bytes=VMEM_LIMIT),
@@ -610,6 +625,38 @@
         ),
         name="feed_forward",
     )(x, c, gate, up, down)
+
+
+def split_ffn(flat, width):
+    down = flat[: 6 * width].reshape(6, width, LANES)
+    rest = flat[6 * width :].reshape(2, width // LANES, D, LANES)
+    join = lambda x: jnp.concatenate([x[i] for i in range(x.shape[0])], axis=1)
+    return join(rest[0]), join(rest[1]), join(down)
+
+
+def weights_kernel(rows, *refs):
+    out_ref = refs[-1]
+    for i in range(len(refs) // 2):
+        g = matmul(flip(refs[2 * i][...]), refs[2 * i + 1][...]).astype(bf16)
+        for f in range(D // rows):
+            out_ref[f % 2, f // 2, i * rows : (i + 1) * rows] = g[f * rows : (f + 1) * rows]
+
+
+def weight_grads(pairs, rows):
+    count = len(pairs)
+    owners = D // rows
+    flat = [x for pair in pairs for x in pair]
+    return pl.pallas_call(
+        functools.partial(weights_kernel, rows),
+        out_shape=jax.ShapeDtypeStruct((2, owners // 2, count * rows, D), bf16),
+        compiler_params=pltpu.CompilerParams(vmem_limit_bytes=VMEM_LIMIT),
+        cost_estimate=pl.CostEstimate(
+            flops=sum(2 * D * D * x.shape[0] for x, _ in pairs),
+            transcendentals=0,
+            bytes_accessed=sum(x.size * 2 for x in flat) + 2 * count * D * D,
+        ),
+        name="weight_grads",
+    )(*flat)
 
 
 def shards(
@@ -641,7 +688,11 @@
     group, split = me // parts, me % parts
     line, side = me // 2, me % 2
     tok = inputs.shape[1]
+    enc = encoded.shape[1]
     block = tok // parts
+    half = owners // 2
+    owner_me = lax.axis_index("fsdp")
+    core = owner_me % 2
     length = count * tok
     rows = self_query.shape[0]
 
@@ -682,18 +733,19 @@
 
     normed_all = jnp.zeros((length, D), bf16)
     qkv = jnp.zeros((length, 3 * GP), bf16)
-    piece = inputs[0]
+    encoder = jnp.zeros((count * enc, D), bf16)
+    piece = jnp.concatenate([inputs[0], encoded[0]], axis=0)
     for s in range(lines):
         at = (line - s) % lines
         beside = lax.ppermute(piece, "ctx", swap)
         following = lax.ppermute(piece, "ctx", ring) if s + 1 < lines else None
         for x, owner in ((piece, 2 * at + side), (beside, 2 * at + 1 - side)):
-            normed, projected = project(x)
+            normed, projected = project(x[:tok])
+            encoder = lax.dynamic_update_slice(encoder, x[tok:], (owner * enc, 0))
             normed_all = lax.dynamic_update_slice(normed_all, normed, (owner * tok, 0))
             qkv = lax.dynamic_update_slice(qkv, projected, (owner * tok, 0))
         piece = following
 
-    encoder = lax.all_gather(encoded[0], "ctx", axis=0, tiled=True)
     gather = lambda w: lax.all_gather(w, "fsdp", axis=0, tiled=True)
     w_output = gather(self_output)
     c_query = gather(cross_query)
@@ -706,16 +758,64 @@
 
     out_chunks, self_full, lse = self_forward(qkv, meta, table, parts, count, tok)
 
+    def turned(x):
+        even = me % 2 == 0
+        return jnp.stack(
+            [jnp.where(even, x[:, s], x[:, parts - 1 - s]) for s in range(parts)], axis=1
+        )
+
     def to_owner(chunks):
         got = lax.all_to_all(chunks, "ctx", 0, 0, tiled=True)
         got = got.reshape(GROUPS, parts, block, GL)
-        got = jnp.where(me % 2 == 0, got, got[:, ::-1])
-        return got.transpose(1, 2, 0, 3).reshape(tok, D)
+        return turned(got).transpose(1, 2, 0, 3).reshape(tok, D)
 
     def to_groups(x):
-        got = x.reshape(parts, block, GROUPS, GL).transpose(2, 0, 1, 3)
-        got = jnp.where(me % 2 == 0, got, got[:, ::-1])
+        got = x.reshape(GROUPS, parts, block, GL)
+        got = turned(got)
         return lax.all_to_all(got.reshape(count, block, GL), "ctx", 0, 0, tiled=True)
+
+    core_pairs = [(i, i ^ 1) for i in range(owners)]
+    core_groups = [[b + 2 * i for i in range(half)] for b in range(2)]
+    group_groups = [[g * parts + s for g in range(GROUPS)] for s in range(parts)]
+
+    def add_up(x):
+        return jnp.sum(x.astype(f32), axis=0)
+
+    def pick(g, i, axis=0):
+        return lax.dynamic_index_in_dim(g, i, axis, keepdims=False)
+
+    def swap_cores(g, axis=0):
+        got = lax.ppermute(pick(g, 1 - core, axis), "fsdp", core_pairs)
+        return (pick(g, core, axis).astype(f32) + got.astype(f32)).astype(bf16)
+
+    def over_chips(g):
+        chip = owner_me // 2
+        got = [pick(g, chip)]
+        for k in range(1, half):
+            route = [(i, (i // 2 + k) % half * 2 + i % 2) for i in range(owners)]
+            got.append(lax.ppermute(pick(g, (chip + k) % half), "fsdp", route))
+        return got
+
+    def over_splits(g):
+        got = [g]
+        for k in range(1, parts):
+            route = [(i, i // parts * parts + (i % parts + k) % parts) for i in range(count)]
+            got.append(lax.ppermute(g, "ctx", route))
+        return got
+
+    def total(got):
+        return sum(x.astype(f32) for x in got)
+
+    def over_ctx(g):
+        g = g.astype(bf16).reshape(count, g.shape[0] // count, g.shape[1])
+        return lax.all_to_all(g, "ctx", 0, 0, tiled=True)
+
+    def over_groups(g):
+        g = jnp.broadcast_to(g[None], (GROUPS,) + g.shape)
+        return lax.all_to_all(g, "ctx", 0, 0, tiled=True, axis_index_groups=group_groups)
+
+    def whole(g):
+        return lax.all_gather(g.astype(bf16), "ctx", axis=0, tiled=True).astype(f32)
 
     attended = to_owner(out_chunks)
     states = inputs[0].astype(f32)
@@ -728,16 +828,9 @@
     second_sum = first_sum + matmul(cross_out, c_output)
     normed_three = (second_sum * inverse_rms(second_sum) * gain_ffn).astype(bf16)
     outer = cotangent[0]
-    down_out, grad_three, d_gate, d_up, d_down = ffn(normed_three, outer, w_gate, w_up, w_down)
+    down_out, grad_three, d_ffn = ffn(normed_three, outer, w_gate, w_up, w_down)
     outputs = (second_sum + down_out).astype(bf16)
-
-    def reduce_weight(g):
-        share = lax.psum_scatter(g, "fsdp", scatter_dimension=0, tiled=True)
-        return lax.psum(share, "ctx").astype(f32)
-
-    d_gate = reduce_weight(d_gate)[0]
-    d_up = reduce_weight(d_up)[0]
-    d_down = reduce_weight(d_down)[0]
+    d_ffn = over_chips(swap_cores(d_ffn))
 
     grad_part, grad_gain_ffn = norm_back(second_sum, gain_ffn, grad_three)
     grad_second = outer.astype(f32) + grad_part
@@ -749,19 +842,67 @@
     grad_part, grad_gain_cross = norm_back(first_sum, gain_cross, right_matmul(grad_cq, c_query))
     grad_first = grad_second + grad_part
     branch_one = grad_first.astype(bf16)
-    grad_attended = right_matmul(branch_one, w_output).astype(bf16)
+    grad_attended = jnp.einsum(
+        "td,gcd->gtc", branch_one, w_output.reshape(GROUPS, GL, D), preferred_element_type=f32
+    ).astype(bf16)
     d_o = to_groups(grad_attended)
-    d_o = jnp.pad(d_o, ((0, 0), (0, 0), (0, GP - GL)))
-
-    d_c_output = reduce_weight(left_matmul(cross_out, branch_two).astype(bf16))
-    d_c_query = reduce_weight(left_matmul(normed_two, grad_cq).astype(bf16))
-    d_c_key = reduce_weight(left_matmul(encoder, grad_ck).astype(bf16))
-    d_c_value = reduce_weight(left_matmul(encoder, grad_cv).astype(bf16))
-    d_output = reduce_weight(left_matmul(attended, branch_one).astype(bf16))
     grad_enc = (right_matmul(grad_ck, c_key) + right_matmul(grad_cv, c_value)).astype(bf16)
-    grad_enc = lax.psum_scatter(grad_enc, "ctx", scatter_dimension=0, tiled=True)
-
+    d_rest = swap_cores(
+        weight_grads(
+            [
+                (attended, branch_one),
+                (normed_two, grad_cq),
+                (encoder, grad_ck),
+                (encoder, grad_cv),
+                (cross_out, branch_two),
+            ],
+            rows,
+        )
+    )
+    grad_enc = over_ctx(grad_enc)
+    d_ffn = total(d_ffn).astype(bf16)
+    d_o, d_ffn, d_rest, grad_enc = lax.optimization_barrier((d_o, d_ffn, d_rest, grad_enc))
+
+    d_ffn = over_ctx(d_ffn)
+    d_rest = over_chips(d_rest)
     d_qkv, table_rows = self_backward(qkv, meta, table, d_o, self_full, lse, parts, count, tok)
+    d_qkv, d_ffn, d_rest = lax.optimization_barrier((d_qkv, d_ffn, d_rest))
+
+    grad_enc = add_up(grad_enc).astype(bf16)
+    d_gate, d_up, d_down = split_ffn(whole(add_up(d_ffn)), ffn_gate.shape[1])
+    d_rest = whole(add_up(over_ctx(total(d_rest))))
+    d_rest = [d_rest[i * rows : (i + 1) * rows] for i in range(5)]
+    d_output, d_c_query, d_c_key, d_c_value, d_c_output = d_rest
+
+    d_w = left_matmul(normed_all, d_qkv).astype(bf16).reshape(owners, rows, 3 * GP)
+    wide = lambda x: jnp.pad(x, ((0, 0), (0, 3 * GP - x.shape[1])))
+    table_part = jnp.sum(table_rows, axis=1)[None]
+    gain_part = jnp.stack([grad_gain_cross, grad_gain_ffn]).reshape(2, owners, rows)
+    extra = jnp.stack(
+        [
+            jnp.broadcast_to(wide(table_part), (owners, 3 * GP)),
+            wide(gain_part[0]),
+            wide(gain_part[1]),
+        ],
+        axis=1,
+    )
+    extra = jnp.pad(extra, ((0, 0), (0, 13), (0, 0))).astype(bf16)
+    d_w = jnp.concatenate([d_w, extra], axis=1)
+    d_w = swap_cores(d_w.reshape((half, 2) + d_w.shape[1:]), 1)
+    d_w = total(over_chips(d_w)).astype(bf16)
+    d_w = total(over_splits(d_w)).astype(bf16)
+    d_w = over_groups(d_w).astype(f32)
+    grad_table = d_w[:, rows, : GH * NB].reshape(H, NB).T
+    grad_gain_cross = jnp.sum(d_w[:, rows + 1, :rows], axis=0)
+    grad_gain_ffn = jnp.sum(d_w[:, rows + 2, :rows], axis=0)
+    d_w = [
+        jnp.concatenate([d_w[g, :rows, i * GP : i * GP + GL] for g in range(GROUPS)], axis=1)
+        for i in range(3)
+    ]
+    grad_gain_self = sum(
+        jnp.sum(w.astype(f32) * d, axis=1)
+        for w, d in zip((self_query, self_key, self_value), d_w)
+    ) / self_gain.astype(f32)
 
     def partial_at(at):
         return right_matmul(lax.dynamic_slice(d_qkv, (at * tok, 0), (tok, 3 * GP)), w_qkv)
@@ -776,42 +917,27 @@
         travelling = both
     grad_one = travelling
 
-    d_w = left_matmul(normed_all, d_qkv).reshape(D, 3, GP)[:, :, :GL].reshape(D, 3 * GL)
-    d_w = lax.psum_scatter(d_w.astype(bf16), "fsdp", scatter_dimension=0, tiled=True)
-    d_w = lax.all_gather(d_w, "ctx", axis=0)
-    d_w = jnp.sum(d_w.astype(f32).reshape(GROUPS, parts, rows, 3, GL), axis=1)
-    d_w = d_w.transpose(2, 1, 0, 3).reshape(3, rows, D)
-
-    grad_part, grad_gain_self = norm_back(states, gain_self, grad_one)
+    grad_part, _ = norm_back(states, gain_self, grad_one)
     grad_states = (grad_first + grad_part).astype(bf16)
-
-    grad_table = jnp.sum(table_rows, axis=1).reshape(GH, NB).T
-    grad_table = lax.dynamic_update_slice(jnp.zeros((NB, H), f32), grad_table, (0, group * GH))
-    small = jnp.concatenate(
-        [grad_gain_self, grad_gain_cross, grad_gain_ffn, grad_table.reshape(-1)]
-    )
-    small = lax.psum(small, ("fsdp", "ctx"))
-    owner = lax.axis_index("fsdp")
-    own_gain = lambda k: lax.dynamic_slice(small, (k * D + owner * rows,), (rows,))
     own_table = lax.dynamic_slice(
-        small[3 * D :].reshape(NB, H), (owner * (NB // owners), 0), (NB // owners, H)
+        grad_table, (owner_me * (NB // owners), 0), (NB // owners, H)
     )
     return (
         outputs[None],
         grad_states[None],
         grad_enc[None],
-        own_gain(0),
+        grad_gain_self,
         d_w[0],
         d_w[1],
         d_w[2],
         d_output,
         own_table,
-        own_gain(1),
+        grad_gain_cross,
         d_c_query,
         d_c_key,
         d_c_value,
         d_c_output,
-        own_gain(2),
+        grad_gain_ffn,
         d_gate,
         d_up,
         d_down,

time: 1030 us -> 682 us (0.66)
  waiting for transfers between devices: 497 us -> 193 us
  blocking collectives: 99.2 us -> 14.8 us
  starting transfers between devices: 22.3 us -> 87.8 us
  other arithmetic: 49.4 us -> 72.4 us
  Pallas kernels: 189 us -> 167 us
  matrix products: 85.8 us -> 68.9 us
    reduce_scatter x8 -> x0, waiting for transfers between devices: 261 us -> none  [the longest x6 205 us: reduce_weight(): share = lax.psum_scatter(g, 'fsdp', scatter_dimension=0, tiled=True)]
    unnamed x22 -> x10, waiting for transfers between devices: 57.2 us -> 4.38 us
    psum x1 -> x0, waiting for transfers between devices: 51.8 us -> none  [reduce_weight(): return lax.psum(share, 'ctx').astype(f32)]
    psum x1 -> x0, blocking collectives: 46.5 us -> none  [shards(): small = lax.psum(small, ('fsdp', 'ctx'))]
    all_gather x1 -> x0, blocking collectives: 36.8 us -> none  [shards(): encoder = lax.all_gather(encoded[0], 'ctx', axis=0, tiled=True)]
    all_to_all x0 -> x4, waiting for transfers between devices: none -> 24.5 us  [the longest x3 21.1 us: over_ctx(): return lax.all_to_all(g, 'ctx', 0, 0, tiled=True)]
    convert_element_type x3 -> x12, other arithmetic: 2.56 us -> 24.3 us  [the longest x3 10.7 us: swap_cores(): return (pick(g, core, axis).astype(f32) + got.astype(f32)).astype(bf16)]
    ppermute x0 -> x7, waiting for transfers between devices: none -> 21.2 us  [the longest x3 21.2 us: over_chips(): got.append(lax.ppermute(pick(g, (chip + k) % half), 'fsdp', route))]
  transfers between devices with their start and end apart: 36 -> 37, of which waited for: 21 -> 15; matrix products, arithmetic and copies ran while one was open for 15% -> 25% of each run, Pallas kernels for 8% -> 22%
where the time goes in v2:
time: 682 us; the launch traced here: 672 us
  waiting for transfers between devices  193 us (28%)
  Pallas kernels  167 us (24%)
  starting transfers between devices  87.8 us (13%)
  other arithmetic  72.4 us (11%)
  matrix products  68.9 us (10%)
  local copies, waits for them, and re-layouts  51.5 us (8%)
  between operations  17.6 us (3%)
  blocking collectives  14.8 us (2%)
    pallas_call x1, Pallas kernels, self_backward(): pl.pallas_call(functools.partial(self_backward_kernel, parts, tok), grid_...  60.4 us
    pallas_call x1, Pallas kernels, self_forward(): pl.pallas_call(functools.partial(self_forward_kernel, parts, tok), grid_s...  49 us
    ppermute x3, waiting for transfers between devices, shards(): both = both + lax.ppermute(travelling.astype(bf16), 'ctx', ring).astype(f32)  42.5 us
    ppermute x4, waiting for transfers between devices, shards(): beside = lax.ppermute(piece, 'ctx', swap)  40.7 us
    dot_general x13, matrix products, matmul(): return jnp.dot(a, b, preferred_element_type=f32)  30.5 us
    ppermute x4, waiting for transfers between devices, shards(): lax.ppermute(partial_at(2 * at + 1 - side).astype(bf16), 'ctx', swap)  29.3 us
    dot_general x12, matrix products, right_matmul(): lax.dot_general(a, b, (((1,), (1,)), ((), ())), preferred_element_type=f32)  27.1 us
    ppermute x4, starting transfers between devices, shards(): lax.ppermute(partial_at(2 * at + 1 - side).astype(bf16), 'ctx', swap)  21.5 us
  transfers between devices with their start and end apart: 37, of which 15 were waited for; matrix products, arithmetic and copies ran while one was open for 25% of the time, Pallas kernels for 22%

profile of v2, /device:TPU:0, one launch (start us, length us, event | category | flops | bytes accessed | tf_op | source)
XLA Modules:
  0.0 672.5 jit_solution(1309749179555946815)
XLA Ops:
  13.0 3.0 collective-permute-start
  20.1 14.8 %all-gather = bf16[832,576]{1,0:T(8,128)(2,1)S(1)} all-gather(bf16[208,576]{1,0:T(8,128)(2,1)S(1)} %pad.33), channel_id=2, replica_groups=mesh['ctx'=8,'fsdp'=4] {'fsdp'}, dimensions={0}, use_global_device_ids=true | all-gather | bytes 1198080 | tf_op jit(solution)/shard_map/all_gather | solution.py:717
  44.0 3.0 broadcast.194.clone
  59.3 2.9 fusion.33
  62.2 10.2 %collective-permute-done.2 = bf16[576,768]{1,0:T(8,128)(2,1)S(1)} collective-permute-done((bf16[576,768]{1,0:T(8,128)(2,1)}, bf16[576,768]{1,0:T(8,128)(2,1)S(1)}, u32[]{:S(2)}, u32[]{:S(2)}) %collective-permute-start.2) | collective-permute-done | bytes 884768 | tf_op jit(solution)/shard_map/ppermute | solution.py:740
  80.0 16.2 %collective-permute-done.4 = bf16[576,768]{1,0:T(8,128)(2,1)S(1)} collective-permute-done((bf16[576,768]{1,0:T(8,128)(2,1)S(1)}, bf16[576,768]{1,0:T(8,128)(2,1)S(1)}, u32[]{:S(2)}, u32[]{:S(2)}) %collective-permute-start.4) | collective-permute-done | bytes 884768 | tf_op jit(solution)/shard_map/ppermute | solution.py:740
  103.7 14.4 %collective-permute-done.6 = bf16[576,768]{1,0:T(8,128)(2,1)S(1)} collective-permute-done((bf16[576,768]{1,0:T(8,128)(2,1)S(1)}, bf16[576,768]{1,0:T(8,128)(2,1)S(1)}, u32[]{:S(2)}, u32[]{:S(2)}) %collective-permute-start.6) | collective-permute-done | bytes 884768 | tf_op jit(solution)/shard_map/ppermute | solution.py:740
  120.8 49.0 %self_forward.1 = (bf16[8,256,192]{2,1,0:T(8,128)(2,1)}, f32[192,2048]{1,0:T(8,128)}, f32[8,2048]{1,0:T(8,128)}) custom-call(s32[4]{0:T(128)} %pad_add_fusion.meta, f32[32,3]{1,0:T(8,128)} %constant_dynamic-slice_fusion.1.table, bf16[4096,768]{1,0:T(8,128)(2,1)} %fusion.38.q_ref.k_ref.v_ref, bf16[4096,768]{1,0:T(8,128)(2,1)} %fusion.38.q_ref.k_ref.v_ref, ...), custom_call_target="tpu_custom_call" | custom-call | flops 6442450944 | bytes 8388608 | tf_op jit(solution)/shard_map/self_forward/pallas_call | solution.py:329
  172.1 13.1 %all-to-all-start = ((bf16[8,256,192]{1,2,0:T(8,128)(2,1)}), bf16[8,256,192]{1,2,0:T(8,128)(2,1)S(1)}, u32[]{:S(2)}, u32[]{:S(2)}) async-start(bf16[8,256,192]{1,2,0:T(8,128)(2,1)} %copy.53), calls=%async_computation | async-start | bytes 1572864 | tf_op jit(solution)/shard_map/all_to_all | solution.py:768
  188.0 3.2 convolution_convert_fusion.7.v_ref
  191.2 2.9 convolution_convert_fusion.8.k_ref
  194.1 8.8 %all-to-all-done = bf16[8,256,192]{1,2,0:T(8,128)(2,1)S(1)} async-done(((bf16[8,256,192]{1,2,0:T(8,128)(2,1)}), bf16[8,256,192]{1,2,0:T(8,128)(2,1)S(1)}, u32[]{:S(2)}, u32[]{:S(2)}) %all-to-all-start) | async-done | bytes 786464 | tf_op jit(solution)/shard_map/all_to_all | solution.py:768
  209.5 3.2 convolution_convert_fusion.9.q_ref
  212.7 13.2 %cross_forward.1 = (bf16[512,768]{1,0:T(8,128)(2,1)}, f32[768,512]{1,0:T(8,128)}, f32[48,512]{1,0:T(8,128)}) custom-call(bf16[512,768]{1,0:T(8,128)(2,1)} %convolution_convert_fusion.9.q_ref, bf16[512,768]{1,0:T(8,128)(2,1)} %convolution_convert_fusion.8.k_ref, bf16[512,768]{1,0:T(8,128)(2,1)} %convolution_convert_fusion.7.v_ref), custom_call_target="tpu_custom_call" | custom-call | flops 3221225472 | bytes 4718592 | tf_op jit(solution)/shard_map/cross_forward/pallas_call | solution.py:482
  229.4 20.7 %feed_forward.1 = (f32[512,768]{1,0:T(8,128)}, f32[512,768]{1,0:T(8,128)}, bf16[2,2,9216,128]{3,2,1,0:T(8,128)(2,1)}) custom-call(bf16[512,768]{1,0:T(8,128)(2,1)} %multiply_convert_fusion.x_ref, bf16[512,768]{1,0:T(8,128)(2,1)} %bitcast.166, bf16[4,768,512]{2,1,0:T(8,128)(2,1)} %bitcast.193, bf16[4,768,512]{2,1,0:T(8,128)(2,1)} %bitcast.194, ...), custom_call_target="tpu_custom_call" | custom-call | flops 14495514624 | bytes 18874368 | tf_op jit(solution)/shard_map/feed_forward/pallas_call | solution.py:607
  250.1 4.0 dynamic-slice_bitcast_fusion
  261.5 14.1 %cross_backward.1 = (bf16[512,768]{1,0:T(8,128)(2,1)}, bf16[512,768]{1,0:T(8,128)(2,1)}, bf16[512,768]{1,0:T(8,128)(2,1)}) custom-call(bf16[512,768]{1,0:T(8,128)(2,1)} %convolution_convert_fusion.9.q_ref, bf16[512,768]{1,0:T(8,128)(2,1)} %convolution_convert_fusion.8.k_ref, bf16[512,768]{1,0:T(8,128)(2,1)} %convolution_convert_fusion.7.v_ref, ...), custom_call_target="tpu_custom_call" | custom-call | flops 8053063680 | bytes 7864320 | tf_op jit(solution)/shard_map/cross_backward/pallas_call | solution.py:514
  280.8 9.1 %weight_grads.1 = bf16[2,2,960,768]{3,2,1,0:T(8,128)(2,1)} custom-call(bf16[512,768]{1,0:T(8,128)(2,1)} %copy.57.refs_0_, bf16[512,768]{1,0:T(8,128)(2,1)} %get-tuple-element.113.refs_1_, bf16[512,768]{1,0:T(8,128)(2,1)} %copy-done.28, bf16[512,768]{1,0:T(8,128)(2,1)} %get-tuple-element.46.refs_3_, bf16[512,768]{1,0:T(8,128)(2,1)} %copy-done.6, ...), custom_call_target="tpu_custom_call" | custom-call | flops 3019898880 | bytes 13762560 | tf_op jit(solution)/shard_map/weight_grads/pallas_call | solution.py:649
  289.9 3.7 dynamic-slice_bitcast_fusion.1
  294.1 4.4 fusion
  306.3 3.7 all-to-all-start.2
  316.8 5.0 fusion.1
  321.8 8.4 %all-to-all-done.2 = bf16[8,64,768]{2,1,0:T(8,128)(2,1)S(1)} async-done(((bf16[8,64,768]{2,1,0:T(8,128)(2,1)}), bf16[8,64,768]{2,1,0:T(8,128)(2,1)S(1)}, u32[]{:S(2)}, u32[]{:S(2)}) %all-to-all-start.2) | async-done | bytes 786464 | tf_op jit(solution)/shard_map/all_to_all | solution.py:811
  330.3 4.0 all-to-all-start.1
  334.3 21.2 %collective-permute-done.8 = bf16[9216,128]{1,0:T(8,128)(2,1)} collective-permute-done((bf16[9216,128]{1,0:T(8,128)(2,1)}, bf16[9216,128]{1,0:T(8,128)(2,1)}, u32[]{:S(2)}, u32[]{:S(2)}) %collective-permute-start.8) | collective-permute-done | bytes 2359328 | tf_op jit(solution)/shard_map/ppermute | solution.py:796
  355.5 3.7 fusion.2
  360.1 3.6 all-to-all-start.3
  363.7 3.1 broadcast.194.clone.1
  378.6 3.7 dynamic-slice_bitcast_fusion.3
  386.2 60.4 %self_backward.1 = (bf16[4096,768]{1,0:T(8,128)(2,1)}, f32[96,256]{1,0:T(8,128)}) custom-call(s32[4]{0:T(128)} %pad_add_fusion.meta, f32[32,3]{1,0:T(8,128)} %constant_dynamic-slice_fusion.1.table, bf16[4096,768]{1,0:T(8,128)(2,1)} %fusion.38.q_ref.k_ref.v_ref, bf16[4096,768]{1,0:T(8,128)(2,1)} %fusion.38.q_ref.k_ref.v_ref, ...), custom_call_target="tpu_custom_call" | custom-call | flops 16106127360 | bytes 16777216 | tf_op jit(solution)/shard_map/self_backward/pallas_call | solution.py:367
  447.7 9.2 %convolution_convert_fusion = bf16[768,768]{1,0:T(8,128)(2,1)S(1)} fusion(bf16[4096,768]{1,0:T(8,128)(2,1)} %fusion.67, bf16[4096,768]{1,0:T(8,128)(2,1)} %get-tuple-element.56), kind=kOutput, calls=%fused_computation.82 | convolution fusion | flops 4832428032 | bytes 13762560 | tf_op jit(solution)/shard_map/dot_general | solution.py:40
  462.8 13.0 %collective-permute-start.14 = (bf16[512,768]{1,0:T(8,128)(2,1)}, bf16[512,768]{1,0:T(8,128)(2,1)}, u32[]{:S(2)}, u32[]{:S(2)}) collective-permute-start(bf16[512,768]{1,0:T(8,128)(2,1)} %convolution_convert_fusion.1), channel_id=1, source_target_pairs={{0,4},{4,0},{8,12},{12,8},{16,20},{20,16},{24,28},{28,24},{1,5},{5... | collective-permute-start | bytes 2359304 | tf_op jit(solution)/shard_map/ppermute | solution.py:913
  475.8 3.3 add_convert_fusion
  479.1 4.7 all-to-all-start.5
  489.1 5.5 collective-permute-start.19
  494.7 10.3 %collective-permute-done.14 = bf16[512,768]{1,0:T(8,128)(2,1)} collective-permute-done((bf16[512,768]{1,0:T(8,128)(2,1)}, bf16[512,768]{1,0:T(8,128)(2,1)}, u32[]{:S(2)}, u32[]{:S(2)}) %collective-permute-start.14) | collective-permute-done | bytes 786464 | tf_op jit(solution)/shard_map/ppermute | solution.py:913
  516.1 18.9 %collective-permute-done.13 = bf16[512,768]{1,0:T(8,128)(2,1)S(1)} collective-permute-done((bf16[512,768]{1,0:T(8,128)(2,1)S(1)}, bf16[512,768]{1,0:T(8,128)(2,1)S(1)}, u32[]{:S(2)}, u32[]{:S(2)}) %collective-permute-start.13) | collective-permute-done | bytes 786464 | tf_op jit(solution)/shard_map/ppermute | solution.py:913
  535.0 15.2 %collective-permute-done.15 = bf16[512,768]{1,0:T(8,128)(2,1)S(1)} collective-permute-done((bf16[512,768]{1,0:T(8,128)(2,1)S(1)}, bf16[512,768]{1,0:T(8,128)(2,1)S(1)}, u32[]{:S(2)}, u32[]{:S(2)}) %collective-permute-start.15) | collective-permute-done | bytes 786464 | tf_op jit(solution)/shard_map/ppermute | solution.py:916
  551.4 9.1 %collective-permute-start.16 = (bf16[512,768]{1,0:T(8,128)(2,1)}, bf16[512,768]{1,0:T(8,128)(2,1)}, u32[]{:S(2)}, u32[]{:S(2)}) collective-permute-start(bf16[512,768]{1,0:T(8,128)(2,1)} %add_convert_fusion.2), channel_id=1, source_target_pairs={{0,8},{4,12},{8,16},{12,20},{16,24},{20,28},{24,0},{28,4},{1,9},{5... | collective-permute-start | bytes 2359304 | tf_op jit(solution)/shard_map/ppermute | solution.py:916
  563.4 4.0 collective-permute-start.11
  567.4 3.1 fusion.53
  570.5 12.7 %all-to-all-done.5 = bf16[8,120,768]{2,1,0:T(8,128)(2,1)S(1)} async-done(((bf16[8,120,768]{2,1,0:T(8,128)(2,1)}), bf16[8,120,768]{2,1,0:T(8,128)(2,1)S(1)}, u32[]{:S(2)}, u32[]{:S(2)}) %all-to-all-start.5) | async-done | bytes 1474592 | tf_op jit(solution)/shard_map/all_to_all | solution.py:811
  584.3 4.3 all-to-all-start.4
  588.7 3.0 add_convert_fusion.1
  595.4 27.3 %collective-permute-done.17 = bf16[512,768]{1,0:T(8,128)(2,1)} collective-permute-done((bf16[512,768]{1,0:T(8,128)(2,1)}, bf16[512,768]{1,0:T(8,128)(2,1)}, u32[]{:S(2)}, u32[]{:S(2)}) %collective-permute-start.17) | collective-permute-done | bytes 786464 | tf_op jit(solution)/shard_map/ppermute | solution.py:916
  628.2 3.4 all-to-all-done.4
  645.9 16.6 %all-gather.25.cloned.1.call-done = bf16[960,768]{1,0:T(8,128)(2,1)} async-done(((bf16[120,768]{1,0:T(8,128)(2,1)}), bf16[960,768]{1,0:T(8,128)(2,1)}) %all-gather.25.cloned.1.call-update) | async-done | bytes 1474576 | tf_op jit(solution)/shard_map/all_gather | solution.py:818
  662.5 2.9 fusion.96
  (307 shorter events, 157.6 us)
Async XLA Ops:
  7.2 180.7 %all-gather.21.cloned.1.call-start = ((), (), s32[]{:S(2)}) async-start(), calls=%async_computation.9 | async-start | bytes 1474560 | tf_op jit(solution)/shard_map/all_gather | solution.py:749
  7.9 183.2 %all-gather.19.cloned.1.call-start = ((), (), s32[]{:S(2)}) async-start(), calls=%async_computation.8 | async-start | bytes 1474560 | tf_op jit(solution)/shard_map/all_gather | solution.py:749
  8.7 198.1 %all-gather.15.cloned.1.call-start = ((), (), s32[]{:S(2)}) async-start(), calls=%async_computation.6 | async-start | bytes 1474560 | tf_op jit(solution)/shard_map/all_gather | solution.py:749
  9.4 200.0 %all-gather.17.cloned.1.call-start = ((), (), s32[]{:S(2)}) async-start(), calls=%async_computation.7 | async-start | bytes 1474560 | tf_op jit(solution)/shard_map/all_gather | solution.py:749
  10.0 215.9 %all-gather.23.cloned.1.call-start = ((), (), s32[]{:S(2)}) async-start(), calls=%async_computation.10 | async-start | bytes 1474560 | tf_op jit(solution)/shard_map/all_gather | solution.py:749
  10.6 218.8 %all-gather.29.cloned.1.call-start = ((), (), s32[]{:S(2)}) async-start(), calls=%async_computation.13 | async-start | bytes 3932160 | tf_op jit(solution)/shard_map/all_gather | solution.py:755
  11.2 6.4 copy-start.45
  11.2 6.4 copy-start.48
  11.2 6.4 copy-start.49
  11.2 6.5 copy-start.47
  11.2 218.2 %all-gather.31.cloned.1.call-start = ((), (), s32[]{:S(2)}) async-start(), calls=%async_computation.14 | async-start | bytes 3932160 | tf_op jit(solution)/shard_map/all_gather | solution.py:756
  12.0 217.4 %all-gather.33.cloned.1.call-start = ((), (), s32[]{:S(2)}) async-start(), calls=%async_computation.15 | async-start | bytes 3932160 | tf_op jit(solution)/shard_map/all_gather | solution.py:757
  13.0 35.8 %collective-permute-start = (bf16[576,768]{1,0:T(8,128)(2,1)}, bf16[576,768]{1,0:T(8,128)(2,1)}, u32[]{:S(2)}, u32[]{:S(2)}) collective-permute-start(bf16[576,768]{1,0:T(8,128)(2,1)} %pad_maximum_fusion.2), channel_id=1, source_target_pairs={{0,4},{4,0},{8,12},{12,8},{16,20},{20,16},{24,28},{28,24},{1,5},{5... | collective-permute-start | bytes 2654216 | tf_op jit(solution)/shard_map/ppermute | solution.py:740
  16.0 34.2 %collective-permute-start.1 = (bf16[576,768]{1,0:T(8,128)(2,1)}, bf16[576,768]{1,0:T(8,128)(2,1)}, u32[]{:S(2)}, u32[]{:S(2)}) collective-permute-start(bf16[576,768]{1,0:T(8,128)(2,1)} %pad_maximum_fusion.2), channel_id=1, source_target_pairs={{0,8},{4,12},{8,16},{12,20},{16,24},{20,28},{24,0},{28,4},{1,9},{5... | collective-permute-start | bytes 2654216 | tf_op jit(solution)/shard_map/ppermute | solution.py:741
  50.2 22.2 %collective-permute-start.2 = (bf16[576,768]{1,0:T(8,128)(2,1)}, bf16[576,768]{1,0:T(8,128)(2,1)S(1)}, u32[]{:S(2)}, u32[]{:S(2)}) collective-permute-start(bf16[576,768]{1,0:T(8,128)(2,1)} %collective-permute-done.1), channel_id=1, source_target_pairs={{0,4},{4,0},{8,12},{12,8},{16,20},{20,16},{24,28},{28,24},{1,5},{5... | collective-permute-start | bytes 2654216 | tf_op jit(solution)/shard_map/ppermute | solution.py:740
  51.7 23.6 %collective-permute-start.3 = (bf16[576,768]{1,0:T(8,128)(2,1)}, bf16[576,768]{1,0:T(8,128)(2,1)S(1)}, u32[]{:S(2)}, u32[]{:S(2)}) collective-permute-start(bf16[576,768]{1,0:T(8,128)(2,1)} %collective-permute-done.1), channel_id=1, source_target_pairs={{0,8},{4,12},{8,16},{12,20},{16,24},{20,28},{24,0},{28,4},{1,9},{5... | collective-permute-start | bytes 2654216 | tf_op jit(solution)/shard_map/ppermute | solution.py:741
  72.4 5.8 copy-start.10
  75.3 109.8 %copy-start.12 = (bf16[576,768]{1,0:T(8,128)(2,1)}, bf16[576,768]{1,0:T(8,128)(2,1)S(1)}, u32[]{:S(2)}) copy-start(bf16[576,768]{1,0:T(8,128)(2,1)S(1)} %collective-permute-done.3) | copy-start | bytes 2654212
  75.3 20.8 %collective-permute-start.4 = (bf16[576,768]{1,0:T(8,128)(2,1)S(1)}, bf16[576,768]{1,0:T(8,128)(2,1)S(1)}, u32[]{:S(2)}, u32[]{:S(2)}) collective-permute-start(bf16[576,768]{1,0:T(8,128)(2,1)S(1)} %collective-permute-done.3), channel_id=1, source_target_pairs={{0,4},{4,0},{8,12},{12,8},{16,20},{20,16},{24,28},{28,24},{1,5},{5... | collective-permute-start | bytes 2654216 | tf_op jit(solution)/shard_map/ppermute | solution.py:740
  75.9 22.6 %collective-permute-start.5 = (bf16[576,768]{1,0:T(8,128)(2,1)S(1)}, bf16[576,768]{1,0:T(8,128)(2,1)S(1)}, u32[]{:S(2)}, u32[]{:S(2)}) collective-permute-start(bf16[576,768]{1,0:T(8,128)(2,1)S(1)} %collective-permute-done.3), channel_id=1, source_target_pairs={{0,8},{4,12},{8,16},{12,20},{16,24},{20,28},{24,0},{28,4},{1,9},{5... | collective-permute-start | bytes 2654216 | tf_op jit(solution)/shard_map/ppermute | solution.py:741
  96.1 5.8 copy-start.14
  98.5 19.6 %collective-permute-start.6 = (bf16[576,768]{1,0:T(8,128)(2,1)S(1)}, bf16[576,768]{1,0:T(8,128)(2,1)S(1)}, u32[]{:S(2)}, u32[]{:S(2)}) collective-permute-start(bf16[576,768]{1,0:T(8,128)(2,1)S(1)} %collective-permute-done.5), channel_id=1, source_target_pairs={{0,4},{4,0},{8,12},{12,8},{16,20},{20,16},{24,28},{28,24},{1,5},{5... | collective-permute-start | bytes 2654216 | tf_op jit(solution)/shard_map/ppermute | solution.py:740
  172.1 30.8 %all-to-all-start = ((bf16[8,256,192]{1,2,0:T(8,128)(2,1)}), bf16[8,256,192]{1,2,0:T(8,128)(2,1)S(1)}, u32[]{:S(2)}, u32[]{:S(2)}) async-start(bf16[8,256,192]{1,2,0:T(8,128)(2,1)} %copy.53), calls=%async_computation | async-start | bytes 1572864 | tf_op jit(solution)/shard_map/all_to_all | solution.py:768
  254.2 40.0 %collective-permute-start.7 = (bf16[2,9216,128]{2,1,0:T(8,128)(2,1)}, bf16[2,9216,128]{2,1,0:T(8,128)(2,1)}, u32[]{:S(2)}, u32[]{:S(2)}) collective-permute-start(bf16[2,9216,128]{2,1,0:T(8,128)(2,1)} %dynamic-slice_bitcast_fusion), channel_id=1, source_target_pairs={{0,1},{1,0},{2,3},{3,2},{4,5},{5,4},{6,7},{7,6},{8,9},{9,8},{10,11... | collective-permute-start | bytes 14155784 | tf_op jit(solution)/shard_map/ppermute | solution.py:788
  293.6 23.2 %collective-permute-start.9 = (bf16[2,960,768]{2,1,0:T(8,128)(2,1)}, bf16[2,960,768]{2,1,0:T(8,128)(2,1)}, u32[]{:S(2)}, u32[]{:S(2)}) collective-permute-start(bf16[2,960,768]{2,1,0:T(8,128)(2,1)} %dynamic-slice_bitcast_fusion.1), channel_id=1, source_target_pairs={{0,1},{1,0},{2,3},{3,2},{4,5},{5,4},{6,7},{7,6},{8,9},{9,8},{10,11... | collective-permute-start | bytes 8847368 | tf_op jit(solution)/shard_map/ppermute | solution.py:788
  301.5 53.9 %collective-permute-start.8 = (bf16[9216,128]{1,0:T(8,128)(2,1)}, bf16[9216,128]{1,0:T(8,128)(2,1)}, u32[]{:S(2)}, u32[]{:S(2)}) collective-permute-start(bf16[9216,128]{1,0:T(8,128)(2,1)} %dynamic-slice_bitcast_fusion.2), channel_id=1, source_target_pairs={{0,2},{1,3},{2,0},{3,1},{4,6},{5,7},{6,4},{7,5},{8,10},{9,11},{10,... | collective-permute-start | bytes 7077896 | tf_op jit(solution)/shard_map/ppermute | solution.py:796
  306.3 24.0 %all-to-all-start.2 = ((bf16[8,64,768]{2,1,0:T(8,128)(2,1)}), bf16[8,64,768]{2,1,0:T(8,128)(2,1)S(1)}, u32[]{:S(2)}, u32[]{:S(2)}) async-start(bf16[8,64,768]{2,1,0:T(8,128)(2,1)} %bitcast.27), calls=%async_computation.2 | async-start | bytes 1572864 | tf_op jit(solution)/shard_map/all_to_all | solution.py:811
  330.3 28.9 %copy-start.23 = (bf16[8,64,768]{2,1,0:T(8,128)(2,1)}, bf16[8,64,768]{2,1,0:T(8,128)(2,1)S(1)}, u32[]{:S(2)}) copy-start(bf16[8,64,768]{2,1,0:T(8,128)(2,1)S(1)} %all-to-all-done.2) | copy-start | bytes 2359300
  330.3 28.9 %all-to-all-start.1 = ((bf16[8,256,192]{1,2,0:T(8,128)(2,1)}), bf16[8,256,192]{1,2,0:T(8,128)(2,1)S(1)}, u32[]{:S(2)}, u32[]{:S(2)}) async-start(bf16[8,256,192]{1,2,0:T(8,128)(2,1)} %bitcast.20), calls=%async_computation.1 | async-start | bytes 1572864 | tf_op jit(solution)/shard_map/all_to_all | solution.py:775
  360.1 87.7 %all-to-all-start.3 = ((bf16[8,1152,128]{2,1,0:T(8,128)(2,1)}), bf16[8,1152,128]{2,1,0:T(8,128)(2,1)S(1)}, u32[]{:S(2)}, u32[]{:S(2)}) async-start(bf16[8,1152,128]{2,1,0:T(8,128)(2,1)} %bitcast.28), calls=%async_computation.3 | async-start | bytes 4718592 | tf_op jit(solution)/shard_map/all_to_all | solution.py:811
  363.7 276.9 %all-gather.27.cloned.1.call-start = ((), (), s32[]{:S(2)}) async-start(), calls=%async_computation.12 | async-start | bytes 2654208 | tf_op jit(solution)/shard_map/all_gather | solution.py:818
  382.2 65.5 %collective-permute-start.10 = (bf16[960,768]{1,0:T(8,128)(2,1)}, bf16[960,768]{1,0:T(8,128)(2,1)}, u32[]{:S(2)}, u32[]{:S(2)}) collective-permute-start(bf16[960,768]{1,0:T(8,128)(2,1)} %get-tuple-element.115), channel_id=1, source_target_pairs={{0,2},{1,3},{2,0},{3,1},{4,6},{5,7},{6,4},{7,5},{8,10},{9,11},{10,... | collective-permute-start | bytes 4423688 | tf_op jit(solution)/shard_map/ppermute | solution.py:796
  458.9 29.0 %collective-permute-start.18 = (bf16[2,208,768]{2,1,0:T(8,128)(2,1)}, bf16[2,208,768]{2,1,0:T(8,128)(2,1)}, u32[]{:S(2)}, u32[]{:S(2)}) collective-permute-start(bf16[2,208,768]{2,1,0:T(8,128)(2,1)} %fusion.61), channel_id=1, source_target_pairs={{0,1},{1,0},{2,3},{3,2},{4,5},{5,4},{6,7},{7,6},{8,9},{9,8},{10,11... | collective-permute-start | bytes 1916936 | tf_op jit(solution)/shard_map/ppermute | solution.py:788
  462.8 42.2 %collective-permute-start.14 = (bf16[512,768]{1,0:T(8,128)(2,1)}, bf16[512,768]{1,0:T(8,128)(2,1)}, u32[]{:S(2)}, u32[]{:S(2)}) collective-permute-start(bf16[512,768]{1,0:T(8,128)(2,1)} %convolution_convert_fusion.1), channel_id=1, source_target_pairs={{0,4},{4,0},{8,12},{12,8},{16,20},{20,16},{24,28},{28,24},{1,5},{5... | collective-permute-start | bytes 2359304 | tf_op jit(solution)/shard_map/ppermute | solution.py:913
  479.1 104.1 %all-to-all-start.5 = ((bf16[8,120,768]{2,1,0:T(8,128)(2,1)}), bf16[8,120,768]{2,1,0:T(8,128)(2,1)S(1)}, u32[]{:S(2)}, u32[]{:S(2)}) async-start(bf16[8,120,768]{2,1,0:T(8,128)(2,1)} %bitcast.160), calls=%async_computation.5 | async-start | bytes 2949120 | tf_op jit(solution)/shard_map/all_to_all | solution.py:811
  485.8 49.2 %collective-permute-start.13 = (bf16[512,768]{1,0:T(8,128)(2,1)S(1)}, bf16[512,768]{1,0:T(8,128)(2,1)S(1)}, u32[]{:S(2)}, u32[]{:S(2)}) collective-permute-start(bf16[512,768]{1,0:T(8,128)(2,1)S(1)} %convolution_convert_fusion.2), channel_id=1, source_target_pairs={{0,4},{4,0},{8,12},{12,8},{16,20},{20,16},{24,28},{28,24},{1,5},{5... | collective-permute-start | bytes 2359304 | tf_op jit(solution)/shard_map/ppermute | solution.py:913
  489.1 26.7 %collective-permute-start.19 = (bf16[208,768]{1,0:T(8,128)(2,1)S(1)}, bf16[208,768]{1,0:T(8,128)(2,1)S(1)}, u32[]{:S(2)}, u32[]{:S(2)}) collective-permute-start(bf16[208,768]{1,0:T(8,128)(2,1)S(1)} %dynamic-slice_bitcast_fusion.5), channel_id=1, source_target_pairs={{0,2},{1,3},{2,0},{3,1},{4,6},{5,7},{6,4},{7,5},{8,10},{9,11},{10,... | collective-permute-start | bytes 958472 | tf_op jit(solution)/shard_map/ppermute | solution.py:796
  507.2 43.0 %collective-permute-start.15 = (bf16[512,768]{1,0:T(8,128)(2,1)S(1)}, bf16[512,768]{1,0:T(8,128)(2,1)S(1)}, u32[]{:S(2)}, u32[]{:S(2)}) collective-permute-start(bf16[512,768]{1,0:T(8,128)(2,1)S(1)} %add_convert_fusion.3), channel_id=1, source_target_pairs={{0,8},{4,12},{8,16},{12,20},{16,24},{20,28},{24,0},{28,4},{1,9},{5... | collective-permute-start | bytes 2359304 | tf_op jit(solution)/shard_map/ppermute | solution.py:916
  511.5 77.2 %collective-permute-start.12 = (bf16[512,768]{1,0:T(8,128)(2,1)}, bf16[512,768]{1,0:T(8,128)(2,1)}, u32[]{:S(2)}, u32[]{:S(2)}) collective-permute-start(bf16[512,768]{1,0:T(8,128)(2,1)} %convolution_convert_fusion.3), channel_id=1, source_target_pairs={{0,4},{4,0},{8,12},{12,8},{16,20},{20,16},{24,28},{28,24},{1,5},{5... | collective-permute-start | bytes 2359304 | tf_op jit(solution)/shard_map/ppermute | solution.py:913
  516.0 54.5 %collective-permute-start.20 = (bf16[208,768]{1,0:T(8,128)(2,1)S(1)}, bf16[208,768]{1,0:T(8,128)(2,1)S(1)}, u32[]{:S(2)}, u32[]{:S(2)}) collective-permute-start(bf16[208,768]{1,0:T(8,128)(2,1)S(1)} %fusion.64), channel_id=1, source_target_pairs={{0,4},{4,0},{8,12},{12,8},{16,20},{20,16},{24,28},{28,24},{1,5},{5... | collective-permute-start | bytes 958472 | tf_op jit(solution)/shard_map/ppermute | solution.py:803
  551.4 37.3 %collective-permute-start.16 = (bf16[512,768]{1,0:T(8,128)(2,1)}, bf16[512,768]{1,0:T(8,128)(2,1)}, u32[]{:S(2)}, u32[]{:S(2)}) collective-permute-start(bf16[512,768]{1,0:T(8,128)(2,1)} %add_convert_fusion.2), channel_id=1, source_target_pairs={{0,8},{4,12},{8,16},{12,20},{16,24},{20,28},{24,0},{28,4},{1,9},{5... | collective-permute-start | bytes 2359304 | tf_op jit(solution)/shard_map/ppermute | solution.py:916
  563.4 32.0 %collective-permute-start.11 = (bf16[512,768]{1,0:T(8,128)(2,1)}, bf16[512,768]{1,0:T(8,128)(2,1)}, u32[]{:S(2)}, u32[]{:S(2)}) collective-permute-start(bf16[512,768]{1,0:T(8,128)(2,1)} %convolution_convert_fusion.4), channel_id=1, source_target_pairs={{0,4},{4,0},{8,12},{12,8},{16,20},{20,16},{24,28},{28,24},{1,5},{5... | collective-permute-start | bytes 2359304 | tf_op jit(solution)/shard_map/ppermute | solution.py:913
  584.3 47.2 %all-to-all-start.4 = ((bf16[4,208,768]{2,1,0:T(8,128)(2,1)}), bf16[4,208,768]{2,1,0:T(8,128)(2,1)}, u32[]{:S(2)}, u32[]{:S(2)}) async-start(bf16[4,208,768]{2,1,0:T(8,128)(2,1)} %broadcast_in_dim.17), calls=%async_computation.4 | async-start | bytes 2555904 | tf_op jit(solution)/shard_map/all_to_all | solution.py:815
  588.7 73.9 %all-gather.25.cloned.1.call-start = ((), (), s32[]{:S(2)}) async-start(), calls=%async_computation.11 | async-start | bytes 1658880 | tf_op jit(solution)/shard_map/all_gather | solution.py:818
  591.7 30.9 %collective-permute-start.17 = (bf16[512,768]{1,0:T(8,128)(2,1)}, bf16[512,768]{1,0:T(8,128)(2,1)}, u32[]{:S(2)}, u32[]{:S(2)}) collective-permute-start(bf16[512,768]{1,0:T(8,128)(2,1)} %add_convert_fusion.1), channel_id=1, source_target_pairs={{0,8},{4,12},{8,16},{12,20},{16,24},{20,28},{24,0},{28,4},{1,9},{5... | collective-permute-start | bytes 2359304 | tf_op jit(solution)/shard_map/ppermute | solution.py:916
  594.4 28.2 %copy-start.33 = (bf16[768,3,256]{0,2,1:T(8,128)(2,1)S(1)}, bf16[768,3,256]{0,2,1:T(8,128)(2,1)}, u32[]{:S(2)}) copy-start(bf16[768,3,256]{0,2,1:T(8,128)(2,1)} %pad.34) | copy-start | bytes 3538948
  595.3 30.0 %copy-start.7 = (f32[512,768]{1,0:T(8,128)S(1)}, f32[512,768]{1,0:T(8,128)}, u32[]{:S(2)}) copy-start(f32[512,768]{1,0:T(8,128)} %get-tuple-element.114) | copy-start | bytes 4718596
  645.9 19.6 %copy-start.43 = (f32[512,768]{1,0:T(8,128)}, f32[512,768]{1,0:T(8,128)S(1)}, u32[]{:S(2)}) copy-start(f32[512,768]{1,0:T(8,128)S(1)} %slice_dynamic-update-slice_fusion) | copy-start | bytes 4718596
  (41 other events, 120.2 us)
Sparse Core Ops, SparseCore 0:
  9.6 24.9 all-gather.20
  36.1 17.9 all-gather.18
  55.6 17.4 all-gather.14
  74.6 17.4 all-gather.16
  93.5 17.4 all-gather.22
  112.4 28.5 all-gather.28
  142.5 28.5 all-gather.30
  172.7 28.7 all-gather.32
  462.9 123.2 all-gather.26
  595.5 66.9 all-gather.24

commit v3 on v2

--- a/solution.py
+++ b/solution.py
@@ -55,6 +55,14 @@
     return grad_v, jnp.sum(e * v * r, axis=0)
 
 
+def fold(x, op):
+    while x.shape[0] > 8:
+        half = x.shape[0] // 2
+        x = op(x[:half], x[half:])
+    reduce = jnp.max if op is jnp.maximum else jnp.sum
+    return reduce(x, axis=0, keepdims=True)
+
+
 def flip(x):
     return x.astype(f32).T.astype(bf16)
 
@@ -169,8 +177,10 @@
         k_tile = k_ref[pl.ds(k0, rows), :]
         if kind != "far":
             mask = tile_mask(kind, k0, rows, first, block, starts)
+        all_scores = [matmul(k_tile, q_masked[h]) for h in range(GH)]
+        probs, scales = [], []
         for h in range(GH):
-            s = matmul(k_tile, q_masked[h])
+            s = all_scores[h]
             shift = table[NB - 1, h]
             if kind == "diag":
                 s, shift = s + bias[h, 0], 0.0
@@ -179,15 +189,16 @@
             if kind != "far":
                 s = jnp.where(mask, s, negative)
             old = top[h : h + 1]
-            new = jnp.maximum(old, jnp.max(s, axis=0, keepdims=True) + shift)
+            new = jnp.maximum(old, fold(s, jnp.maximum) + shift)
             scale = jnp.exp(old - new)
             p = jnp.exp(s - (new - shift))
             top[h : h + 1] = new
-            total[h : h + 1] = total[h : h + 1] * scale + jnp.sum(p, axis=0, keepdims=True)
+            total[h : h + 1] = total[h : h + 1] * scale + fold(p, jnp.add)
+            probs.append(p.astype(bf16))
+            scales.append(scale)
+        for h in range(GH):
             rows_h = slice(h * DH, (h + 1) * DH)
-            acc[rows_h] = acc[rows_h] * scale + matmul(
-                v_t[rows_h, pl.ds(k0, rows)], p.astype(bf16)
-            )
+            acc[rows_h] = acc[rows_h] * scales[h] + matmul(v_t[rows_h, pl.ds(k0, rows)], probs[h])
 
     sweep(meta, first, block, step)
     for h in range(GH):
@@ -267,7 +278,7 @@
             elif kind == "prev":
                 near[h, 1] += ds
             else:
-                far_sum[h : h + 1] += jnp.sum(ds, axis=0, keepdims=True)
+                far_sum[h : h + 1] += fold(ds, jnp.add)
             probs.append(p.astype(bf16))
             grads.append(ds.astype(bf16))
             rows_h = slice(h * DH, (h + 1) * DH)
@@ -429,9 +440,9 @@
         for h in range(2):
             rows_h = slice(h * DH, (h + 1) * DH)
             s = matmul(k_ref[...], pair_rows(q_t[:, cols], h))
-            top = jnp.max(s, axis=0, keepdims=True)
+            top = fold(s, jnp.maximum)
             p = jnp.exp(s - top)
-            total = jnp.sum(p, axis=0, keepdims=True)
+            total = fold(p, jnp.add)
             full_ref[rows_h, cols] = matmul(v_t[rows_h], p.astype(bf16)) / total
             lse_ref[h : h + 1, cols] = top + jnp.log(total)
     o_ref[...] = full_ref[...].T.astype(bf16)
@@ -700,11 +711,13 @@
     ring = [(i, (i + 2) % count) for i in range(count)]
 
     def columns(w):
-        return lax.dynamic_slice(w, (0, group * GL), (rows, GL))
+        return jnp.pad(
+            lax.dynamic_slice(w, (0, group * GL), (rows, GL)), ((0, 0), (0, GP - GL))
+        )
 
     def as_row(v):
         v = v.reshape(1, -1)
-        return jnp.pad(v, ((0, 0), (0, 3 * GL - v.shape[1])))
+        return jnp.pad(v, ((0, 0), (0, 3 * GP - v.shape[1])))
 
     packed = jnp.concatenate(
         [columns(self_query), columns(self_key), columns(self_value)], axis=1
@@ -714,9 +727,15 @@
         axis=0,
     )
     packed = jnp.pad(packed, ((0, 14), (0, 0)))
-    packed = lax.all_gather(packed, "fsdp", axis=0)
-    w_qkv = packed[:, :rows].reshape(D, 3, GL)
-    w_qkv = jnp.pad(w_qkv, ((0, 0), (0, 0), (0, GP - GL))).reshape(D, 3 * GP)
+    packed = packed[None]
+    while packed.shape[0] < owners:
+        step = packed.shape[0]
+        theirs = lax.ppermute(packed, "fsdp", [(i, i ^ step) for i in range(owners)])
+        upper = (lax.axis_index("fsdp") // step) % 2 == 1
+        packed = jnp.concatenate(
+            [jnp.where(upper, theirs, packed), jnp.where(upper, packed, theirs)], axis=0
+        )
+    w_qkv = packed[:, :rows].reshape(D, 3 * GP)
     gains = packed[:, rows, : 3 * rows].reshape(owners, 3, rows).transpose(1, 0, 2).reshape(3, D)
     gains = gains.astype(f32)
     gain_self, gain_cross, gain_ffn = gains[0], gains[1], gains[2]
@@ -735,17 +754,27 @@
     qkv = jnp.zeros((length, 3 * GP), bf16)
     encoder = jnp.zeros((count * enc, D), bf16)
     piece = jnp.concatenate([inputs[0], encoded[0]], axis=0)
-    for s in range(lines):
-        at = (line - s) % lines
-        beside = lax.ppermute(piece, "ctx", swap)
-        following = lax.ppermute(piece, "ctx", ring) if s + 1 < lines else None
-        for x, owner in ((piece, 2 * at + side), (beside, 2 * at + 1 - side)):
+    def place(arrived, blocks):
+        normed_all, qkv, encoder = blocks
+        for x, owner in arrived:
             normed, projected = project(x[:tok])
             encoder = lax.dynamic_update_slice(encoder, x[tok:], (owner * enc, 0))
             normed_all = lax.dynamic_update_slice(normed_all, normed, (owner * tok, 0))
             qkv = lax.dynamic_update_slice(qkv, projected, (owner * tok, 0))
-        piece = following
-
+        return normed_all, qkv, encoder
+
+    blocks = (normed_all, qkv, encoder)
+    for s in range(lines):
+        at = (line - s) % lines
+        beside = lax.ppermute(piece, "ctx", swap)
+        mine = piece
+        if s + 1 < lines:
+            piece = lax.ppermute(piece, "ctx", ring)
+            mine, beside, piece = lax.optimization_barrier((mine, beside, piece))
+        blocks = place([(mine, 2 * at + side), (beside, 2 * at + 1 - side)], blocks)
+    normed_all, qkv, encoder = blocks
+
+    qkv, normed_all, encoder = lax.optimization_barrier((qkv, normed_all, encoder))
     gather = lambda w: lax.all_gather(w, "fsdp", axis=0, tiled=True)
     w_output = gather(self_output)
     c_query = gather(cross_query)
@@ -830,15 +859,17 @@
     outer = cotangent[0]
     down_out, grad_three, d_ffn = ffn(normed_three, outer, w_gate, w_up, w_down)
     outputs = (second_sum + down_out).astype(bf16)
-    d_ffn = over_chips(swap_cores(d_ffn))
+    d_ffn = swap_cores(d_ffn)
 
     grad_part, grad_gain_ffn = norm_back(second_sum, gain_ffn, grad_three)
     grad_second = outer.astype(f32) + grad_part
     branch_two = grad_second.astype(bf16)
     grad_cross_out = right_matmul(branch_two, c_output).astype(bf16)
+    grad_cross_out, d_ffn = lax.optimization_barrier((grad_cross_out, d_ffn))
     grad_cq, grad_ck, grad_cv = cross_backward(
         cross_queries, cross_keys, cross_values, grad_cross_out, cross_full, cross_lse
     )
+    d_ffn = over_chips(d_ffn)
     grad_part, grad_gain_cross = norm_back(first_sum, gain_cross, right_matmul(grad_cq, c_query))
     grad_first = grad_second + grad_part
     branch_one = grad_first.astype(bf16)
@@ -859,16 +890,33 @@
             rows,
         )
     )
-    grad_enc = over_ctx(grad_enc)
+    grad_enc = lax.psum_scatter(grad_enc, "ctx", scatter_dimension=0, tiled=True)
     d_ffn = total(d_ffn).astype(bf16)
-    d_o, d_ffn, d_rest, grad_enc = lax.optimization_barrier((d_o, d_ffn, d_rest, grad_enc))
+    d_o, d_ffn, d_rest = lax.optimization_barrier((d_o, d_ffn, d_rest))
 
     d_ffn = over_ctx(d_ffn)
     d_rest = over_chips(d_rest)
     d_qkv, table_rows = self_backward(qkv, meta, table, d_o, self_full, lse, parts, count, tok)
-    d_qkv, d_ffn, d_rest = lax.optimization_barrier((d_qkv, d_ffn, d_rest))
-
-    grad_enc = add_up(grad_enc).astype(bf16)
+    d_qkv, d_ffn, d_rest, grad_enc = lax.optimization_barrier((d_qkv, d_ffn, d_rest, grad_enc))
+
+    def partial_at(at):
+        return right_matmul(lax.dynamic_slice(d_qkv, (at * tok, 0), (tok, 3 * GP)), w_qkv)
+
+    travelling = None
+    for s in range(1, lines + 1):
+        at = (line - s) % lines
+        leaving = partial_at(2 * at + 1 - side).astype(bf16)
+        if s == 1:
+            leaving, d_qkv, d_ffn, d_rest = lax.optimization_barrier(
+                (leaving, d_qkv, d_ffn, d_rest)
+            )
+        theirs = lax.ppermute(leaving, "ctx", swap)
+        both = partial_at(2 * at + side) + theirs.astype(f32)
+        if travelling is not None:
+            both = both + lax.ppermute(travelling.astype(bf16), "ctx", ring).astype(f32)
+        travelling = both
+    grad_one = travelling
+
     d_gate, d_up, d_down = split_ffn(whole(add_up(d_ffn)), ffn_gate.shape[1])
     d_rest = whole(add_up(over_ctx(total(d_rest))))
     d_rest = [d_rest[i * rows : (i + 1) * rows] for i in range(5)]
@@ -903,19 +951,6 @@
         jnp.sum(w.astype(f32) * d, axis=1)
         for w, d in zip((self_query, self_key, self_value), d_w)
     ) / self_gain.astype(f32)
-
-    def partial_at(at):
-        return right_matmul(lax.dynamic_slice(d_qkv, (at * tok, 0), (tok, 3 * GP)), w_qkv)
-
-    travelling = None
-    for s in range(1, lines + 1):
-        at = (line - s) % lines
-        theirs = lax.ppermute(partial_at(2 * at + 1 - side).astype(bf16), "ctx", swap)
-        both = partial_at(2 * at + side) + theirs.astype(f32)
-        if travelling is not None:
-            both = both + lax.ppermute(travelling.astype(bf16), "ctx", ring).astype(f32)
-        travelling = both
-    grad_one = travelling
 
     grad_part, _ = norm_back(states, gain_self, grad_one)
     grad_states = (grad_first + grad_part).astype(bf16)

time: 682 us -> 613 us (0.90)
  starting transfers between devices: 87.8 us -> 57.1 us
  blocking collectives: 14.8 us -> 0 us
  local copies, waits for them, and re-layouts: 51.5 us -> 41.1 us
  Pallas kernels: 167 us -> 177 us
  other arithmetic: 72.4 us -> 63.1 us
  waiting for transfers between devices: 193 us -> 186 us
    ppermute x7 -> x9, waiting for transfers between devices: 34.1 us -> 54.9 us  [the longest x4 43.7 us: shards(): theirs = lax.ppermute(leaving, 'ctx', swap)]
    pallas_call x1, Pallas kernels: 60.4 us -> 77 us  [self_backward(): pl.pallas_call(functools.partial(self_backward_kernel, parts, tok), grid_...]
    all_gather x1 -> x0, blocking collectives: 14.8 us -> none  [shards(): packed = lax.all_gather(packed, 'fsdp', axis=0)]
    ppermute x7 -> x9, starting transfers between devices: 24.9 us -> 10.9 us  [the longest x4 7.62 us: shards(): theirs = lax.ppermute(leaving, 'ctx', swap)]
    all_gather x2, waiting for transfers between devices: 16.6 us -> 4.92 us  [whole(): return lax.all_gather(g.astype(bf16), 'ctx', axis=0, tiled=True).astype(f32)]
    all_to_all x3 -> x2, waiting for transfers between devices: 21.1 us -> 9.54 us  [over_ctx(): return lax.all_to_all(g, 'ctx', 0, 0, tiled=True)]
    ppermute x3, waiting for transfers between devices: 21.2 us -> 10.3 us  [over_chips(): got.append(lax.ppermute(pick(g, (chip + k) % half), 'fsdp', route))]
    ppermute x4, waiting for transfers between devices: 40.7 us -> 30.9 us  [shards(): beside = lax.ppermute(piece, 'ctx', swap)]
  transfers between devices with their start and end apart: 37 -> 39, of which waited for: 15 -> 21; matrix products, arithmetic and copies ran while one was open for 25% -> 23% of each run, Pallas kernels for 22% -> 26%
where the time goes in v3:
time: 613 us; the launch traced here: 607 us
  waiting for transfers between devices  186 us (30%)
  Pallas kernels  177 us (29%)
  matrix products  66.1 us (11%)
  other arithmetic  63.1 us (10%)
  starting transfers between devices  57.1 us (9%)
  local copies, waits for them, and re-layouts  41.1 us (7%)
  between operations  17.2 us (3%)
    pallas_call x1, Pallas kernels, self_backward(): pl.pallas_call(functools.partial(self_backward_kernel, parts, tok), grid_...  77 us
    ppermute x3, waiting for transfers between devices, shards(): both = both + lax.ppermute(travelling.astype(bf16), 'ctx', ring).astype(f32)  49.9 us
    ppermute x4, waiting for transfers between devices, shards(): theirs = lax.ppermute(leaving, 'ctx', swap)  43.7 us
    pallas_call x1, Pallas kernels, self_forward(): pl.pallas_call(functools.partial(self_forward_kernel, parts, tok), grid_s...  42.8 us
    ppermute x4, waiting for transfers between devices, shards(): beside = lax.ppermute(piece, 'ctx', swap)  30.9 us
    dot_general x13, matrix products, matmul(): return jnp.dot(a, b, preferred_element_type=f32)  30.3 us
    dot_general x12, matrix products, right_matmul(): lax.dot_general(a, b, (((1,), (1,)), ((), ())), preferred_element_type=f32)  25.8 us
    pallas_call x1, Pallas kernels, ffn(): pl.pallas_call(ffn_kernel, grid=(parts,), in_specs=[whole, whole, wide, w...  20.6 us
  transfers between devices with their start and end apart: 39, of which 21 were waited for; matrix products, arithmetic and copies ran while one was open for 23% of the time, Pallas kernels for 26%

profile of v3, /device:TPU:0, one launch (start us, length us, event | category | flops | bytes accessed | tf_op | source)
XLA Modules:
  0.0 607.4 jit_solution(5151546643574066721)
XLA Ops:
  12.1 3.0 collective-permute-start.2
  25.7 9.1 %collective-permute-done.2 = bf16[576,768]{1,0:T(8,128)(2,1)S(1)} collective-permute-done((bf16[576,768]{1,0:T(8,128)(2,1)S(1)}, bf16[576,768]{1,0:T(8,128)(2,1)S(1)}, u32[]{:S(2)}, u32[]{:S(2)}) %collective-permute-start.2) | collective-permute-done | bytes 884768 | tf_op jit(solution)/shard_map/ppermute | solution.py:769
  34.8 3.3 collective-permute-done.3
  39.1 2.9 collective-permute-done.1
  45.2 3.1 broadcast.207.clone
  51.8 6.7 %collective-permute-done.4 = bf16[576,768]{1,0:T(8,128)(2,1)} collective-permute-done((bf16[576,768]{1,0:T(8,128)(2,1)S(1)}, bf16[576,768]{1,0:T(8,128)(2,1)}, u32[]{:S(2)}, u32[]{:S(2)}) %collective-permute-start.4) | collective-permute-done | bytes 884768 | tf_op jit(solution)/shard_map/ppermute | solution.py:769
  68.1 2.9 fusion.35
  71.0 9.3 %collective-permute-done.6 = bf16[576,768]{1,0:T(8,128)(2,1)S(1)} collective-permute-done((bf16[576,768]{1,0:T(8,128)(2,1)}, bf16[576,768]{1,0:T(8,128)(2,1)S(1)}, u32[]{:S(2)}, u32[]{:S(2)}) %collective-permute-start.6) | collective-permute-done | bytes 884768 | tf_op jit(solution)/shard_map/ppermute | solution.py:769
  88.6 2.9 fusion.36
  95.0 5.8 collective-permute-done.8
  105.7 42.8 %self_forward.1 = (bf16[8,256,192]{2,1,0:T(8,128)(2,1)}, f32[192,2048]{1,0:T(8,128)}, f32[8,2048]{1,0:T(8,128)}) custom-call(s32[4]{0:T(128)} %pad_add_fusion.meta, f32[32,3]{1,0:T(8,128)} %constant_dynamic-slice_fusion.1.table, bf16[4096,768]{1,0:T(8,128)(2,1)} %fusion.39.q_ref.k_ref.v_ref, bf16[4096,768]{1,0:T(8,128)(2,1)} %fusion.39.q_ref.k_ref.v_ref, ...), custom_call_target="tpu_custom_call" | custom-call | flops 6442450944 | bytes 8388608 | tf_op jit(solution)/shard_map/self_forward/pallas_call | solution.py:340
  151.0 4.0 all-to-all-start
  155.1 3.0 convolution_convert_fusion.7.v_ref
  158.1 2.9 convolution_convert_fusion.8.k_ref
  161.0 7.1 %all-to-all-done = bf16[8,256,192]{1,2,0:T(8,128)(2,1)S(1)} async-done(((bf16[8,256,192]{1,2,0:T(8,128)(2,1)}), bf16[8,256,192]{1,2,0:T(8,128)(2,1)S(1)}, u32[]{:S(2)}, u32[]{:S(2)}) %all-to-all-start) | async-done | bytes 786464 | tf_op jit(solution)/shard_map/all_to_all | solution.py:797
  174.6 3.2 convolution_convert_fusion.9.q_ref
  177.8 13.3 %cross_forward.1 = (bf16[512,768]{1,0:T(8,128)(2,1)}, f32[768,512]{1,0:T(8,128)}, f32[48,512]{1,0:T(8,128)}) custom-call(bf16[512,768]{1,0:T(8,128)(2,1)} %convolution_convert_fusion.9.q_ref, bf16[512,768]{1,0:T(8,128)(2,1)} %convolution_convert_fusion.8.k_ref, bf16[512,768]{1,0:T(8,128)(2,1)} %convolution_convert_fusion.7.v_ref), custom_call_target="tpu_custom_call" | custom-call | flops 3221225472 | bytes 4718592 | tf_op jit(solution)/shard_map/cross_forward/pallas_call | solution.py:493
  194.6 4.9 all-gather.32.cloned.1.call-done
  199.5 20.6 %feed_forward.1 = (f32[512,768]{1,0:T(8,128)}, f32[512,768]{1,0:T(8,128)}, bf16[2,2,9216,128]{3,2,1,0:T(8,128)(2,1)}) custom-call(bf16[512,768]{1,0:T(8,128)(2,1)} %multiply_convert_fusion.x_ref, bf16[512,768]{1,0:T(8,128)(2,1)} %bitcast.155, bf16[4,768,512]{2,1,0:T(8,128)(2,1)} %bitcast.182, bf16[4,768,512]{2,1,0:T(8,128)(2,1)} %bitcast.183, ...), custom_call_target="tpu_custom_call" | custom-call | flops 14495514624 | bytes 18874368 | tf_op jit(solution)/shard_map/feed_forward/pallas_call | solution.py:618
  220.1 4.0 dynamic-slice_bitcast_fusion
  231.0 3.3 convolution_convert_fusion.6.do_ref
  234.3 3.0 fusion
  240.5 13.9 %cross_backward.1 = (bf16[512,768]{1,0:T(8,128)(2,1)}, bf16[512,768]{1,0:T(8,128)(2,1)}, bf16[512,768]{1,0:T(8,128)(2,1)}) custom-call(bf16[512,768]{1,0:T(8,128)(2,1)} %convolution_convert_fusion.9.q_ref, bf16[512,768]{1,0:T(8,128)(2,1)} %convolution_convert_fusion.8.k_ref, bf16[512,768]{1,0:T(8,128)(2,1)} %convolution_convert_fusion.7.v_ref, ...), custom_call_target="tpu_custom_call" | custom-call | flops 8053063680 | bytes 7864320 | tf_op jit(solution)/shard_map/cross_backward/pallas_call | solution.py:525
  259.6 9.0 %weight_grads.1 = bf16[2,2,960,768]{3,2,1,0:T(8,128)(2,1)} custom-call(bf16[512,768]{1,0:T(8,128)(2,1)} %copy.50.refs_0_, bf16[512,768]{1,0:T(8,128)(2,1)} %get-tuple-element.153.refs_1_, bf16[512,768]{1,0:T(8,128)(2,1)} %copy-done.16, bf16[512,768]{1,0:T(8,128)(2,1)} %get-tuple-element.78.refs_3_, bf16[512,768]{1,0:T(8,128)(2,1)} %copy-done.5, ...), custom_call_target="tpu_custom_call" | custom-call | flops 3019898880 | bytes 13762560 | tf_op jit(solution)/shard_map/weight_grads/pallas_call | solution.py:660
  268.6 3.7 dynamic-slice_bitcast_fusion.1
  277.8 5.7 all-to-all-start.1
  283.6 10.3 %collective-permute-done.10 = bf16[9216,128]{1,0:T(8,128)(2,1)} collective-permute-done((bf16[9216,128]{1,0:T(8,128)(2,1)}, bf16[9216,128]{1,0:T(8,128)(2,1)}, u32[]{:S(2)}, u32[]{:S(2)}) %collective-permute-start.10) | collective-permute-done | bytes 2359328 | tf_op jit(solution)/shard_map/ppermute | solution.py:825
  293.9 3.7 fusion.2
  297.6 3.4 fusion.1
  301.0 3.5 all-to-all-done.1
  304.5 4.4 all-to-all-start.2
  319.3 77.0 %self_backward.1 = (bf16[4096,768]{1,0:T(8,128)(2,1)}, f32[96,256]{1,0:T(8,128)}) custom-call(s32[4]{0:T(128)} %pad_add_fusion.meta, f32[32,3]{1,0:T(8,128)} %constant_dynamic-slice_fusion.1.table, bf16[4096,768]{1,0:T(8,128)(2,1)} %fusion.39.q_ref.k_ref.v_ref, bf16[4096,768]{1,0:T(8,128)(2,1)} %fusion.39.q_ref.k_ref.v_ref, ...), custom_call_target="tpu_custom_call" | custom-call | flops 16106127360 | bytes 16777216 | tf_op jit(solution)/shard_map/self_backward/pallas_call | solution.py:378
  397.5 3.5 reduce-scatter.2.cloned.1.call-done
  401.0 3.4 convolution_convert_fusion.4
  404.3 9.2 %convolution_convert_fusion = bf16[768,768]{1,0:T(8,128)(2,1)S(1)} fusion(bf16[4096,768]{1,0:T(8,128)(2,1)} %copy-done.6, bf16[4096,768]{1,0:T(8,128)(2,1)} %get-tuple-element.92), kind=kOutput, calls=%fused_computation.83 | convolution fusion | flops 4832428032 | bytes 13762560 | tf_op jit(solution)/shard_map/dot_general | solution.py:40
  414.4 2.9 reduce_sum.253
  418.7 2.8 add_convert_fusion
  421.5 3.8 all-to-all-start.4
  431.4 16.5 %collective-permute-done.16 = bf16[512,768]{1,0:T(8,128)(2,1)} collective-permute-done((bf16[512,768]{1,0:T(8,128)(2,1)}, bf16[512,768]{1,0:T(8,128)(2,1)}, u32[]{:S(2)}, u32[]{:S(2)}) %collective-permute-start.16) | collective-permute-done | bytes 786464 | tf_op jit(solution)/shard_map/ppermute | solution.py:913
  456.8 27.2 %collective-permute-done.15 = bf16[512,768]{1,0:T(8,128)(2,1)S(1)} collective-permute-done((bf16[512,768]{1,0:T(8,128)(2,1)S(1)}, bf16[512,768]{1,0:T(8,128)(2,1)S(1)}, u32[]{:S(2)}, u32[]{:S(2)}) %collective-permute-start.15) | collective-permute-done | bytes 786464 | tf_op jit(solution)/shard_map/ppermute | solution.py:913
  484.0 8.0 %collective-permute-done.17 = bf16[512,768]{1,0:T(8,128)(2,1)S(1)} collective-permute-done((bf16[512,768]{1,0:T(8,128)(2,1)S(1)}, bf16[512,768]{1,0:T(8,128)(2,1)S(1)}, u32[]{:S(2)}, u32[]{:S(2)}) %collective-permute-start.17) | collective-permute-done | bytes 786464 | tf_op jit(solution)/shard_map/ppermute | solution.py:916
  493.3 10.7 %collective-permute-start.18 = (bf16[512,768]{1,0:T(8,128)(2,1)}, bf16[512,768]{1,0:T(8,128)(2,1)}, u32[]{:S(2)}, u32[]{:S(2)}) collective-permute-start(bf16[512,768]{1,0:T(8,128)(2,1)} %add_convert_fusion.2), channel_id=1, source_target_pairs={{0,8},{4,12},{8,16},{12,20},{16,24},{20,28},{24,0},{28,4},{1,9},{5... | collective-permute-start | bytes 2359304 | tf_op jit(solution)/shard_map/ppermute | solution.py:916
  510.2 9.5 %all-to-all-done.4 = bf16[8,120,768]{2,1,0:T(8,128)(2,1)S(1)} async-done(((bf16[8,120,768]{2,1,0:T(8,128)(2,1)}), bf16[8,120,768]{2,1,0:T(8,128)(2,1)S(1)}, u32[]{:S(2)}, u32[]{:S(2)}) %all-to-all-start.4) | async-done | bytes 1474592 | tf_op jit(solution)/shard_map/all_to_all | solution.py:840
  520.9 4.3 all-to-all-start.3
  530.6 41.9 %collective-permute-done.19 = bf16[512,768]{1,0:T(8,128)(2,1)S(1)} collective-permute-done((bf16[512,768]{1,0:T(8,128)(2,1)}, bf16[512,768]{1,0:T(8,128)(2,1)S(1)}, u32[]{:S(2)}, u32[]{:S(2)}) %collective-permute-start.19) | collective-permute-done | bytes 786464 | tf_op jit(solution)/shard_map/ppermute | solution.py:916
  572.5 2.8 fusion.27
  592.8 4.9 all-gather.24.cloned.1.call-done
  597.7 2.9 fusion.111
  (279 shorter events, 140.1 us)
Async XLA Ops:
  7.2 147.9 %all-gather.20.cloned.1.call-start = ((), (), s32[]{:S(2)}) async-start(), calls=%async_computation.9 | async-start | bytes 1474560 | tf_op jit(solution)/shard_map/all_gather | solution.py:778
  7.9 150.1 %all-gather.18.cloned.1.call-start = ((), (), s32[]{:S(2)}) async-start(), calls=%async_computation.8 | async-start | bytes 1474560 | tf_op jit(solution)/shard_map/all_gather | solution.py:778
  8.7 163.2 %all-gather.14.cloned.1.call-start = ((), (), s32[]{:S(2)}) async-start(), calls=%async_computation.6 | async-start | bytes 1474560 | tf_op jit(solution)/shard_map/all_gather | solution.py:778
  9.4 165.2 %all-gather.16.cloned.1.call-start = ((), (), s32[]{:S(2)}) async-start(), calls=%async_computation.7 | async-start | bytes 1474560 | tf_op jit(solution)/shard_map/all_gather | solution.py:778
  10.0 181.1 %all-gather.22.cloned.1.call-start = ((), (), s32[]{:S(2)}) async-start(), calls=%async_computation.10 | async-start | bytes 1474560 | tf_op jit(solution)/shard_map/all_gather | solution.py:778
  10.6 184.0 %all-gather.28.cloned.1.call-start = ((), (), s32[]{:S(2)}) async-start(), calls=%async_computation.14 | async-start | bytes 3932160 | tf_op jit(solution)/shard_map/all_gather | solution.py:784
  11.2 183.4 %all-gather.30.cloned.1.call-start = ((), (), s32[]{:S(2)}) async-start(), calls=%async_computation.15 | async-start | bytes 3932160 | tf_op jit(solution)/shard_map/all_gather | solution.py:785
  12.0 187.6 %all-gather.32.cloned.1.call-start = ((), (), s32[]{:S(2)}) async-start(), calls=%async_computation.16 | async-start | bytes 3932160 | tf_op jit(solution)/shard_map/all_gather | solution.py:786
  12.1 8.0 %copy-start.30 = (s32[1,4]{1,0:T(1,128)S(1)}, s32[1,4]{1,0:T(1,128)}, u32[]{:S(2)}) copy-start(s32[1,4]{1,0:T(1,128)} %param.21) | copy-start | bytes 52
  12.1 22.7 %collective-permute-start.2 = (bf16[576,768]{1,0:T(8,128)(2,1)S(1)}, bf16[576,768]{1,0:T(8,128)(2,1)S(1)}, u32[]{:S(2)}, u32[]{:S(2)}) collective-permute-start(bf16[576,768]{1,0:T(8,128)(2,1)S(1)} %pad_maximum_fusion.3), channel_id=1, source_target_pairs={{0,4},{4,0},{8,12},{12,8},{16,20},{20,16},{24,28},{28,24},{1,5},{5... | collective-permute-start | bytes 2654216 | tf_op jit(solution)/shard_map/ppermute | solution.py:769
  15.1 23.0 %collective-permute-start.3 = (bf16[576,768]{1,0:T(8,128)(2,1)S(1)}, bf16[576,768]{1,0:T(8,128)(2,1)S(1)}, u32[]{:S(2)}, u32[]{:S(2)}) collective-permute-start(bf16[576,768]{1,0:T(8,128)(2,1)S(1)} %pad_maximum_fusion.3), channel_id=1, source_target_pairs={{0,8},{4,12},{8,16},{12,20},{16,24},{20,28},{24,0},{28,4},{1,9},{5... | collective-permute-start | bytes 2654216 | tf_op jit(solution)/shard_map/ppermute | solution.py:772
  19.9 4.0 collective-permute-start
  24.1 17.9 %collective-permute-start.1 = (bf16[2,208,768]{2,1,0:T(8,128)(2,1)S(1)}, bf16[2,208,768]{2,1,0:T(8,128)(2,1)S(1)}, u32[]{:S(2)}, u32[]{:S(2)}) collective-permute-start(bf16[2,208,768]{2,1,0:T(8,128)(2,1)S(1)} %pad_maximum_fusion.6), channel_id=1, source_target_pairs={{0,2},{1,3},{2,0},{3,1},{4,6},{5,7},{6,4},{7,5},{8,10},{9,11},{10,... | collective-permute-start | bytes 1916936 | tf_op jit(solution)/shard_map/ppermute | solution.py:733
  38.1 20.4 %collective-permute-start.4 = (bf16[576,768]{1,0:T(8,128)(2,1)S(1)}, bf16[576,768]{1,0:T(8,128)(2,1)}, u32[]{:S(2)}, u32[]{:S(2)}) collective-permute-start(bf16[576,768]{1,0:T(8,128)(2,1)S(1)} %collective-permute-done.3), channel_id=1, source_target_pairs={{0,4},{4,0},{8,12},{12,8},{16,20},{20,16},{24,28},{28,24},{1,5},{5... | collective-permute-start | bytes 2654216 | tf_op jit(solution)/shard_map/ppermute | solution.py:769
  38.6 22.1 %collective-permute-start.5 = (bf16[576,768]{1,0:T(8,128)(2,1)S(1)}, bf16[576,768]{1,0:T(8,128)(2,1)}, u32[]{:S(2)}, u32[]{:S(2)}) collective-permute-start(bf16[576,768]{1,0:T(8,128)(2,1)S(1)} %collective-permute-done.3), channel_id=1, source_target_pairs={{0,8},{4,12},{8,16},{12,20},{16,24},{20,28},{24,0},{28,4},{1,9},{5... | collective-permute-start | bytes 2654216 | tf_op jit(solution)/shard_map/ppermute | solution.py:772
  60.8 19.5 %collective-permute-start.6 = (bf16[576,768]{1,0:T(8,128)(2,1)}, bf16[576,768]{1,0:T(8,128)(2,1)S(1)}, u32[]{:S(2)}, u32[]{:S(2)}) collective-permute-start(bf16[576,768]{1,0:T(8,128)(2,1)} %collective-permute-done.5), channel_id=1, source_target_pairs={{0,4},{4,0},{8,12},{12,8},{16,20},{20,16},{24,28},{28,24},{1,5},{5... | collective-permute-start | bytes 2654216 | tf_op jit(solution)/shard_map/ppermute | solution.py:769
  62.0 20.9 %collective-permute-start.7 = (bf16[576,768]{1,0:T(8,128)(2,1)}, bf16[576,768]{1,0:T(8,128)(2,1)S(1)}, u32[]{:S(2)}, u32[]{:S(2)}) collective-permute-start(bf16[576,768]{1,0:T(8,128)(2,1)} %collective-permute-done.5), channel_id=1, source_target_pairs={{0,8},{4,12},{8,16},{12,20},{16,24},{20,28},{24,0},{28,4},{1,9},{5... | collective-permute-start | bytes 2654216 | tf_op jit(solution)/shard_map/ppermute | solution.py:772
  83.0 17.9 %collective-permute-start.8 = (bf16[576,768]{1,0:T(8,128)(2,1)S(1)}, bf16[576,768]{1,0:T(8,128)(2,1)S(1)}, u32[]{:S(2)}, u32[]{:S(2)}) collective-permute-start(bf16[576,768]{1,0:T(8,128)(2,1)S(1)} %collective-permute-done.7), channel_id=1, source_target_pairs={{0,4},{4,0},{8,12},{12,8},{16,20},{20,16},{24,28},{28,24},{1,5},{5... | collective-permute-start | bytes 2654216 | tf_op jit(solution)/shard_map/ppermute | solution.py:769
  105.7 52.3 %copy-start.5 = (bf16[512,768]{1,0:T(8,128)(2,1)}, bf16[512,768]{1,0:T(8,128)(2,1)S(1)}, u32[]{:S(2)}) copy-start(bf16[512,768]{1,0:T(8,128)(2,1)S(1)} %slice_dynamic-update-slice_fusion.6.refs_4_.refs_6_) | copy-start | bytes 2359300
  151.0 17.1 %all-to-all-start = ((bf16[8,256,192]{1,2,0:T(8,128)(2,1)}), bf16[8,256,192]{1,2,0:T(8,128)(2,1)S(1)}, u32[]{:S(2)}, u32[]{:S(2)}) async-start(bf16[8,256,192]{1,2,0:T(8,128)(2,1)} %copy.46), calls=%async_computation | async-start | bytes 1572864 | tf_op jit(solution)/shard_map/all_to_all | solution.py:797
  224.1 10.1 %collective-permute-start.9 = (bf16[2,9216,128]{2,1,0:T(8,128)(2,1)}, bf16[2,9216,128]{2,1,0:T(8,128)(2,1)}, u32[]{:S(2)}, u32[]{:S(2)}) collective-permute-start(bf16[2,9216,128]{2,1,0:T(8,128)(2,1)} %dynamic-slice_bitcast_fusion), channel_id=1, source_target_pairs={{0,1},{1,0},{2,3},{3,2},{4,5},{5,4},{6,7},{7,6},{8,9},{9,8},{10,11... | collective-permute-start | bytes 14155784 | tf_op jit(solution)/shard_map/ppermute | solution.py:817
  226.7 7.6 %copy-start.4 = (bf16[2,2,9216,128]{3,2,1,0:T(8,128)(2,1)S(1)}, bf16[2,2,9216,128]{3,2,1,0:T(8,128)(2,1)}, u32[]{:S(2)}) copy-start(bf16[2,2,9216,128]{3,2,1,0:T(8,128)(2,1)} %get-tuple-element.74) | copy-start | bytes 28311556
  240.2 53.7 %collective-permute-start.10 = (bf16[9216,128]{1,0:T(8,128)(2,1)}, bf16[9216,128]{1,0:T(8,128)(2,1)}, u32[]{:S(2)}, u32[]{:S(2)}) collective-permute-start(bf16[9216,128]{1,0:T(8,128)(2,1)} %dynamic-slice_bitcast_fusion.2), channel_id=1, source_target_pairs={{0,2},{1,3},{2,0},{3,1},{4,6},{5,7},{6,4},{7,5},{8,10},{9,11},{10,... | collective-permute-start | bytes 7077896 | tf_op jit(solution)/shard_map/ppermute | solution.py:825
  272.3 25.3 %collective-permute-start.11 = (bf16[2,960,768]{2,1,0:T(8,128)(2,1)}, bf16[2,960,768]{2,1,0:T(8,128)(2,1)}, u32[]{:S(2)}, u32[]{:S(2)}) collective-permute-start(bf16[2,960,768]{2,1,0:T(8,128)(2,1)} %dynamic-slice_bitcast_fusion.1), channel_id=1, source_target_pairs={{0,1},{1,0},{2,3},{3,2},{4,5},{5,4},{6,7},{7,6},{8,9},{9,8},{10,11... | collective-permute-start | bytes 8847368 | tf_op jit(solution)/shard_map/ppermute | solution.py:817
  277.8 26.7 %all-to-all-start.1 = ((bf16[8,256,192]{1,2,0:T(8,128)(2,1)}), bf16[8,256,192]{1,2,0:T(8,128)(2,1)}, u32[]{:S(2)}, u32[]{:S(2)}) async-start(bf16[8,256,192]{1,2,0:T(8,128)(2,1)} %bitcast.21), calls=%async_computation.1 | async-start | bytes 1572864 | tf_op jit(solution)/shard_map/all_to_all | solution.py:804
  304.5 96.5 %all-to-all-start.2 = ((bf16[8,1152,128]{2,1,0:T(8,128)(2,1)}), bf16[8,1152,128]{2,1,0:T(8,128)(2,1)}, u32[]{:S(2)}, u32[]{:S(2)}) async-start(bf16[8,1152,128]{2,1,0:T(8,128)(2,1)} %bitcast.152), calls=%async_computation.2 | async-start | bytes 4718592 | tf_op jit(solution)/shard_map/all_to_all | solution.py:840
  308.9 92.1 %reduce-scatter.2.cloned.1.call-start = ((), (), s32[]{:S(2)}) async-start(), calls=%async_computation.11 | async-start | bytes 884736 | tf_op jit(solution)/shard_map/reduce_scatter | solution.py:893
  313.2 274.3 %all-gather.26.cloned.1.call-start = ((), (), s32[]{:S(2)}) async-start(), calls=%async_computation.13 | async-start | bytes 2654208 | tf_op jit(solution)/shard_map/all_gather | solution.py:847
  315.2 85.8 %collective-permute-start.12 = (bf16[960,768]{1,0:T(8,128)(2,1)}, bf16[960,768]{1,0:T(8,128)(2,1)S(1)}, u32[]{:S(2)}, u32[]{:S(2)}) collective-permute-start(bf16[960,768]{1,0:T(8,128)(2,1)} %get-tuple-element.155), channel_id=1, source_target_pairs={{0,2},{1,3},{2,0},{3,1},{4,6},{5,7},{6,4},{7,5},{8,10},{9,11},{10,... | collective-permute-start | bytes 4423688 | tf_op jit(solution)/shard_map/ppermute | solution.py:825
  319.3 81.7 %copy-start.20 = (bf16[4,192,768]{2,1,0:T(8,128)(2,1)S(1)}, bf16[4,192,768]{2,1,0:T(8,128)(2,1)}, u32[]{:S(2)}) copy-start(bf16[4,192,768]{2,1,0:T(8,128)(2,1)} %pad_maximum_fusion.2) | copy-start | bytes 3538948
  414.4 15.3 %collective-permute-start.20 = (bf16[2,208,768]{2,1,0:T(8,128)(2,1)}, bf16[2,208,768]{2,1,0:T(8,128)(2,1)S(1)}, u32[]{:S(2)}, u32[]{:S(2)}) collective-permute-start(bf16[2,208,768]{2,1,0:T(8,128)(2,1)} %fusion.57), channel_id=1, source_target_pairs={{0,1},{1,0},{2,3},{3,2},{4,5},{5,4},{6,7},{7,6},{8,9},{9,8},{10,11... | collective-permute-start | bytes 1916936 | tf_op jit(solution)/shard_map/ppermute | solution.py:817
  417.4 30.6 %collective-permute-start.16 = (bf16[512,768]{1,0:T(8,128)(2,1)}, bf16[512,768]{1,0:T(8,128)(2,1)}, u32[]{:S(2)}, u32[]{:S(2)}) collective-permute-start(bf16[512,768]{1,0:T(8,128)(2,1)} %convolution_convert_fusion.4), channel_id=1, source_target_pairs={{0,4},{4,0},{8,12},{12,8},{16,20},{20,16},{24,28},{28,24},{1,5},{5... | collective-permute-start | bytes 2359304 | tf_op jit(solution)/shard_map/ppermute | solution.py:913
  421.5 98.2 %all-to-all-start.4 = ((bf16[8,120,768]{2,1,0:T(8,128)(2,1)}), bf16[8,120,768]{2,1,0:T(8,128)(2,1)S(1)}, u32[]{:S(2)}, u32[]{:S(2)}) async-start(bf16[8,120,768]{2,1,0:T(8,128)(2,1)} %bitcast.52), calls=%async_computation.5 | async-start | bytes 2949120 | tf_op jit(solution)/shard_map/all_to_all | solution.py:840
  427.6 20.3 %copy-start.21 = (bf16[4,192,768]{2,1,0:T(8,128)(2,1)S(1)}, bf16[4,192,768]{2,1,0:T(8,128)(2,1)}, u32[]{:S(2)}) copy-start(bf16[4,192,768]{2,1,0:T(8,128)(2,1)} %pad_maximum_fusion.2) | copy-start | bytes 3538948
  427.6 56.4 %collective-permute-start.15 = (bf16[512,768]{1,0:T(8,128)(2,1)S(1)}, bf16[512,768]{1,0:T(8,128)(2,1)S(1)}, u32[]{:S(2)}, u32[]{:S(2)}) collective-permute-start(bf16[512,768]{1,0:T(8,128)(2,1)S(1)} %convolution_convert_fusion.1), channel_id=1, source_target_pairs={{0,4},{4,0},{8,12},{12,8},{16,20},{20,16},{24,28},{28,24},{1,5},{5... | collective-permute-start | bytes 2359304 | tf_op jit(solution)/shard_map/ppermute | solution.py:913
  429.7 21.9 %copy-start.38 = (bf16[4096,768]{1,0:T(8,128)(2,1)S(1)}, bf16[4096,768]{1,0:T(8,128)(2,1)}, u32[]{:S(2)}) copy-start(bf16[4096,768]{1,0:T(8,128)(2,1)} %get-tuple-element.92) | copy-start | bytes 18874372
  429.9 26.7 %collective-permute-start.21 = (bf16[208,768]{1,0:T(8,128)(2,1)S(1)}, bf16[208,768]{1,0:T(8,128)(2,1)S(1)}, u32[]{:S(2)}, u32[]{:S(2)}) collective-permute-start(bf16[208,768]{1,0:T(8,128)(2,1)S(1)} %dynamic-slice_bitcast_fusion.5), channel_id=1, source_target_pairs={{0,2},{1,3},{2,0},{3,1},{4,6},{5,7},{6,4},{7,5},{8,10},{9,11},{10,... | collective-permute-start | bytes 958472 | tf_op jit(solution)/shard_map/ppermute | solution.py:825
  450.1 41.9 %collective-permute-start.17 = (bf16[512,768]{1,0:T(8,128)(2,1)S(1)}, bf16[512,768]{1,0:T(8,128)(2,1)S(1)}, u32[]{:S(2)}, u32[]{:S(2)}) collective-permute-start(bf16[512,768]{1,0:T(8,128)(2,1)S(1)} %add_convert_fusion.3), channel_id=1, source_target_pairs={{0,8},{4,12},{8,16},{12,20},{16,24},{20,28},{24,0},{28,4},{1,9},{5... | collective-permute-start | bytes 2359304 | tf_op jit(solution)/shard_map/ppermute | solution.py:916
  453.4 71.9 %collective-permute-start.14 = (bf16[512,768]{1,0:T(8,128)(2,1)}, bf16[512,768]{1,0:T(8,128)(2,1)}, u32[]{:S(2)}, u32[]{:S(2)}) collective-permute-start(bf16[512,768]{1,0:T(8,128)(2,1)} %convolution_convert_fusion.2), channel_id=1, source_target_pairs={{0,4},{4,0},{8,12},{12,8},{16,20},{20,16},{24,28},{28,24},{1,5},{5... | collective-permute-start | bytes 2359304 | tf_op jit(solution)/shard_map/ppermute | solution.py:913
  456.8 53.4 %collective-permute-start.22 = (bf16[208,768]{1,0:T(8,128)(2,1)S(1)}, bf16[208,768]{1,0:T(8,128)(2,1)S(1)}, u32[]{:S(2)}, u32[]{:S(2)}) collective-permute-start(bf16[208,768]{1,0:T(8,128)(2,1)S(1)} %fusion.60), channel_id=1, source_target_pairs={{0,4},{4,0},{8,12},{12,8},{16,20},{20,16},{24,28},{28,24},{1,5},{5... | collective-permute-start | bytes 958472 | tf_op jit(solution)/shard_map/ppermute | solution.py:832
  493.3 32.0 %collective-permute-start.18 = (bf16[512,768]{1,0:T(8,128)(2,1)}, bf16[512,768]{1,0:T(8,128)(2,1)}, u32[]{:S(2)}, u32[]{:S(2)}) collective-permute-start(bf16[512,768]{1,0:T(8,128)(2,1)} %add_convert_fusion.2), channel_id=1, source_target_pairs={{0,8},{4,12},{8,16},{12,20},{16,24},{20,28},{24,0},{28,4},{1,9},{5... | collective-permute-start | bytes 2359304 | tf_op jit(solution)/shard_map/ppermute | solution.py:916
  505.8 24.8 %collective-permute-start.13 = (bf16[512,768]{1,0:T(8,128)(2,1)}, bf16[512,768]{1,0:T(8,128)(2,1)}, u32[]{:S(2)}, u32[]{:S(2)}) collective-permute-start(bf16[512,768]{1,0:T(8,128)(2,1)} %convolution_convert_fusion.3), channel_id=1, source_target_pairs={{0,4},{4,0},{8,12},{12,8},{16,20},{20,16},{24,28},{28,24},{1,5},{5... | collective-permute-start | bytes 2359304 | tf_op jit(solution)/shard_map/ppermute | solution.py:913
  520.9 57.6 %all-to-all-start.3 = ((bf16[4,208,768]{2,1,0:T(8,128)(2,1)}), bf16[4,208,768]{2,1,0:T(8,128)(2,1)}, u32[]{:S(2)}, u32[]{:S(2)}) async-start(bf16[4,208,768]{2,1,0:T(8,128)(2,1)} %broadcast_in_dim.20), calls=%async_computation.4 | async-start | bytes 2555904 | tf_op jit(solution)/shard_map/all_to_all | solution.py:844
  525.2 72.6 %all-gather.24.cloned.1.call-start = ((), (), s32[]{:S(2)}) async-start(), calls=%async_computation.12 | async-start | bytes 1658880 | tf_op jit(solution)/shard_map/all_gather | solution.py:847
  527.7 44.7 %copy-start.12 = (bf16[1,512,768]{2,1,0:T(8,128)(2,1)S(1)}, bf16[1,512,768]{2,1,0:T(8,128)(2,1)}, u32[]{:S(2)}) copy-start(bf16[1,512,768]{2,1,0:T(8,128)(2,1)} %param.19) | copy-start | bytes 2359300
  527.7 44.7 %collective-permute-start.19 = (bf16[512,768]{1,0:T(8,128)(2,1)}, bf16[512,768]{1,0:T(8,128)(2,1)S(1)}, u32[]{:S(2)}, u32[]{:S(2)}) collective-permute-start(bf16[512,768]{1,0:T(8,128)(2,1)} %add_convert_fusion.1), channel_id=1, source_target_pairs={{0,8},{4,12},{8,16},{12,20},{16,24},{20,28},{24,0},{28,4},{1,9},{5... | collective-permute-start | bytes 2359304 | tf_op jit(solution)/shard_map/ppermute | solution.py:916
  530.6 44.7 %copy-start.7 = (f32[512,768]{1,0:T(8,128)S(1)}, f32[512,768]{1,0:T(8,128)}, u32[]{:S(2)}) copy-start(f32[512,768]{1,0:T(8,128)} %get-tuple-element.154) | copy-start | bytes 4718596
  592.8 7.9 %copy-start.29 = (f32[512,768]{1,0:T(8,128)}, f32[512,768]{1,0:T(8,128)S(1)}, u32[]{:S(2)}) copy-start(f32[512,768]{1,0:T(8,128)S(1)} %slice_dynamic-update-slice_fusion) | copy-start | bytes 4718596
  (30 other events, 102.4 us)
Sparse Core Ops, SparseCore 0:
  9.6 21.2 all-gather.19
  32.5 19.8 all-gather.17
  53.9 17.4 all-gather.13
  72.8 17.4 all-gather.15
  91.7 17.4 all-gather.21
  110.6 28.5 all-gather.27
  140.8 28.5 all-gather.29
  171.0 28.5 all-gather.31
  313.6 87.3 reduce-scatter.1
  417.5 105.9 all-gather.25
  530.7 67.0 all-gather.23
